TPU v7x, 32 devices: a whole 2x2x4 slice. The times are simulated.
32 devices in a mesh: pipe: 4 (over y, x), tensor: 2 (over core), dp: 4 (over z).
Axes of the slice: x: 2, y: 2, z: 4, core: 2. Of those that a mesh axis runs over, the one named last changes fastest.
Arguments:
- x_fwd: bfloat16 [4, 4, 96, 4096], P('pipe', 'dp', 'tensor'), may hold values from -6 to 6
- x_bwd: bfloat16 [4, 4, 96, 4096], P('pipe', 'dp', 'tensor'), may hold values from -6 to 6
- grad_out: bfloat16 [4, 4, 96, 4096], P('pipe', 'dp', 'tensor'), may hold values from -6 to 6
- saved_qkv: bfloat16 [4, 4, 96, 6144], P('pipe', 'dp', None, 'tensor'), may hold values from -32 to 32
- norm_gain: float32 [4, 4096], P('pipe'), may hold values from 0.5 to 1.5
- w_qkv: bfloat16 [4, 4096, 6144], P('pipe', None, 'tensor'), may hold values from -8 to 8
- w_out: bfloat16 [4, 4608, 4096], P('pipe', 'tensor', 'dp'), may hold values from -0.09375 to 0.09375
Outputs:
- next_input: bfloat16 [4, 4, 96, 4096], P('pipe', 'dp', 'tensor')
- prev_grad: bfloat16 [4, 4, 96, 4096], P('pipe', 'dp', 'tensor')
All inputs are finite; a program needn't handle non-finite values.
Results may differ from a plain program's by a relative error of at most 0.019.
Values may be sent and summed in bfloat16 or wider, within the bound.
No kernel may reach another device: no remote copies, remote signals or barrier semaphores. Data moves between devices by JAX's collectives and lax.ppermute only.
A program may use at most 64 MiB of HBM per device.

v0:
```python
import math

import jax
import jax.numpy as jnp
from jax import lax
from jax.experimental import pallas as pl
from jax.experimental.pallas import tpu as pltpu
from jax.sharding import PartitionSpec as P


HD = 128
GROUP = 6
UNIT = (GROUP + 2) * HD


def shift_pairs(count, steps):
    return [(source, (source + steps) % count) for source in range(count)]


def partner_pairs(count, step):
    if count & (count - 1):
        raise ValueError("dp size")
    return [(source, source ^ step) for source in range(count)]


def partner_index(axis, step):
    return jnp.bitwise_xor(lax.axis_index(axis), step)


def cross_pairs(step, forward):
    pipes = lax.axis_size("pipe")
    count = lax.axis_size("dp")
    return [
        (p * count + d, ((p + forward) % pipes) * count + (d ^ step))
        for p in range(pipes)
        for d in range(count)
    ]


def over_dp(value, step):
    return lax.ppermute(value, "dp", partner_pairs(lax.axis_size("dp"), step))


def over_pipe(value, steps):
    return lax.ppermute(value, "pipe", shift_pairs(lax.axis_size("pipe"), steps))


def blocks_of_cores(value):
    count = lax.axis_size("tensor")
    return [value] + [
        lax.ppermute(value, "tensor", shift_pairs(count, -step)) for step in range(1, count)
    ]


def sum_over_cores(keep, sends):
    count = lax.axis_size("tensor")
    total = keep.astype(jnp.float32)
    for step in range(1, count):
        block = lax.ppermute(sends[step - 1], "tensor", shift_pairs(count, step))
        total = total + block.astype(jnp.float32)
    return total


def normalize(inputs, gain_row):
    widened = inputs.astype(jnp.float32)
    inverse = lax.rsqrt(jnp.mean(widened * widened, axis=-1, keepdims=True) + 1e-05)
    return (widened * inverse * gain_row).astype(jnp.bfloat16)


def norm_back(inputs, grad_rows, scaled):
    widened = inputs.astype(jnp.float32)
    inverse = lax.rsqrt(jnp.mean(widened * widened, axis=-1, keepdims=True) + 1e-05)
    middle = jnp.mean(widened * scaled, axis=-1, keepdims=True)
    result = (
        grad_rows.astype(jnp.float32)
        + inverse * scaled
        - widened * inverse * inverse * inverse * middle
    )
    return result.astype(jnp.bfloat16)


def mxu(left, right, left_dim, right_dim):
    return lax.dot_general(
        left,
        right,
        (((left_dim,), (right_dim,)), ((), ())),
        preferred_element_type=jnp.float32,
    )


def later_keys(length, start):
    rows_at = lax.broadcasted_iota(jnp.int32, (length, length), 0) + start
    cols_at = lax.broadcasted_iota(jnp.int32, (length, length), 1) + start
    rows_at = jnp.where(rows_at >= length, rows_at - length, rows_at)
    cols_at = jnp.where(cols_at >= length, cols_at - length, cols_at)
    return cols_at > rows_at


def head_columns(value, head):
    return value[:, head * HD : (head + 1) * HD]


def stacked_heads(value):
    return jnp.concatenate([head_columns(value, g) for g in range(GROUP)], axis=0)


def probabilities(queries, keys, masked):
    length = keys.shape[0]
    scores = mxu(queries, keys, 1, 1) * (1.0 / math.sqrt(HD))
    rows = []
    for g in range(GROUP):
        part = jnp.where(masked, -1e30, scores[g * length : (g + 1) * length])
        part = jnp.exp(part - jnp.max(part, axis=-1, keepdims=True))
        rows.append(part / jnp.sum(part, axis=-1, keepdims=True))
    return jnp.concatenate(rows, axis=0)


def attend_unit(qkv, masked, out_ref, at):
    length = qkv.shape[0]
    keys, values = head_columns(qkv, GROUP), head_columns(qkv, GROUP + 1)
    probs = probabilities(stacked_heads(qkv), keys, masked).astype(jnp.bfloat16)
    heads = mxu(probs, values, 1, 0).astype(jnp.bfloat16)
    for g in range(GROUP):
        out_ref[:, at + g * HD : at + (g + 1) * HD] = heads[g * length : (g + 1) * length]


def attend_back_unit(qkv, grads, masked, out_ref, at):
    length = qkv.shape[0]
    factor = 1.0 / math.sqrt(HD)
    keys, values = head_columns(qkv, GROUP), head_columns(qkv, GROUP + 1)
    queries = stacked_heads(qkv)
    grads = stacked_heads(grads)
    probs = probabilities(queries, keys, masked)
    grad_values = mxu(probs.astype(jnp.bfloat16), grads, 0, 0)
    grad_probs = mxu(grads, values, 1, 1)
    grad_scores = probs * (grad_probs - jnp.sum(probs * grad_probs, axis=-1, keepdims=True))
    grad_scores = grad_scores.astype(jnp.bfloat16)
    grad_queries = mxu(grad_scores, keys, 1, 0) * factor
    grad_keys = mxu(grad_scores, queries, 0, 0) * factor
    for g in range(GROUP):
        out_ref[:, at + g * HD : at + (g + 1) * HD] = grad_queries[
            g * length : (g + 1) * length
        ].astype(jnp.bfloat16)
    out_ref[:, at + GROUP * HD : at + (GROUP + 1) * HD] = grad_keys.astype(jnp.bfloat16)
    out_ref[:, at + (GROUP + 1) * HD : at + UNIT] = grad_values.astype(jnp.bfloat16)


def divisor(size, most):
    parts = 1
    while size % parts or size // parts > most or (size // parts) % HD:
        parts += 1
        if parts > size:
            raise ValueError("block size")
    return size // parts


SCALAR = pl.BlockSpec(memory_space=pltpu.SMEM)
LOCAL = pl.BlockSpec(memory_space=pltpu.VMEM)
REMOTE = pl.BlockSpec(memory_space=pltpu.HBM)


def call(kernel, args, weight, outs, copies, block, scratch, flops):
    count = len(args)

    def body(*refs):
        ins, weight_ref = refs[:count], refs[count]
        results = refs[count + 1 : count + 1 + len(outs)]
        held, sems, *rest = refs[count + 1 + len(outs) :]
        moves = [
            pltpu.make_async_copy(
                weight_ref.at[pl.ds(row, block[0]), pl.ds(column, block[1])],
                held.at[index],
                sems.at[index],
            )
            for index, (row, column) in enumerate(copies)
        ]
        for move in moves:
            move.start()
        kernel(ins, results, held, lambda index: moves[index].wait(), *rest)

    moved = 2 * len(copies) * block[0] * block[1]
    return pl.pallas_call(
        body,
        in_specs=[SCALAR if arg.dtype == jnp.int32 else LOCAL for arg in args] + [REMOTE],
        out_specs=[LOCAL for _ in outs],
        out_shape=[jax.ShapeDtypeStruct(shape, jnp.bfloat16) for shape in outs],
        scratch_shapes=[
            pltpu.VMEM((len(copies),) + block, jnp.bfloat16),
            pltpu.SemaphoreType.DMA((len(copies),)),
        ]
        + scratch,
        compiler_params=pltpu.CompilerParams(vmem_limit_bytes=moved + (8 << 20)),
        cost_estimate=pl.CostEstimate(flops=flops, bytes_accessed=moved, transcendentals=0),
    )(*args, weight)


def forward_heads(blocks, weight, start):
    rows, width = blocks[0].shape
    length = rows * len(blocks)
    merged = weight.shape[1]
    units = merged // UNIT
    depth = divisor(width, 1024)
    steps = width // depth

    def kernel(ins, outs, held, wait):
        masked = later_keys(length, ins[0][0])
        for unit in range(units):
            total = None
            for step in range(steps):
                at = slice(step * depth, (step + 1) * depth)
                left = jnp.concatenate([ref[:, at] for ref in ins[1:]], axis=0)
                wait(unit * steps + step)
                product = mxu(left, held[unit * steps + step], 1, 0)
                total = product if total is None else total + product
            attend_unit(total.astype(jnp.bfloat16), masked, outs[0], unit * GROUP * HD)

    copies = [(step * depth, unit * UNIT) for unit in range(units) for step in range(steps)]
    return call(
        kernel,
        [start] + blocks,
        weight,
        [(length, units * GROUP * HD)],
        copies,
        (depth, UNIT),
        [],
        2 * length * width * merged,
    )[0]


def head_terms(pieces, weight):
    rows, columns = pieces[0][0].shape
    length = rows * len(pieces[0])
    depth = weight.shape[0]
    block = divisor(depth, 768)
    flat = [part for parts in pieces for part in parts]

    def kernel(ins, outs, held, wait):
        left = jnp.concatenate([ref[...] for ref in ins], axis=0)
        for step in range(depth // block):
            wait(step)
            product = mxu(left, held[step], 1, 1).astype(jnp.bfloat16)
            for index, out_ref in enumerate(outs):
                out_ref[:, step * block : (step + 1) * block] = product[
                    index * length : (index + 1) * length
                ]

    return call(
        kernel,
        flat,
        weight,
        [(length, depth) for _ in pieces],
        [(row, 0) for row in range(0, depth, block)],
        (block, columns),
        [],
        2 * len(pieces) * length * depth * columns,
    )


def project(heads, weight, cores):
    length, depth = heads[0].shape
    columns = weight.shape[1]
    rows = length // cores
    block = divisor(depth, 768)
    count = len(heads)

    def kernel(ins, outs, held, wait):
        total = None
        for step in range(depth // block):
            at = slice(step * block, (step + 1) * block)
            left = jnp.concatenate([ref[:, at] for ref in ins], axis=0)
            wait(step)
            product = mxu(left, held[step], 1, 0)
            total = product if total is None else total + product
        total = total.astype(jnp.bfloat16)
        for core, out_ref in enumerate(outs):
            for index in range(count):
                at = index * length + core * rows
                out_ref[index * rows : (index + 1) * rows] = total[at : at + rows]

    return call(
        kernel,
        heads,
        weight,
        [(count * rows, columns) for _ in range(cores)],
        [(row, 0) for row in range(0, depth, block)],
        (block, columns),
        [],
        2 * count * length * depth * columns,
    )


def back_columns(grad, outs, held, wait, cores, steps, block):
    rows = grad.shape[0] // cores
    for step in range(steps):
        wait(step)
        product = mxu(grad, held[step], 1, 1).astype(jnp.bfloat16)
        for core, out_ref in enumerate(outs):
            out_ref[:, step * block : (step + 1) * block] = product[
                core * rows : (core + 1) * rows
            ]


def back_first(qkv, terms, weight, start, cores, steps, block):
    length, merged = qkv.shape
    units = merged // UNIT
    rows = length // cores

    def kernel(ins, outs, held, wait):
        masked = later_keys(length, ins[0][0])
        for unit in range(units):
            at = unit * UNIT
            part = slice(unit * GROUP * HD, (unit + 1) * GROUP * HD)
            grads = ins[2][:, part].astype(jnp.float32)
            for ref in ins[3:]:
                grads = grads + ref[:, part].astype(jnp.float32)
            attend_back_unit(
                ins[1][:, at : at + UNIT], grads.astype(jnp.bfloat16), masked, outs[0], at
            )
        back_columns(outs[0][...], outs[1:], held, wait, cores, steps, block)

    results = call(
        kernel,
        [start, qkv] + terms,
        weight,
        [qkv.shape] + [(rows, steps * block) for _ in range(cores)],
        [(step * block, 0) for step in range(steps)],
        (block, merged),
        [],
        2 * length * merged * steps * block,
    )
    return results[0], results[1:]


def back_rest(grad_qkv, weight, cores, first, steps, block):
    length, merged = grad_qkv.shape
    rows = length // cores

    def kernel(ins, outs, held, wait):
        back_columns(ins[0][...], outs, held, wait, cores, steps, block)

    return call(
        kernel,
        [grad_qkv],
        weight,
        [(rows, steps * block) for _ in range(cores)],
        [((first + step) * block, 0) for step in range(steps)],
        (block, merged),
        [],
        2 * length * merged * steps * block,
    )


def per_device(x_fwd, x_bwd, grad_out, saved_qkv, norm_gain, w_qkv, w_out):
    return window(
        x_fwd[0, 0],
        x_bwd[0, 0],
        grad_out[0, 0],
        saved_qkv[0, 0],
        norm_gain,
        w_qkv[0],
        w_out[0],
    )


def window(fwd_rows, bwd_rows, grad_rows, qkv_saved, gain_row, weight_qkv, weight_out):
    rows, width = fwd_rows.shape
    cores = lax.axis_size("tensor")
    replicas = lax.axis_size("dp")
    columns = weight_out.shape[1]
    start = lax.axis_index("tensor") * rows
    start_word = jnp.full((1,), start, jnp.int32)
    if replicas != 4:
        raise ValueError("dp size")

    def grad_piece(step):
        at = partner_index("dp", step) * columns
        return lax.dynamic_slice_in_dim(grad_rows, at, columns, axis=1)

    pieces = [grad_piece(0)]
    pieces += [over_dp(grad_piece(step), step) for step in range(1, replicas)]

    normed_rows = normalize(fwd_rows, gain_row)
    normed_far = over_dp(normed_rows, 2)
    own_heads = forward_heads(blocks_of_cores(normed_rows), weight_qkv, start_word)
    far_heads = forward_heads(blocks_of_cores(normed_far), weight_qkv, start_word)
    near_heads = over_dp(own_heads, 1)
    last_heads = over_dp(far_heads, 1)

    exchanged = [blocks_of_cores(piece) for piece in pieces]
    terms = head_terms(exchanged, weight_out)
    relay = over_dp(terms[3], 1)
    near = over_dp(terms[1], 1)
    joined = (terms[2].astype(jnp.float32) + relay.astype(jnp.float32)).astype(jnp.bfloat16)
    terms = [terms[0], near, over_dp(joined, 2)]

    fwd_prev = over_pipe(fwd_rows, 1)
    bwd_next = over_pipe(bwd_rows, -1)
    grad_next = over_pipe(grad_rows, -1)

    qkv_rolled = jnp.roll(qkv_saved, -start, axis=0)
    half = width // 2
    block = divisor(half, 512)
    steps = half // block
    grad_qkv, (keep, *sends) = back_first(
        qkv_rolled, terms, weight_qkv, start_word, cores, steps, block
    )
    scaled = sum_over_cores(keep, sends) * gain_row[:, :half]
    arrived = [over_pipe(scaled.astype(jnp.bfloat16), -1)]
    keep, *sends = back_rest(grad_qkv, weight_qkv, cores, steps, steps, block)
    scaled = sum_over_cores(keep, sends) * gain_row[:, half:]
    arrived.append(over_pipe(scaled.astype(jnp.bfloat16), -1))
    scaled = jnp.concatenate(arrived, axis=1).astype(jnp.float32)
    grad_input = norm_back(bwd_next, grad_next, scaled)

    output = fwd_prev
    groups = (((0, 2), [own_heads, far_heads]), ((1, 3), [near_heads, last_heads]))
    for group, heads in groups:
        keep, *sends = project(heads, weight_out, cores)
        summed = sum_over_cores(keep, sends).astype(jnp.bfloat16)
        for index, step in enumerate(group):
            piece = lax.ppermute(
                summed[index * rows : (index + 1) * rows],
                ("pipe", "dp"),
                cross_pairs(step, 1),
            )
            at = partner_index("dp", step) * columns
            part = lax.dynamic_slice_in_dim(fwd_prev, at, columns, axis=1).astype(jnp.float32)
            part = (part + piece.astype(jnp.float32)).astype(jnp.bfloat16)
            output = lax.dynamic_update_slice_in_dim(output, part, at, axis=1)
    return (output[None, None], grad_input[None, None])


def solution(mesh):
    return jax.shard_map(
        per_device,
        mesh=mesh,
        in_specs=(
            P("pipe", "dp", "tensor", None),
            P("pipe", "dp", "tensor", None),
            P("pipe", "dp", "tensor", None),
            P("pipe", "dp", None, "tensor"),
            P("pipe", None),
            P("pipe", None, "tensor"),
            P("pipe", "tensor", "dp"),
        ),
        out_specs=(P("pipe", "dp", "tensor", None), P("pipe", "dp", "tensor", None)),
        check_vma=False,
    )
```

profile of v0, /device:TPU:0, one launch (start us, length us, event | category | flops | bytes accessed | tf_op | source)
XLA Modules:
  0.0 145.3 jit_solution(16934383597035678294)
XLA Ops:
  0.7 1.1 dynamic-slice_bitcast_fusion
  1.8 3.1 %collective-permute-start.15 = (bf16[48,1024]{1,0:T(8,128)(2,1)S(1)}, bf16[48,1024]{1,0:T(8,128)(2,1)S(1)}, u32[]{:S(2)}, u32[]{:S(2)}) collective-permute-start(bf16[48,1024]{1,0:T(8,128)(2,1)S(1)} %get-tuple-element.31), channel_id=1, source_target_pairs={{0,1},{1,0},{2,3},{3,2},{4,5},{5,4},{6,7},{7,6},{8,9},{9,8},{10,11... | collective-permute-start | bytes 294920 | tf_op jit(solution)/shard_map/ppermute | solution.py:41
  5.0 2.6 %collective-permute-start.17 = (bf16[48,1024]{1,0:T(8,128)(2,1)S(1)}, bf16[48,1024]{1,0:T(8,128)(2,1)S(1)}, u32[]{:S(2)}, u32[]{:S(2)}) collective-permute-start(bf16[48,1024]{1,0:T(8,128)(2,1)S(1)} %get-tuple-element.33), channel_id=1, source_target_pairs={{0,2},{1,3},{2,0},{3,1},{4,6},{5,7},{6,4},{7,5},{8,10},{9,11},{10,... | collective-permute-start | bytes 294920 | tf_op jit(solution)/shard_map/ppermute | solution.py:41
  7.6 1.2 fusion
  9.0 2.0 %collective-permute-start.2 = (bf16[48,4096]{1,0:T(8,128)(2,1)S(1)}, bf16[48,4096]{1,0:T(8,128)(2,1)S(1)}, u32[]{:S(2)}, u32[]{:S(2)}) collective-permute-start(bf16[48,4096]{1,0:T(8,128)(2,1)S(1)} %fusion.2.refs_1_), channel_id=1, source_target_pairs={{0,2},{1,3},{2,0},{3,1},{4,6},{5,7},{6,4},{7,5},{8,10},{9,11},{10,... | collective-permute-start | bytes 1179656 | tf_op jit(solution)/shard_map/ppermute | solution.py:41
  11.1 12.7 %collective-permute-done.17.refs_4_ = bf16[48,1024]{1,0:T(8,128)(2,1)S(1)} collective-permute-done((bf16[48,1024]{1,0:T(8,128)(2,1)S(1)}, bf16[48,1024]{1,0:T(8,128)(2,1)S(1)}, u32[]{:S(2)}, u32[]{:S(2)}) %collective-permute-start.17) | collective-permute-done | bytes 98336 | tf_op jit(solution)/shard_map/ppermute | solution.py:41
  23.9 1.5 %collective-permute-start = (bf16[48,4096]{1,0:T(8,128)(2,1)S(1)}, bf16[48,4096]{1,0:T(8,128)(2,1)S(1)}, u32[]{:S(2)}, u32[]{:S(2)}) collective-permute-start(bf16[48,4096]{1,0:T(8,128)(2,1)S(1)} %bitcast.48), channel_id=1, source_target_pairs={{0,8},{8,16},{16,24},{24,0},{1,9},{9,17},{17,25},{25,1},{2,10},{10... | collective-permute-start | bytes 1179656 | tf_op jit(solution)/shard_map/ppermute | solution.py:45
  26.7 1.5 %collective-permute-start.13 = (bf16[48,4096]{1,0:T(8,128)(2,1)S(1)}, bf16[48,4096]{1,0:T(8,128)(2,1)S(1)}, u32[]{:S(2)}, u32[]{:S(2)}) collective-permute-start(bf16[48,4096]{1,0:T(8,128)(2,1)S(1)} %bitcast.55), channel_id=1, source_target_pairs={{0,24},{8,0},{16,8},{24,16},{1,25},{9,1},{17,9},{25,17},{2,26},{10... | collective-permute-start | bytes 1179656 | tf_op jit(solution)/shard_map/ppermute | solution.py:45
  28.2 1.5 %collective-permute-start.12 = (bf16[48,4096]{1,0:T(8,128)(2,1)S(1)}, bf16[48,4096]{1,0:T(8,128)(2,1)S(1)}, u32[]{:S(2)}, u32[]{:S(2)}) collective-permute-start(bf16[48,4096]{1,0:T(8,128)(2,1)S(1)} %bitcast.51), channel_id=1, source_target_pairs={{0,24},{8,0},{16,8},{24,16},{1,25},{9,1},{17,9},{25,17},{2,26},{10... | collective-permute-start | bytes 1179656 | tf_op jit(solution)/shard_map/ppermute | solution.py:45
  29.6 3.6 %collective-permute-done.2.refs_1_ = bf16[48,4096]{1,0:T(8,128)(2,1)S(1)} collective-permute-done((bf16[48,4096]{1,0:T(8,128)(2,1)S(1)}, bf16[48,4096]{1,0:T(8,128)(2,1)S(1)}, u32[]{:S(2)}, u32[]{:S(2)}) %collective-permute-start.2) | collective-permute-done | bytes 393248 | tf_op jit(solution)/shard_map/ppermute | solution.py:41
  33.3 2.3 %copy-done.2 = bf16[1,2304,1024]{2,1,0:T(8,128)(2,1)S(1)} copy-done((bf16[1,2304,1024]{2,1,0:T(8,128)(2,1)S(1)}, bf16[1,2304,1024]{2,1,0:T(8,128)(2,1)}, u32[]{:S(2)}) %copy-start.2) | copy-done | bytes 4718616
  35.6 3.2 %shard_map.90 = (bf16[96,2304]{1,0:T(8,128)(2,1)S(1)}, bf16[96,2304]{1,0:T(8,128)(2,1)S(1)}, bf16[96,2304]{1,0:T(8,128)(2,1)S(1)}, bf16[96,2304]{1,0:T(8,128)(2,1)S(1)}) custom-call(bf16[48,1024]{1,0:T(8,128)(2,1)S(1)} %get-tuple-element.32.refs_0_, bf16[48,1024]{1,0:T(8,128)(2,1)S(1)} %collective-permute-done.14.refs_1_, ...), custom_call_target="tpu_custom_call" | custom-call | flops 1811939328 | bytes 4718592 | tf_op jit(solution)/shard_map/pallas_call | solution.py:182
  39.1 1.9 %collective-permute-start.21 = (bf16[96,2304]{1,0:T(8,128)(2,1)S(1)}, bf16[96,2304]{1,0:T(8,128)(2,1)S(1)}, u32[]{:S(2)}, u32[]{:S(2)}) collective-permute-start(bf16[96,2304]{1,0:T(8,128)(2,1)S(1)} %get-tuple-element.20), channel_id=1, source_target_pairs={{0,1},{1,0},{2,3},{3,2},{4,5},{5,4},{6,7},{7,6},{8,9},{9,8},{10,11... | collective-permute-start | bytes 1327112 | tf_op jit(solution)/shard_map/ppermute | solution.py:41
  41.0 9.6 %shard_map.86.refs_0_ = bf16[96,2304]{1,0:T(8,128)(2,1)S(1)} custom-call(s32[1]{0:T(128)} %bitcast.2.refs_0_, bf16[48,4096]{1,0:T(8,128)(2,1)S(1)} %fusion.2.refs_1_, bf16[48,4096]{1,0:T(8,128)(2,1)S(1)} %collective-permute-done.1.refs_2_, bf16[4096,3072]{1,0:T(8,128)(2,1)} %bitcast.39), custom_call_target="tpu_custom_call" | custom-call | flops 2415919104 | bytes 25165824 | tf_op jit(solution)/shard_map/pallas_call | solution.py:182
  50.9 9.5 %shard_map.87.refs_1_ = bf16[96,2304]{1,0:T(8,128)(2,1)S(1)} custom-call(s32[1]{0:T(128)} %bitcast.2.refs_0_, bf16[48,4096]{1,0:T(8,128)(2,1)S(1)} %collective-permute-done.2.refs_1_, bf16[48,4096]{1,0:T(8,128)(2,1)S(1)} %collective-permute-done.3.refs_2_, bf16[4096,3072]{1,0:T(8,128)(2,1)} %bitcast.40), custom_call_target="tpu_custom_call" | custom-call | flops 2415919104 | bytes 25165824 | tf_op jit(solution)/shard_map/pallas_call | solution.py:182
  60.4 1.6 %shard_map.88 = (bf16[96,1024]{1,0:T(8,128)(2,1)S(1)}, bf16[96,1024]{1,0:T(8,128)(2,1)S(1)}) custom-call(bf16[96,2304]{1,0:T(8,128)(2,1)S(1)} %shard_map.86.refs_0_, bf16[96,2304]{1,0:T(8,128)(2,1)S(1)} %shard_map.87.refs_1_, bf16[2304,1024]{1,0:T(8,128)(2,1)S(1)} %bitcast.46), custom_call_target="tpu_custom_call" | custom-call | flops 905969664 | bytes 4718592 | tf_op jit(solution)/shard_map/pallas_call | solution.py:182
  62.3 1.3 collective-permute-done.4
  63.6 2.9 %collective-permute-start.23 = (bf16[96,2304]{1,0:T(8,128)(2,1)S(1)}, bf16[96,2304]{1,0:T(8,128)(2,1)S(1)}, u32[]{:S(2)}, u32[]{:S(2)}) collective-permute-start(bf16[96,2304]{1,0:T(8,128)(2,1)S(1)} %add_convert_fusion), channel_id=1, source_target_pairs={{0,2},{1,3},{2,0},{3,1},{4,6},{5,7},{6,4},{7,5},{8,10},{9,11},{10,... | collective-permute-start | bytes 1327112 | tf_op jit(solution)/shard_map/ppermute | solution.py:41
  66.8 19.8 %collective-permute-done.23.refs_4_ = bf16[96,2304]{1,0:T(8,128)(2,1)S(1)} collective-permute-done((bf16[96,2304]{1,0:T(8,128)(2,1)S(1)}, bf16[96,2304]{1,0:T(8,128)(2,1)S(1)}, u32[]{:S(2)}, u32[]{:S(2)}) %collective-permute-start.23) | collective-permute-done | bytes 442400 | tf_op jit(solution)/shard_map/ppermute | solution.py:41
  86.6 1.5 %collective-permute-start.5 = (bf16[48,1024]{1,0:T(8,128)(2,1)S(1)}, bf16[48,1024]{1,0:T(8,128)(2,1)S(1)}, u32[]{:S(2)}, u32[]{:S(2)}) collective-permute-start(bf16[48,1024]{1,0:T(8,128)(2,1)S(1)} %get-tuple-element.37), channel_id=1, source_target_pairs={{0,8},{1,9},{2,10},{3,11},{8,16},{9,17},{10,18},{11,19},{16,24},{1... | collective-permute-start | bytes 294920 | tf_op jit(solution)/shard_map/ppermute | solution.py:421
  88.1 8.2 %copy-done = bf16[1,4096,3072]{2,1,0:T(8,128)(2,1)S(1)} copy-done((bf16[1,4096,3072]{2,1,0:T(8,128)(2,1)S(1)}, bf16[1,4096,3072]{2,1,0:T(8,128)(2,1)}, u32[]{:S(2)}) %copy-start) | copy-done | bytes 25165848
  96.2 7.4 %shard_map.91 = (bf16[96,3072]{1,0:T(8,128)(2,1)S(1)}, bf16[48,2048]{1,0:T(8,128)(2,1)S(1)}, bf16[48,2048]{1,0:T(8,128)(2,1)S(1)}) custom-call(s32[1]{0:T(128)} %bitcast.2.refs_0_, bf16[96,3072]{1,0:T(8,128)(2,1)S(1)} %fusion.11.refs_1_, bf16[96,2304]{1,0:T(8,128)(2,1)S(1)} %get-tuple-element.19.refs_2_, ...), custom_call_target="tpu_custom_call" | custom-call | flops 1207959552 | bytes 12582912 | tf_op jit(solution)/shard_map/pallas_call | solution.py:182
  103.7 8.1 %copy-done.1 = bf16[1,4096,3072]{2,1,0:T(8,128)(2,1)S(1)} copy-done((bf16[1,4096,3072]{2,1,0:T(8,128)(2,1)S(1)}, bf16[1,4096,3072]{2,1,0:T(8,128)(2,1)}, u32[]{:S(2)}) %copy-start.1) | copy-done | bytes 25165848
  111.8 5.3 %shard_map.92 = (bf16[48,2048]{1,0:T(8,128)(2,1)S(1)}, bf16[48,2048]{1,0:T(8,128)(2,1)S(1)}) custom-call(bf16[96,3072]{1,0:T(8,128)(2,1)S(1)} %get-tuple-element.25.refs_0_, bf16[4096,3072]{1,0:T(8,128)(2,1)S(1)} %bitcast.42), custom_call_target="tpu_custom_call" | custom-call | flops 1207959552 | bytes 12582912 | tf_op jit(solution)/shard_map/pallas_call | solution.py:182
  117.7 7.1 %collective-permute-done.6 = bf16[48,1024]{1,0:T(8,128)(2,1)S(1)} collective-permute-done((bf16[48,1024]{1,0:T(8,128)(2,1)S(1)}, bf16[48,1024]{1,0:T(8,128)(2,1)S(1)}, u32[]{:S(2)}, u32[]{:S(2)}) %collective-permute-start.6) | collective-permute-done | bytes 98336 | tf_op jit(solution)/shard_map/ppermute | solution.py:421
  125.5 1.6 %shard_map.89 = (bf16[96,1024]{1,0:T(8,128)(2,1)S(1)}, bf16[96,1024]{1,0:T(8,128)(2,1)S(1)}) custom-call(bf16[96,2304]{1,0:T(8,128)(2,1)S(1)} %collective-permute-done.7.refs_0_, bf16[96,2304]{1,0:T(8,128)(2,1)S(1)} %collective-permute-done.8.refs_1_, bf16[2304,1024]{1,0:T(8,128)(2,1)S(1)} %bitcast.47), custom_call_target="tpu_custom_call" | custom-call | flops 905969664 | bytes 4718592 | tf_op jit(solution)/shard_map/pallas_call | solution.py:182
  127.3 0.9 collective-permute-start.25
  128.3 2.1 %collective-permute-start.27 = (bf16[48,2048]{1,0:T(8,128)(2,1)S(1)}, bf16[48,2048]{1,0:T(8,128)(2,1)S(1)}, u32[]{:S(2)}, u32[]{:S(2)}) collective-permute-start(bf16[48,2048]{1,0:T(8,128)(2,1)S(1)} %multiply_convert_fusion), channel_id=1, source_target_pairs={{0,24},{8,0},{16,8},{24,16},{1,25},{9,1},{17,9},{25,17},{2,26},{10... | collective-permute-start | bytes 589832 | tf_op jit(solution)/shard_map/ppermute | solution.py:45
  130.6 1.5 %collective-permute-start.11 = (bf16[48,1024]{1,0:T(8,128)(2,1)S(1)}, bf16[48,1024]{1,0:T(8,128)(2,1)S(1)}, u32[]{:S(2)}, u32[]{:S(2)}) collective-permute-start(bf16[48,1024]{1,0:T(8,128)(2,1)S(1)} %get-tuple-element.34), channel_id=1, source_target_pairs={{0,11},{1,10},{2,9},{3,8},{8,19},{9,18},{10,17},{11,16},{16,27},{1... | collective-permute-start | bytes 294920 | tf_op jit(solution)/shard_map/ppermute | solution.py:421
  132.1 7.2 %collective-permute-done.25 = bf16[48,2048]{1,0:T(8,128)(2,1)S(1)} collective-permute-done((bf16[48,2048]{1,0:T(8,128)(2,1)S(1)}, bf16[48,2048]{1,0:T(8,128)(2,1)S(1)}, u32[]{:S(2)}, u32[]{:S(2)}) %collective-permute-start.25) | collective-permute-done | bytes 196640 | tf_op jit(solution)/shard_map/ppermute | solution.py:45
  139.3 3.7 %collective-permute-done.27 = bf16[48,2048]{1,0:T(8,128)(2,1)S(1)} collective-permute-done((bf16[48,2048]{1,0:T(8,128)(2,1)S(1)}, bf16[48,2048]{1,0:T(8,128)(2,1)S(1)}, u32[]{:S(2)}, u32[]{:S(2)}) %collective-permute-start.27) | collective-permute-done | bytes 196640 | tf_op jit(solution)/shard_map/ppermute | solution.py:45
  143.3 1.1 fusion.12
  (75 shorter events, 5.3 us)
Async XLA Ops:
  0.7 25.2 %copy-start.4 = (bf16[1,1,96,3072]{3,2,1,0:T(8,128)(2,1)S(1)}, bf16[1,1,96,3072]{3,2,1,0:T(8,128)(2,1)}, u32[]{:S(2)}) copy-start(bf16[1,1,96,3072]{3,2,1,0:T(8,128)(2,1)} %param.10) | copy-start | bytes 1769476
  1.8 9.1 %collective-permute-start.15 = (bf16[48,1024]{1,0:T(8,128)(2,1)S(1)}, bf16[48,1024]{1,0:T(8,128)(2,1)S(1)}, u32[]{:S(2)}, u32[]{:S(2)}) collective-permute-start(bf16[48,1024]{1,0:T(8,128)(2,1)S(1)} %get-tuple-element.31), channel_id=1, source_target_pairs={{0,1},{1,0},{2,3},{3,2},{4,5},{5,4},{6,7},{7,6},{8,9},{9,8},{10,11... | collective-permute-start | bytes 294920 | tf_op jit(solution)/shard_map/ppermute | solution.py:41
  5.0 18.9 %collective-permute-start.17 = (bf16[48,1024]{1,0:T(8,128)(2,1)S(1)}, bf16[48,1024]{1,0:T(8,128)(2,1)S(1)}, u32[]{:S(2)}, u32[]{:S(2)}) collective-permute-start(bf16[48,1024]{1,0:T(8,128)(2,1)S(1)} %get-tuple-element.33), channel_id=1, source_target_pairs={{0,2},{1,3},{2,0},{3,1},{4,6},{5,7},{6,4},{7,5},{8,10},{9,11},{10,... | collective-permute-start | bytes 294920 | tf_op jit(solution)/shard_map/ppermute | solution.py:41
  7.5 16.3 %collective-permute-start.19 = (bf16[48,1024]{1,0:T(8,128)(2,1)S(1)}, bf16[48,1024]{1,0:T(8,128)(2,1)S(1)}, u32[]{:S(2)}, u32[]{:S(2)}) collective-permute-start(bf16[48,1024]{1,0:T(8,128)(2,1)S(1)} %get-tuple-element.30), channel_id=1, source_target_pairs={{0,3},{1,2},{2,1},{3,0},{4,7},{5,6},{6,5},{7,4},{8,11},{9,10},{10,... | collective-permute-start | bytes 294920 | tf_op jit(solution)/shard_map/ppermute | solution.py:41
  7.5 19.1 %copy-start.8 = (bf16[1,1,48,4096]{3,2,1,0:T(8,128)(2,1)S(1)}, bf16[1,1,48,4096]{3,2,1,0:T(8,128)(2,1)}, u32[]{:S(2)}) copy-start(bf16[1,1,48,4096]{3,2,1,0:T(8,128)(2,1)} %param.8) | copy-start | bytes 1179652
  7.5 20.6 %copy-start.5 = (bf16[1,1,48,4096]{3,2,1,0:T(8,128)(2,1)S(1)}, bf16[1,1,48,4096]{3,2,1,0:T(8,128)(2,1)}, u32[]{:S(2)}) copy-start(bf16[1,1,48,4096]{3,2,1,0:T(8,128)(2,1)} %param.9) | copy-start | bytes 1179652
  7.5 17.8 %collective-permute-start.14 = (bf16[48,1024]{1,0:T(8,128)(2,1)S(1)}, bf16[48,1024]{1,0:T(8,128)(2,1)S(1)}, u32[]{:S(2)}, u32[]{:S(2)}) collective-permute-start(bf16[48,1024]{1,0:T(8,128)(2,1)S(1)} %get-tuple-element.32.refs_0_), channel_id=1, source_target_pairs={{0,4},{4,0},{1,5},{5,1},{2,6},{6,2},{3,7},{7,3},{8,12},{12,8},{9,1... | collective-permute-start | bytes 294920 | tf_op jit(solution)/shard_map/ppermute | solution.py:51
  9.0 24.3 %collective-permute-start.2 = (bf16[48,4096]{1,0:T(8,128)(2,1)S(1)}, bf16[48,4096]{1,0:T(8,128)(2,1)S(1)}, u32[]{:S(2)}, u32[]{:S(2)}) collective-permute-start(bf16[48,4096]{1,0:T(8,128)(2,1)S(1)} %fusion.2.refs_1_), channel_id=1, source_target_pairs={{0,2},{1,3},{2,0},{3,1},{4,6},{5,7},{6,4},{7,5},{8,10},{9,11},{10,... | collective-permute-start | bytes 1179656 | tf_op jit(solution)/shard_map/ppermute | solution.py:41
  11.0 14.6 %collective-permute-start.16 = (bf16[48,1024]{1,0:T(8,128)(2,1)S(1)}, bf16[48,1024]{1,0:T(8,128)(2,1)S(1)}, u32[]{:S(2)}, u32[]{:S(2)}) collective-permute-start(bf16[48,1024]{1,0:T(8,128)(2,1)S(1)} %collective-permute-done.15.refs_2_), channel_id=1, source_target_pairs={{0,4},{4,0},{1,5},{5,1},{2,6},{6,2},{3,7},{7,3},{8,12},{12,8},{9,1... | collective-permute-start | bytes 294920 | tf_op jit(solution)/shard_map/ppermute | solution.py:51
  23.8 15.3 %collective-permute-start.1 = (bf16[48,4096]{1,0:T(8,128)(2,1)S(1)}, bf16[48,4096]{1,0:T(8,128)(2,1)S(1)}, u32[]{:S(2)}, u32[]{:S(2)}) collective-permute-start(bf16[48,4096]{1,0:T(8,128)(2,1)S(1)} %fusion.2.refs_1_), channel_id=1, source_target_pairs={{0,4},{4,0},{1,5},{5,1},{2,6},{6,2},{3,7},{7,3},{8,12},{12,8},{9,1... | collective-permute-start | bytes 1179656 | tf_op jit(solution)/shard_map/ppermute | solution.py:51
  23.9 15.0 %collective-permute-start = (bf16[48,4096]{1,0:T(8,128)(2,1)S(1)}, bf16[48,4096]{1,0:T(8,128)(2,1)S(1)}, u32[]{:S(2)}, u32[]{:S(2)}) collective-permute-start(bf16[48,4096]{1,0:T(8,128)(2,1)S(1)} %bitcast.48), channel_id=1, source_target_pairs={{0,8},{8,16},{16,24},{24,0},{1,9},{9,17},{17,25},{25,1},{2,10},{10... | collective-permute-start | bytes 1179656 | tf_op jit(solution)/shard_map/ppermute | solution.py:45
  25.4 1.3 collective-permute-start.18
  25.6 2.6 %collective-permute-start.20 = (bf16[48,1024]{1,0:T(8,128)(2,1)S(1)}, bf16[48,1024]{1,0:T(8,128)(2,1)S(1)}, u32[]{:S(2)}, u32[]{:S(2)}) collective-permute-start(bf16[48,1024]{1,0:T(8,128)(2,1)S(1)} %collective-permute-done.19.refs_6_), channel_id=1, source_target_pairs={{0,4},{4,0},{1,5},{5,1},{2,6},{6,2},{3,7},{7,3},{8,12},{12,8},{9,1... | collective-permute-start | bytes 294920 | tf_op jit(solution)/shard_map/ppermute | solution.py:51
  26.7 103.9 %collective-permute-start.13 = (bf16[48,4096]{1,0:T(8,128)(2,1)S(1)}, bf16[48,4096]{1,0:T(8,128)(2,1)S(1)}, u32[]{:S(2)}, u32[]{:S(2)}) collective-permute-start(bf16[48,4096]{1,0:T(8,128)(2,1)S(1)} %bitcast.55), channel_id=1, source_target_pairs={{0,24},{8,0},{16,8},{24,16},{1,25},{9,1},{17,9},{25,17},{2,26},{10... | collective-permute-start | bytes 1179656 | tf_op jit(solution)/shard_map/ppermute | solution.py:45
  28.2 115.2 %collective-permute-start.12 = (bf16[48,4096]{1,0:T(8,128)(2,1)S(1)}, bf16[48,4096]{1,0:T(8,128)(2,1)S(1)}, u32[]{:S(2)}, u32[]{:S(2)}) collective-permute-start(bf16[48,4096]{1,0:T(8,128)(2,1)S(1)} %bitcast.51), channel_id=1, source_target_pairs={{0,24},{8,0},{16,8},{24,16},{1,25},{9,1},{17,9},{25,17},{2,26},{10... | collective-permute-start | bytes 1179656 | tf_op jit(solution)/shard_map/ppermute | solution.py:45
  33.3 17.4 %collective-permute-start.3 = (bf16[48,4096]{1,0:T(8,128)(2,1)S(1)}, bf16[48,4096]{1,0:T(8,128)(2,1)S(1)}, u32[]{:S(2)}, u32[]{:S(2)}) collective-permute-start(bf16[48,4096]{1,0:T(8,128)(2,1)S(1)} %collective-permute-done.2.refs_1_), channel_id=1, source_target_pairs={{0,4},{4,0},{1,5},{5,1},{2,6},{6,2},{3,7},{7,3},{8,12},{12,8},{9,1... | collective-permute-start | bytes 1179656 | tf_op jit(solution)/shard_map/ppermute | solution.py:51
  38.8 23.3 %collective-permute-start.22 = (bf16[96,2304]{1,0:T(8,128)(2,1)S(1)}, bf16[96,2304]{1,0:T(8,128)(2,1)S(1)}, u32[]{:S(2)}, u32[]{:S(2)}) collective-permute-start(bf16[96,2304]{1,0:T(8,128)(2,1)S(1)} %get-tuple-element.22), channel_id=1, source_target_pairs={{0,1},{1,0},{2,3},{3,2},{4,5},{5,4},{6,7},{7,6},{8,9},{9,8},{10,11... | collective-permute-start | bytes 1327112 | tf_op jit(solution)/shard_map/ppermute | solution.py:41
  39.1 27.5 %collective-permute-start.21 = (bf16[96,2304]{1,0:T(8,128)(2,1)S(1)}, bf16[96,2304]{1,0:T(8,128)(2,1)S(1)}, u32[]{:S(2)}, u32[]{:S(2)}) collective-permute-start(bf16[96,2304]{1,0:T(8,128)(2,1)S(1)} %get-tuple-element.20), channel_id=1, source_target_pairs={{0,1},{1,0},{2,3},{3,2},{4,5},{5,4},{6,7},{7,6},{8,9},{9,8},{10,11... | collective-permute-start | bytes 1327112 | tf_op jit(solution)/shard_map/ppermute | solution.py:41
  41.0 19.4 %slice-start = ((s8[4718592]{0:T(1024)(128)(4,1)}), s8[4194304]{0:T(1024)(128)(4,1)S(1)}, s32[]{:S(2)}) async-start(s8[4718592]{0:T(1024)(128)(4,1)} %bitcast.44), calls=%async_computation | async-start | bytes 8388608
  50.6 74.2 %collective-permute-start.7 = (bf16[96,2304]{1,0:T(8,128)(2,1)S(1)}, bf16[96,2304]{1,0:T(8,128)(2,1)S(1)}, u32[]{:S(2)}, u32[]{:S(2)}) collective-permute-start(bf16[96,2304]{1,0:T(8,128)(2,1)S(1)} %shard_map.86.refs_0_), channel_id=1, source_target_pairs={{0,1},{1,0},{2,3},{3,2},{4,5},{5,4},{6,7},{7,6},{8,9},{9,8},{10,11... | collective-permute-start | bytes 1327112 | tf_op jit(solution)/shard_map/ppermute | solution.py:41
  62.1 1.5 %collective-permute-start.4 = (bf16[96,1024]{1,0:T(8,128)(2,1)S(1)}, bf16[96,1024]{1,0:T(8,128)(2,1)S(1)}, u32[]{:S(2)}, u32[]{:S(2)}) collective-permute-start(bf16[96,1024]{1,0:T(8,128)(2,1)S(1)} %get-tuple-element.16), channel_id=1, source_target_pairs={{0,4},{4,0},{1,5},{5,1},{2,6},{6,2},{3,7},{7,3},{8,12},{12,8},{9,1... | collective-permute-start | bytes 589832 | tf_op jit(solution)/shard_map/ppermute | solution.py:59
  63.6 23.0 %collective-permute-start.23 = (bf16[96,2304]{1,0:T(8,128)(2,1)S(1)}, bf16[96,2304]{1,0:T(8,128)(2,1)S(1)}, u32[]{:S(2)}, u32[]{:S(2)}) collective-permute-start(bf16[96,2304]{1,0:T(8,128)(2,1)S(1)} %add_convert_fusion), channel_id=1, source_target_pairs={{0,2},{1,3},{2,0},{3,1},{4,6},{5,7},{6,4},{7,5},{8,10},{9,11},{10,... | collective-permute-start | bytes 1327112 | tf_op jit(solution)/shard_map/ppermute | solution.py:41
  66.6 58.9 %collective-permute-start.8 = (bf16[96,2304]{1,0:T(8,128)(2,1)S(1)}, bf16[96,2304]{1,0:T(8,128)(2,1)S(1)}, u32[]{:S(2)}, u32[]{:S(2)}) collective-permute-start(bf16[96,2304]{1,0:T(8,128)(2,1)S(1)} %shard_map.87.refs_1_), channel_id=1, source_target_pairs={{0,1},{1,0},{2,3},{3,2},{4,5},{5,4},{6,7},{7,6},{8,9},{9,8},{10,11... | collective-permute-start | bytes 1327112 | tf_op jit(solution)/shard_map/ppermute | solution.py:41
  86.6 30.5 %collective-permute-start.5 = (bf16[48,1024]{1,0:T(8,128)(2,1)S(1)}, bf16[48,1024]{1,0:T(8,128)(2,1)S(1)}, u32[]{:S(2)}, u32[]{:S(2)}) collective-permute-start(bf16[48,1024]{1,0:T(8,128)(2,1)S(1)} %get-tuple-element.37), channel_id=1, source_target_pairs={{0,8},{1,9},{2,10},{3,11},{8,16},{9,17},{10,18},{11,19},{16,24},{1... | collective-permute-start | bytes 294920 | tf_op jit(solution)/shard_map/ppermute | solution.py:421
  117.1 7.7 %collective-permute-start.6 = (bf16[48,1024]{1,0:T(8,128)(2,1)S(1)}, bf16[48,1024]{1,0:T(8,128)(2,1)S(1)}, u32[]{:S(2)}, u32[]{:S(2)}) collective-permute-start(bf16[48,1024]{1,0:T(8,128)(2,1)S(1)} %get-tuple-element.36), channel_id=1, source_target_pairs={{0,10},{1,11},{2,8},{3,9},{8,18},{9,19},{10,16},{11,17},{16,26},{1... | collective-permute-start | bytes 294920 | tf_op jit(solution)/shard_map/ppermute | solution.py:421
  124.8 2.4 %collective-permute-start.24 = (bf16[48,2048]{1,0:T(8,128)(2,1)S(1)}, bf16[48,2048]{1,0:T(8,128)(2,1)S(1)}, u32[]{:S(2)}, u32[]{:S(2)}) collective-permute-start(bf16[48,2048]{1,0:T(8,128)(2,1)S(1)} %get-tuple-element.24), channel_id=1, source_target_pairs={{0,4},{4,0},{1,5},{5,1},{2,6},{6,2},{3,7},{7,3},{8,12},{12,8},{9,1... | collective-permute-start | bytes 589832 | tf_op jit(solution)/shard_map/ppermute | solution.py:59
  124.9 3.3 %collective-permute-start.26 = (bf16[48,2048]{1,0:T(8,128)(2,1)S(1)}, bf16[48,2048]{1,0:T(8,128)(2,1)S(1)}, u32[]{:S(2)}, u32[]{:S(2)}) collective-permute-start(bf16[48,2048]{1,0:T(8,128)(2,1)S(1)} %get-tuple-element.27), channel_id=1, source_target_pairs={{0,4},{4,0},{1,5},{5,1},{2,6},{6,2},{3,7},{7,3},{8,12},{12,8},{9,1... | collective-permute-start | bytes 589832 | tf_op jit(solution)/shard_map/ppermute | solution.py:59
  127.1 3.3 %collective-permute-start.9 = (bf16[96,1024]{1,0:T(8,128)(2,1)S(1)}, bf16[96,1024]{1,0:T(8,128)(2,1)S(1)}, u32[]{:S(2)}, u32[]{:S(2)}) collective-permute-start(bf16[96,1024]{1,0:T(8,128)(2,1)S(1)} %get-tuple-element.18), channel_id=1, source_target_pairs={{0,4},{4,0},{1,5},{5,1},{2,6},{6,2},{3,7},{7,3},{8,12},{12,8},{9,1... | collective-permute-start | bytes 589832 | tf_op jit(solution)/shard_map/ppermute | solution.py:59
  127.3 12.0 %collective-permute-start.25 = (bf16[48,2048]{1,0:T(8,128)(2,1)S(1)}, bf16[48,2048]{1,0:T(8,128)(2,1)S(1)}, u32[]{:S(2)}, u32[]{:S(2)}) collective-permute-start(bf16[48,2048]{1,0:T(8,128)(2,1)S(1)} %multiply_convert_fusion.1), channel_id=1, source_target_pairs={{0,24},{8,0},{16,8},{24,16},{1,25},{9,1},{17,9},{25,17},{2,26},{10... | collective-permute-start | bytes 589832 | tf_op jit(solution)/shard_map/ppermute | solution.py:45
  128.3 14.8 %collective-permute-start.27 = (bf16[48,2048]{1,0:T(8,128)(2,1)S(1)}, bf16[48,2048]{1,0:T(8,128)(2,1)S(1)}, u32[]{:S(2)}, u32[]{:S(2)}) collective-permute-start(bf16[48,2048]{1,0:T(8,128)(2,1)S(1)} %multiply_convert_fusion), channel_id=1, source_target_pairs={{0,24},{8,0},{16,8},{24,16},{1,25},{9,1},{17,9},{25,17},{2,26},{10... | collective-permute-start | bytes 589832 | tf_op jit(solution)/shard_map/ppermute | solution.py:45
  130.5 13.9 %collective-permute-start.10 = (bf16[48,1024]{1,0:T(8,128)(2,1)S(1)}, bf16[48,1024]{1,0:T(8,128)(2,1)S(1)}, u32[]{:S(2)}, u32[]{:S(2)}) collective-permute-start(bf16[48,1024]{1,0:T(8,128)(2,1)S(1)} %get-tuple-element.35), channel_id=1, source_target_pairs={{0,9},{1,8},{2,11},{3,10},{8,17},{9,16},{10,19},{11,18},{16,25},{1... | collective-permute-start | bytes 294920 | tf_op jit(solution)/shard_map/ppermute | solution.py:421
  130.6 13.9 %collective-permute-start.11 = (bf16[48,1024]{1,0:T(8,128)(2,1)S(1)}, bf16[48,1024]{1,0:T(8,128)(2,1)S(1)}, u32[]{:S(2)}, u32[]{:S(2)}) collective-permute-start(bf16[48,1024]{1,0:T(8,128)(2,1)S(1)} %get-tuple-element.34), channel_id=1, source_target_pairs={{0,11},{1,10},{2,9},{3,8},{8,19},{9,18},{10,17},{11,16},{16,27},{1... | collective-permute-start | bytes 294920 | tf_op jit(solution)/shard_map/ppermute | solution.py:421
  (7 other events, 45.6 us)
where the time goes:
time: 146 us; the launch traced here: 145 us
  waiting for transfers between devices  55.9 us (38%)
  Pallas kernels  38.3 us (26%)
  starting transfers between devices  25.8 us (18%)
  local copies, waits for them, and re-layouts  20.6 us (14%)
  other arithmetic  3.65 us (2%)
    pallas_call x7, Pallas kernels, call(): pl.pallas_call(body, in_specs=[SCALAR if arg.dtype == jnp.int32 else LOCA...  38.3 us
    ppermute x9, waiting for transfers between devices, over_dp(): return lax.ppermute(value, 'dp', partner_pairs(lax.axis_size('dp'), step))  36.2 us
    unnamed x23, local copies, waits for them, and re-layouts  19.4 us
    ppermute x9, starting transfers between devices, over_dp(): return lax.ppermute(value, 'dp', partner_pairs(lax.axis_size('dp'), step))  13.2 us
    ppermute x5, waiting for transfers between devices, over_pipe(): lax.ppermute(value, 'pipe', shift_pairs(lax.axis_size('pipe'), steps))  10.9 us
    ppermute x5, starting transfers between devices, over_pipe(): lax.ppermute(value, 'pipe', shift_pairs(lax.axis_size('pipe'), steps))  7.55 us
    ppermute x4, waiting for transfers between devices, window(): lax.ppermute(summed[index * rows:(index + 1) * rows], ('pipe', 'dp'), cro...  7.14 us
    ppermute x4, starting transfers between devices, window(): lax.ppermute(summed[index * rows:(index + 1) * rows], ('pipe', 'dp'), cro...  3.65 us
  transfers between devices with their start and end apart: 28, of which 8 were waited for; matrix products, arithmetic and copies ran while one was open for 3% of the time, Pallas kernels for 26%

commit v1 on v0

--- a/solution.py
+++ b/solution.py
@@ -21,10 +21,6 @@
     if count & (count - 1):
         raise ValueError("dp size")
     return [(source, source ^ step) for source in range(count)]
-
-
-def partner_index(axis, step):
-    return jnp.bitwise_xor(lax.axis_index(axis), step)
 
 
 def cross_pairs(step, forward):
@@ -159,50 +155,67 @@
 REMOTE = pl.BlockSpec(memory_space=pltpu.HBM)
 
 
-def call(kernel, args, weight, outs, copies, block, scratch, flops):
+def call(kernel, args, weight, outs, blocks, keep, flops):
     count = len(args)
+    moved = 0
+    if blocks:
+        shape = (len(blocks), blocks[0][0].size, blocks[0][1].size)
+        moved = 2 * math.prod(shape)
 
     def body(*refs):
         ins, weight_ref = refs[:count], refs[count]
         results = refs[count + 1 : count + 1 + len(outs)]
-        held, sems, *rest = refs[count + 1 + len(outs) :]
+        if not blocks:
+            kernel(ins, results, weight_ref, lambda index: None)
+            return
+        held, sems = refs[count + 1 + len(outs) :]
         moves = [
-            pltpu.make_async_copy(
-                weight_ref.at[pl.ds(row, block[0]), pl.ds(column, block[1])],
-                held.at[index],
-                sems.at[index],
-            )
-            for index, (row, column) in enumerate(copies)
+            pltpu.make_async_copy(weight_ref.at[part], held.at[index], sems.at[index])
+            for index, part in enumerate(blocks)
         ]
         for move in moves:
             move.start()
-        kernel(ins, results, held, lambda index: moves[index].wait(), *rest)
-
-    moved = 2 * len(copies) * block[0] * block[1]
+        kernel(ins, results, held, lambda index: moves[index].wait())
+
+    out_specs = [LOCAL for _ in outs]
+    out_shape = [jax.ShapeDtypeStruct(out, jnp.bfloat16) for out in outs]
+    scratch = []
+    if blocks:
+        scratch = [pltpu.SemaphoreType.DMA((len(blocks),))]
+        if keep:
+            out_specs.append(LOCAL)
+            out_shape.append(pltpu.VMEM(shape, jnp.bfloat16))
+        else:
+            scratch.insert(0, pltpu.VMEM(shape, jnp.bfloat16))
+        weight = pltpu.with_memory_space_constraint(weight, pltpu.HBM)
+    else:
+        weight = pltpu.with_memory_space_constraint(weight, pltpu.VMEM)
+    limit = (0 if keep else moved) + (8 << 20)
     return pl.pallas_call(
         body,
-        in_specs=[SCALAR if arg.dtype == jnp.int32 else LOCAL for arg in args] + [REMOTE],
-        out_specs=[LOCAL for _ in outs],
-        out_shape=[jax.ShapeDtypeStruct(shape, jnp.bfloat16) for shape in outs],
-        scratch_shapes=[
-            pltpu.VMEM((len(copies),) + block, jnp.bfloat16),
-            pltpu.SemaphoreType.DMA((len(copies),)),
-        ]
-        + scratch,
-        compiler_params=pltpu.CompilerParams(vmem_limit_bytes=moved + (8 << 20)),
+        in_specs=[SCALAR if arg.dtype == jnp.int32 else LOCAL for arg in args]
+        + [REMOTE if blocks else LOCAL],
+        out_specs=out_specs,
+        out_shape=out_shape,
+        scratch_shapes=scratch,
+        compiler_params=pltpu.CompilerParams(vmem_limit_bytes=limit),
         cost_estimate=pl.CostEstimate(flops=flops, bytes_accessed=moved, transcendentals=0),
     )(*args, weight)
 
 
-def forward_heads(blocks, weight, start):
-    rows, width = blocks[0].shape
-    length = rows * len(blocks)
-    merged = weight.shape[1]
-    units = merged // UNIT
+def row_blocks(size, columns, most):
+    block = divisor(size, most)
+    return [(pl.ds(row, block), pl.ds(0, columns)) for row in range(0, size, block)]
+
+
+def forward_heads(parts, weight, held, start):
+    rows, width = parts[0].shape
+    length = rows * len(parts)
+    units = weight.shape[1] // UNIT
     depth = divisor(width, 1024)
     steps = width // depth
 
-    def kernel(ins, outs, held, wait):
+    def kernel(ins, outs, blocks, wait):
         masked = later_keys(length, ins[0][0])
         for unit in range(units):
             total = None
@@ -210,33 +223,33 @@
                 at = slice(step * depth, (step + 1) * depth)
                 left = jnp.concatenate([ref[:, at] for ref in ins[1:]], axis=0)
                 wait(unit * steps + step)
-                product = mxu(left, held[unit * steps + step], 1, 0)
+                product = mxu(left, blocks[unit * steps + step], 1, 0)
                 total = product if total is None else total + product
             attend_unit(total.astype(jnp.bfloat16), masked, outs[0], unit * GROUP * HD)
 
-    copies = [(step * depth, unit * UNIT) for unit in range(units) for step in range(steps)]
-    return call(
-        kernel,
-        [start] + blocks,
-        weight,
-        [(length, units * GROUP * HD)],
-        copies,
-        (depth, UNIT),
-        [],
-        2 * length * width * merged,
-    )[0]
+    blocks = [
+        (pl.ds(step * depth, depth), pl.ds(unit * UNIT, UNIT))
+        for unit in range(units)
+        for step in range(steps)
+    ]
+    flops = 2 * length * width * units * UNIT
+    outs = [(length, units * GROUP * HD)]
+    if held is None:
+        return call(kernel, [start] + parts, weight, outs, blocks, True, flops)
+    return call(kernel, [start] + parts, held, outs, [], False, flops)[0]
 
 
 def head_terms(pieces, weight):
     rows, columns = pieces[0][0].shape
     length = rows * len(pieces[0])
     depth = weight.shape[0]
-    block = divisor(depth, 768)
     flat = [part for parts in pieces for part in parts]
+    blocks = row_blocks(depth, columns, 768)
+    block = depth // len(blocks)
 
     def kernel(ins, outs, held, wait):
         left = jnp.concatenate([ref[...] for ref in ins], axis=0)
-        for step in range(depth // block):
+        for step in range(len(blocks)):
             wait(step)
             product = mxu(left, held[step], 1, 1).astype(jnp.bfloat16)
             for index, out_ref in enumerate(outs):
@@ -244,32 +257,23 @@
                     index * length : (index + 1) * length
                 ]
 
-    return call(
-        kernel,
-        flat,
-        weight,
-        [(length, depth) for _ in pieces],
-        [(row, 0) for row in range(0, depth, block)],
-        (block, columns),
-        [],
-        2 * len(pieces) * length * depth * columns,
-    )
-
-
-def project(heads, weight, cores):
+    outs = [(length, depth) for _ in pieces]
+    flops = 2 * len(pieces) * length * depth * columns
+    *terms, held = call(kernel, flat, weight, outs, blocks, True, flops)
+    return terms, held
+
+
+def project(heads, held, cores):
     length, depth = heads[0].shape
-    columns = weight.shape[1]
+    count, (steps, block, columns) = len(heads), held.shape
     rows = length // cores
-    block = divisor(depth, 768)
-    count = len(heads)
-
-    def kernel(ins, outs, held, wait):
+
+    def kernel(ins, outs, blocks, wait):
         total = None
-        for step in range(depth // block):
+        for step in range(steps):
             at = slice(step * block, (step + 1) * block)
             left = jnp.concatenate([ref[:, at] for ref in ins], axis=0)
-            wait(step)
-            product = mxu(left, held[step], 1, 0)
+            product = mxu(left, blocks[step], 1, 0)
             total = product if total is None else total + product
         total = total.astype(jnp.bfloat16)
         for core, out_ref in enumerate(outs):
@@ -277,77 +281,89 @@
                 at = index * length + core * rows
                 out_ref[index * rows : (index + 1) * rows] = total[at : at + rows]
 
-    return call(
-        kernel,
-        heads,
-        weight,
-        [(count * rows, columns) for _ in range(cores)],
-        [(row, 0) for row in range(0, depth, block)],
-        (block, columns),
-        [],
-        2 * count * length * depth * columns,
-    )
-
-
-def back_columns(grad, outs, held, wait, cores, steps, block):
-    rows = grad.shape[0] // cores
-    for step in range(steps):
-        wait(step)
-        product = mxu(grad, held[step], 1, 1).astype(jnp.bfloat16)
+    outs = [(count * rows, columns) for _ in range(cores)]
+    flops = 2 * count * length * depth * columns
+    return call(kernel, heads, held, outs, [], False, flops)
+
+
+def back_columns(grad_ref, outs, held, picked, steps):
+    depth = held.shape[1]
+    units = held.shape[0] // steps
+    rows = grad_ref.shape[0] // len(outs)
+    for place, step in enumerate(picked):
+        total = None
+        for unit in range(units):
+            grads = grad_ref[:, unit * UNIT : (unit + 1) * UNIT]
+            product = mxu(grads, held[unit * steps + step], 1, 1)
+            total = product if total is None else total + product
+        total = total.astype(jnp.bfloat16)
         for core, out_ref in enumerate(outs):
-            out_ref[:, step * block : (step + 1) * block] = product[
+            out_ref[:, place * depth : (place + 1) * depth] = total[
                 core * rows : (core + 1) * rows
             ]
 
 
-def back_first(qkv, terms, weight, start, cores, steps, block):
+def back_first(qkv, terms, held, start, cores, picked, steps):
     length, merged = qkv.shape
-    units = merged // UNIT
     rows = length // cores
 
-    def kernel(ins, outs, held, wait):
-        masked = later_keys(length, ins[0][0])
-        for unit in range(units):
+    def kernel(ins, outs, blocks, wait):
+        start = ins[0][0]
+        masked = later_keys(length, start)
+        ranges = []
+        for core in range(cores):
+            at = start + core * rows
+            at = jnp.where(at >= length, at - length, at)
+            ranges.append(pl.ds(pl.multiple_of(at, rows), rows))
+        rolled = jnp.concatenate([ins[1][part] for part in ranges], axis=0)
+        for unit in range(merged // UNIT):
             at = unit * UNIT
             part = slice(unit * GROUP * HD, (unit + 1) * GROUP * HD)
             grads = ins[2][:, part].astype(jnp.float32)
             for ref in ins[3:]:
                 grads = grads + ref[:, part].astype(jnp.float32)
             attend_back_unit(
-                ins[1][:, at : at + UNIT], grads.astype(jnp.bfloat16), masked, outs[0], at
+                rolled[:, at : at + UNIT], grads.astype(jnp.bfloat16), masked, outs[0], at
             )
-        back_columns(outs[0][...], outs[1:], held, wait, cores, steps, block)
-
-    results = call(
+        back_columns(outs[0], outs[1:], blocks, picked, steps)
+
+    columns = len(picked) * held.shape[1]
+    outs = [qkv.shape] + [(rows, columns) for _ in range(cores)]
+    flops = 2 * length * merged * columns
+    results = call(kernel, [start, qkv] + terms, held, outs, [], False, flops)
+    return results[0], results[1:]
+
+
+def back_rest(grad_qkv, held, cores, picked, steps):
+    length, merged = grad_qkv.shape
+
+    def kernel(ins, outs, blocks, wait):
+        back_columns(ins[0], outs, blocks, picked, steps)
+
+    columns = len(picked) * held.shape[1]
+    outs = [(length // cores, columns) for _ in range(cores)]
+    flops = 2 * length * merged * columns
+    return call(kernel, [grad_qkv], held, outs, [], False, flops)
+
+
+def add_landed(words, residual, pieces):
+    columns = pieces[0].shape[1]
+
+    def kernel(words_ref, residual_ref, *refs):
+        out_ref = refs[-1]
+        for step, piece_ref in enumerate(refs[:-1]):
+            at = pl.ds(pl.multiple_of(words_ref[1 + step], columns), columns)
+            total = residual_ref[:, at].astype(jnp.float32) + piece_ref[...].astype(jnp.float32)
+            out_ref[:, at] = total.astype(jnp.bfloat16)
+
+    return pl.pallas_call(
         kernel,
-        [start, qkv] + terms,
-        weight,
-        [qkv.shape] + [(rows, steps * block) for _ in range(cores)],
-        [(step * block, 0) for step in range(steps)],
-        (block, merged),
-        [],
-        2 * length * merged * steps * block,
-    )
-    return results[0], results[1:]
-
-
-def back_rest(grad_qkv, weight, cores, first, steps, block):
-    length, merged = grad_qkv.shape
-    rows = length // cores
-
-    def kernel(ins, outs, held, wait):
-        back_columns(ins[0][...], outs, held, wait, cores, steps, block)
-
-    return call(
-        kernel,
-        [grad_qkv],
-        weight,
-        [(rows, steps * block) for _ in range(cores)],
-        [((first + step) * block, 0) for step in range(steps)],
-        (block, merged),
-        [],
-        2 * length * merged * steps * block,
-    )
+        in_specs=[SCALAR] + [LOCAL for _ in range(1 + len(pieces))],
+        out_specs=LOCAL,
+        out_shape=jax.ShapeDtypeStruct(residual.shape, jnp.bfloat16),
+        compiler_params=pltpu.CompilerParams(vmem_limit_bytes=8 << 20),
+        name="add_landed",
+    )(words, residual, *pieces)
 
 
 def per_device(x_fwd, x_bwd, grad_out, saved_qkv, norm_gain, w_qkv, w_out):
@@ -367,13 +383,13 @@
     cores = lax.axis_size("tensor")
     replicas = lax.axis_size("dp")
     columns = weight_out.shape[1]
-    start = lax.axis_index("tensor") * rows
-    start_word = jnp.full((1,), start, jnp.int32)
+    places = jnp.bitwise_xor(lax.axis_index("dp"), jnp.arange(replicas, dtype=jnp.int32)) * columns
+    words = jnp.concatenate([jnp.full((1,), lax.axis_index("tensor") * rows), places])
     if replicas != 4:
         raise ValueError("dp size")
 
     def grad_piece(step):
-        at = partner_index("dp", step) * columns
+        at = jnp.bitwise_xor(lax.axis_index("dp"), step) * columns
         return lax.dynamic_slice_in_dim(grad_rows, at, columns, axis=1)
 
     pieces = [grad_piece(0)]
@@ -381,13 +397,14 @@
 
     normed_rows = normalize(fwd_rows, gain_row)
     normed_far = over_dp(normed_rows, 2)
-    own_heads = forward_heads(blocks_of_cores(normed_rows), weight_qkv, start_word)
-    far_heads = forward_heads(blocks_of_cores(normed_far), weight_qkv, start_word)
-    near_heads = over_dp(own_heads, 1)
+    normed_near = over_dp(normed_rows, 1)
+    own_heads, held = forward_heads(blocks_of_cores(normed_rows), weight_qkv, None, words)
+    far_heads = forward_heads(blocks_of_cores(normed_far), weight_qkv, held, words)
+    near_heads = forward_heads(blocks_of_cores(normed_near), weight_qkv, held, words)
     last_heads = over_dp(far_heads, 1)
 
     exchanged = [blocks_of_cores(piece) for piece in pieces]
-    terms = head_terms(exchanged, weight_out)
+    terms, held_out = head_terms(exchanged, weight_out)
     relay = over_dp(terms[3], 1)
     near = over_dp(terms[1], 1)
     joined = (terms[2].astype(jnp.float32) + relay.astype(jnp.float32)).astype(jnp.bfloat16)
@@ -397,36 +414,30 @@
     bwd_next = over_pipe(bwd_rows, -1)
     grad_next = over_pipe(grad_rows, -1)
 
-    qkv_rolled = jnp.roll(qkv_saved, -start, axis=0)
-    half = width // 2
-    block = divisor(half, 512)
-    steps = half // block
-    grad_qkv, (keep, *sends) = back_first(
-        qkv_rolled, terms, weight_qkv, start_word, cores, steps, block
-    )
+    steps = width // held.shape[1]
+    first, rest = range(steps // 2), range(steps // 2, steps)
+    half = len(first) * held.shape[1]
+    grad_qkv, (keep, *sends) = back_first(qkv_saved, terms, held, words, cores, first, steps)
     scaled = sum_over_cores(keep, sends) * gain_row[:, :half]
     arrived = [over_pipe(scaled.astype(jnp.bfloat16), -1)]
-    keep, *sends = back_rest(grad_qkv, weight_qkv, cores, steps, steps, block)
+    keep, *sends = back_rest(grad_qkv, held, cores, rest, steps)
     scaled = sum_over_cores(keep, sends) * gain_row[:, half:]
     arrived.append(over_pipe(scaled.astype(jnp.bfloat16), -1))
     scaled = jnp.concatenate(arrived, axis=1).astype(jnp.float32)
     grad_input = norm_back(bwd_next, grad_next, scaled)
 
-    output = fwd_prev
-    groups = (((0, 2), [own_heads, far_heads]), ((1, 3), [near_heads, last_heads]))
+    landed = {}
+    groups = (((0, 1, 2), [own_heads, near_heads, far_heads]), ((3,), [last_heads]))
     for group, heads in groups:
-        keep, *sends = project(heads, weight_out, cores)
+        keep, *sends = project(heads, held_out, cores)
         summed = sum_over_cores(keep, sends).astype(jnp.bfloat16)
         for index, step in enumerate(group):
-            piece = lax.ppermute(
+            landed[step] = lax.ppermute(
                 summed[index * rows : (index + 1) * rows],
                 ("pipe", "dp"),
                 cross_pairs(step, 1),
             )
-            at = partner_index("dp", step) * columns
-            part = lax.dynamic_slice_in_dim(fwd_prev, at, columns, axis=1).astype(jnp.float32)
-            part = (part + piece.astype(jnp.float32)).astype(jnp.bfloat16)
-            output = lax.dynamic_update_slice_in_dim(output, part, at, axis=1)
+    output = add_landed(words, fwd_prev, [landed[step] for step in range(replicas)])
     return (output[None, None], grad_input[None, None])
 
 

time: 146 us -> 117 us (0.80)
  waiting for transfers between devices: 55.9 us -> 38.2 us
  local copies, waits for them, and re-layouts: 20.6 us -> 3.26 us
  other arithmetic: 3.65 us -> 7.12 us
  Pallas kernels: 38.3 us -> 40.4 us
    unnamed x23 -> x12, local copies, waits for them, and re-layouts: 19.4 us -> 2.16 us
    ppermute x9, waiting for transfers between devices: 36.2 us -> 21.6 us  [over_dp(): return lax.ppermute(value, 'dp', partner_pairs(lax.axis_size('dp'), step))]
    ppermute x5, waiting for transfers between devices: 10.9 us -> 7.94 us  [over_pipe(): lax.ppermute(value, 'pipe', shift_pairs(lax.axis_size('pipe'), steps))]
    ppermute x4, starting transfers between devices: 3.65 us -> 5.18 us  [window(): lax.ppermute(summed[index * rows:(index + 1) * rows], ('pipe', 'dp'), cro...]
    ppermute x4, waiting for transfers between devices: 7.14 us -> 8.64 us  [window(): lax.ppermute(summed[index * rows:(index + 1) * rows], ('pipe', 'dp'), cro...]
    pallas_call x7 -> x8, Pallas kernels: 38.3 us -> 39 us  [call(): pl.pallas_call(body, in_specs=[SCALAR if arg.dtype == jnp.int32 else LOCA...]
  transfers between devices with their start and end apart: 28 -> 29, of which waited for: 8 -> 8; matrix products, arithmetic and copies ran while one was open for 3% -> 4% of each run, Pallas kernels for 26% -> 35%
where the time goes in v1:
time: 117 us
  Pallas kernels  40.4 us (35%)
  waiting for transfers between devices  38.2 us (33%)
  starting transfers between devices  26.9 us (23%)
  other arithmetic  7.12 us (6%)
  local copies, waits for them, and re-layouts  3.26 us (3%)
    pallas_call x8, Pallas kernels, call(): pl.pallas_call(body, in_specs=[SCALAR if arg.dtype == jnp.int32 else LOCA...  39 us
    ppermute x9, waiting for transfers between devices, over_dp(): return lax.ppermute(value, 'dp', partner_pairs(lax.axis_size('dp'), step))  21.6 us
    ppermute x9, starting transfers between devices, over_dp(): return lax.ppermute(value, 'dp', partner_pairs(lax.axis_size('dp'), step))  12.3 us
    ppermute x4, waiting for transfers between devices, window(): lax.ppermute(summed[index * rows:(index + 1) * rows], ('pipe', 'dp'), cro...  8.64 us
    ppermute x5, waiting for transfers between devices, over_pipe(): lax.ppermute(value, 'pipe', shift_pairs(lax.axis_size('pipe'), steps))  7.94 us
    ppermute x5, starting transfers between devices, over_pipe(): lax.ppermute(value, 'pipe', shift_pairs(lax.axis_size('pipe'), steps))  7.04 us
    ppermute x4, starting transfers between devices, window(): lax.ppermute(summed[index * rows:(index + 1) * rows], ('pipe', 'dp'), cro...  5.18 us
  transfers between devices with their start and end apart: 29, of which 8 were waited for; matrix products, arithmetic and copies ran while one was open for 4% of the time, Pallas kernels for 35%

profile of v1, /device:TPU:0, one launch (start us, length us, event | category | flops | bytes accessed | tf_op | source)
XLA Modules:
  0.0 116.8 jit_solution(3761029694555380133)
XLA Ops:
  0.7 1.1 dynamic-slice_bitcast_fusion
  1.7 4.1 %collective-permute-start.9 = (bf16[48,1024]{1,0:T(8,128)(2,1)S(1)}, bf16[48,1024]{1,0:T(8,128)(2,1)S(1)}, u32[]{:S(2)}, u32[]{:S(2)}) collective-permute-start(bf16[48,1024]{1,0:T(8,128)(2,1)S(1)} %get-tuple-element.37), channel_id=1, source_target_pairs={{0,2},{1,3},{2,0},{3,1},{4,6},{5,7},{6,4},{7,5},{8,10},{9,11},{10,... | collective-permute-start | bytes 294920 | tf_op jit(solution)/shard_map/ppermute | solution.py:37
  5.9 1.3 %collective-permute-start.11 = (bf16[48,1024]{1,0:T(8,128)(2,1)S(1)}, bf16[48,1024]{1,0:T(8,128)(2,1)S(1)}, u32[]{:S(2)}, u32[]{:S(2)}) collective-permute-start(bf16[48,1024]{1,0:T(8,128)(2,1)S(1)} %get-tuple-element.36), channel_id=1, source_target_pairs={{0,3},{1,2},{2,1},{3,0},{4,7},{5,6},{6,5},{7,4},{8,11},{9,10},{10,... | collective-permute-start | bytes 294920 | tf_op jit(solution)/shard_map/ppermute | solution.py:37
  7.4 1.2 %fusion = f32[48]{0:T(128)S(1)} fusion(bf16[1,1,48,4096]{3,2,1,0:T(8,128)(2,1)} %param.7), kind=kLoop, calls=%fused_computation.7 | loop fusion | flops 589776 | bytes 393408 | tf_op jit(solution)/shard_map/reduce_sum | solution.py:62
  8.6 5.1 %collective-permute-done.9.refs_4_ = bf16[48,1024]{1,0:T(8,128)(2,1)S(1)} collective-permute-done((bf16[48,1024]{1,0:T(8,128)(2,1)S(1)}, bf16[48,1024]{1,0:T(8,128)(2,1)S(1)}, u32[]{:S(2)}, u32[]{:S(2)}) %collective-permute-start.9) | collective-permute-done | bytes 98336 | tf_op jit(solution)/shard_map/ppermute | solution.py:37
  14.3 1.2 %fusion.2.refs_1_ = bf16[48,4096]{1,0:T(8,128)(2,1)S(1)} fusion(f32[4096]{0:T(1024)} %bitcast.30, f32[48]{0:T(128)S(1)} %add_rsqrt_fusion.1, bf16[1,1,48,4096]{3,2,1,0:T(8,128)(2,1)} %param.7), kind=kLoop, calls=%fused_computation.9 | loop fusion | flops 786432 | bytes 803008 | tf_op jit(solution)/shard_map/convert_element_type | solution.py:63
  16.0 3.5 %collective-permute-start.4 = (bf16[48,4096]{1,0:T(8,128)(2,1)S(1)}, bf16[48,4096]{1,0:T(8,128)(2,1)S(1)}, u32[]{:S(2)}, u32[]{:S(2)}) collective-permute-start(bf16[48,4096]{1,0:T(8,128)(2,1)S(1)} %fusion.2.refs_1_), channel_id=1, source_target_pairs={{0,2},{1,3},{2,0},{3,1},{4,6},{5,7},{6,4},{7,5},{8,10},{9,11},{10,... | collective-permute-start | bytes 1179656 | tf_op jit(solution)/shard_map/ppermute | solution.py:37
  19.9 2.4 %collective-permute-start.21 = (bf16[48,4096]{1,0:T(8,128)(2,1)}, bf16[48,4096]{1,0:T(8,128)(2,1)}, u32[]{:S(2)}, u32[]{:S(2)}) collective-permute-start(bf16[48,4096]{1,0:T(8,128)(2,1)} %bitcast.34), channel_id=1, source_target_pairs={{0,24},{8,0},{16,8},{24,16},{1,25},{9,1},{17,9},{25,17},{2,26},{10... | collective-permute-start | bytes 1179656 | tf_op jit(solution)/shard_map/ppermute | solution.py:41
  22.4 4.3 %shard_map.89 = (bf16[96,2304]{1,0:T(8,128)(2,1)S(1)}, bf16[96,2304]{1,0:T(8,128)(2,1)S(1)}, bf16[96,2304]{1,0:T(8,128)(2,1)S(1)}, bf16[96,2304]{1,0:T(8,128)(2,1)S(1)}, bf16[3,768,1024]{2,1,0:T(8,128)(2,1)S(1)}) custom-call(bf16[48,1024]{1,0:T(8,128)(2,1)S(1)} %get-tuple-element.39.refs_0_, bf16[48,1024]{1,0:T(8,128)(2,1)S(1)} %collective-permute-done.6.refs_1_, ...), custom_call_target="tpu_custom_call" | custom-call | flops 1811939328 | bytes 4718592 | tf_op jit(solution)/shard_map/pallas_call | solution.py:194
  26.7 2.1 %copy-done = bf16[3,768,1024]{2,1,0:T(8,128)(2,1)} copy-done((bf16[3,768,1024]{2,1,0:T(8,128)(2,1)}, bf16[3,768,1024]{2,1,0:T(8,128)(2,1)S(1)}, u32[]{:S(2)}) %copy-start) | copy-done | bytes 4718616
  28.8 1.6 %collective-permute-start.23 = (bf16[96,2304]{1,0:T(8,128)(2,1)S(1)}, bf16[96,2304]{1,0:T(8,128)(2,1)}, u32[]{:S(2)}, u32[]{:S(2)}) collective-permute-start(bf16[96,2304]{1,0:T(8,128)(2,1)S(1)} %get-tuple-element.28), channel_id=1, source_target_pairs={{0,1},{1,0},{2,3},{3,2},{4,5},{5,4},{6,7},{7,6},{8,9},{9,8},{10,11... | collective-permute-start | bytes 1327112 | tf_op jit(solution)/shard_map/ppermute | solution.py:37
  30.7 10.0 %shard_map.86 = (bf16[96,2304]{1,0:T(8,128)(2,1)S(1)}, bf16[12,1024,1024]{2,1,0:T(8,128)(2,1)S(1)}) custom-call(s32[5]{0:T(128)S(1)} %pad_add_fusion.refs_0_.words_ref, bf16[48,4096]{1,0:T(8,128)(2,1)S(1)} %fusion.2.refs_1_, bf16[48,4096]{1,0:T(8,128)(2,1)S(1)} %collective-permute-done.1.refs_2_, bf16[4096,3072]{1,0:T(8,128)(2,1)} %bitcast.26), custom_call_target="tpu_custom_call" | custom-call | flops 2415919104 | bytes 25165824 | tf_op jit(solution)/shard_map/pallas_call | solution.py:194
  41.2 8.1 %collective-permute-done.23 = bf16[96,2304]{1,0:T(8,128)(2,1)} collective-permute-done((bf16[96,2304]{1,0:T(8,128)(2,1)S(1)}, bf16[96,2304]{1,0:T(8,128)(2,1)}, u32[]{:S(2)}, u32[]{:S(2)}) %collective-permute-start.23) | collective-permute-done | bytes 442400 | tf_op jit(solution)/shard_map/ppermute | solution.py:37
  49.2 1.1 add_convert_fusion
  50.5 5.8 %shard_map.88.refs_2_ = bf16[96,2304]{1,0:T(8,128)(2,1)S(1)} custom-call(s32[5]{0:T(128)S(1)} %pad_add_fusion.refs_0_.words_ref, bf16[48,4096]{1,0:T(8,128)(2,1)S(1)} %collective-permute-done.4.refs_1_, bf16[48,4096]{1,0:T(8,128)(2,1)S(1)} %collective-permute-done.5.refs_2_, bf16[12,1024,1024]{2,1,0:T(8,128)(2,1)S(1)} %get-tuple-element.19.refs_3_.refs_5_.refs_1_), custom_call_target="tpu_custom_call" | custom-call | flops 2415919104 | tf_op jit(solution)/shard_map/pallas_call | solution.py:194
  56.3 6.1 %shard_map.87.refs_1_ = bf16[96,2304]{1,0:T(8,128)(2,1)S(1)} custom-call(s32[5]{0:T(128)S(1)} %pad_add_fusion.refs_0_.words_ref, bf16[48,4096]{1,0:T(8,128)(2,1)S(1)} %collective-permute-done.2.refs_1_, bf16[48,4096]{1,0:T(8,128)(2,1)S(1)} %collective-permute-done.3.refs_2_, bf16[12,1024,1024]{2,1,0:T(8,128)(2,1)S(1)} %get-tuple-element.19.refs_3_.refs_5_.refs_1_), custom_call_target="tpu_custom_call" | custom-call | flops 2415919104 | tf_op jit(solution)/shard_map/pallas_call | solution.py:194
  62.5 1.5 %shard_map.90 = (bf16[144,1024]{1,0:T(8,128)(2,1)S(1)}, bf16[144,1024]{1,0:T(8,128)(2,1)S(1)}) custom-call(bf16[96,2304]{1,0:T(8,128)(2,1)S(1)} %get-tuple-element.18.refs_0_, bf16[96,2304]{1,0:T(8,128)(2,1)S(1)} %shard_map.87.refs_1_, bf16[96,2304]{1,0:T(8,128)(2,1)S(1)} %shard_map.88.refs_2_, bf16[3,768,1024]{2,1,0:T(8,128)(2,1)S(1)} %bitcast.24), custom_call_target="tpu_custom_call" | custom-call | flops 1358954496 | tf_op jit(solution)/shard_map/pallas_call | solution.py:194
  65.2 8.4 %collective-permute-done.24.refs_4_ = bf16[96,2304]{1,0:T(8,128)(2,1)S(1)} collective-permute-done((bf16[96,2304]{1,0:T(8,128)(2,1)S(1)}, bf16[96,2304]{1,0:T(8,128)(2,1)S(1)}, u32[]{:S(2)}, u32[]{:S(2)}) %collective-permute-start.24) | collective-permute-done | bytes 442400 | tf_op jit(solution)/shard_map/ppermute | solution.py:37
  73.5 6.4 %shard_map.92 = (bf16[96,3072]{1,0:T(8,128)(2,1)S(1)}, bf16[48,2048]{1,0:T(8,128)(2,1)S(1)}, bf16[48,2048]{1,0:T(8,128)(2,1)S(1)}) custom-call(s32[5]{0:T(128)S(1)} %pad_add_fusion.refs_0_.words_ref, bf16[96,3072]{1,0:T(8,128)(2,1)S(1)} %bitcast.25, bf16[96,2304]{1,0:T(8,128)(2,1)S(1)} %get-tuple-element.25.refs_2_, ...), custom_call_target="tpu_custom_call" | custom-call | flops 1207959552 | tf_op jit(solution)/shard_map/pallas_call | solution.py:194
  80.0 3.9 %shard_map.93 = (bf16[48,2048]{1,0:T(8,128)(2,1)S(1)}, bf16[48,2048]{1,0:T(8,128)(2,1)S(1)}) custom-call(bf16[96,3072]{1,0:T(8,128)(2,1)S(1)} %get-tuple-element.31.refs_0_, bf16[12,1024,1024]{2,1,0:T(8,128)(2,1)S(1)} %get-tuple-element.19.refs_3_.refs_5_.refs_1_), custom_call_target="tpu_custom_call" | custom-call | flops 1207959552 | tf_op jit(solution)/shard_map/pallas_call | solution.py:194
  84.7 1.5 %collective-permute-start.14 = (bf16[48,1024]{1,0:T(8,128)(2,1)S(1)}, bf16[48,1024]{1,0:T(8,128)(2,1)S(1)}, u32[]{:S(2)}, u32[]{:S(2)}) collective-permute-start(bf16[48,1024]{1,0:T(8,128)(2,1)S(1)} %get-tuple-element.42), channel_id=1, source_target_pairs={{0,8},{1,9},{2,10},{3,11},{8,16},{9,17},{10,18},{11,19},{16,24},{1... | collective-permute-start | bytes 294920 | tf_op jit(solution)/shard_map/ppermute | solution.py:435
  87.4 2.7 %collective-permute-start.16 = (bf16[48,1024]{1,0:T(8,128)(2,1)S(1)}, bf16[48,1024]{1,0:T(8,128)(2,1)S(1)}, u32[]{:S(2)}, u32[]{:S(2)}) collective-permute-start(bf16[48,1024]{1,0:T(8,128)(2,1)S(1)} %get-tuple-element.40), channel_id=1, source_target_pairs={{0,10},{1,11},{2,8},{3,9},{8,18},{9,19},{10,16},{11,17},{16,26},{1... | collective-permute-start | bytes 294920 | tf_op jit(solution)/shard_map/ppermute | solution.py:435
  90.3 1.6 %collective-permute-start.26 = (bf16[48,2048]{1,0:T(8,128)(2,1)S(1)}, bf16[48,2048]{1,0:T(8,128)(2,1)S(1)}, u32[]{:S(2)}, u32[]{:S(2)}) collective-permute-start(bf16[48,2048]{1,0:T(8,128)(2,1)S(1)} %multiply_convert_fusion.1), channel_id=1, source_target_pairs={{0,24},{8,0},{16,8},{24,16},{1,25},{9,1},{17,9},{25,17},{2,26},{10... | collective-permute-start | bytes 589832 | tf_op jit(solution)/shard_map/ppermute | solution.py:41
  91.9 1.4 %collective-permute-start.28 = (bf16[48,2048]{1,0:T(8,128)(2,1)S(1)}, bf16[48,2048]{1,0:T(8,128)(2,1)S(1)}, u32[]{:S(2)}, u32[]{:S(2)}) collective-permute-start(bf16[48,2048]{1,0:T(8,128)(2,1)S(1)} %multiply_convert_fusion), channel_id=1, source_target_pairs={{0,24},{8,0},{16,8},{24,16},{1,25},{9,1},{17,9},{25,17},{2,26},{10... | collective-permute-start | bytes 589832 | tf_op jit(solution)/shard_map/ppermute | solution.py:41
  93.4 2.4 %collective-permute-done.15.refs_1_ = bf16[48,1024]{1,0:T(8,128)(2,1)S(1)} collective-permute-done((bf16[48,1024]{1,0:T(8,128)(2,1)S(1)}, bf16[48,1024]{1,0:T(8,128)(2,1)S(1)}, u32[]{:S(2)}, u32[]{:S(2)}) %collective-permute-start.15) | collective-permute-done | bytes 98336 | tf_op jit(solution)/shard_map/ppermute | solution.py:435
  95.8 0.9 collective-permute-start.19
  96.7 1.4 %collective-permute-start.20 = (bf16[48,4096]{1,0:T(8,128)(2,1)S(1)}, bf16[48,4096]{1,0:T(8,128)(2,1)S(1)}, u32[]{:S(2)}, u32[]{:S(2)}) collective-permute-start(bf16[48,4096]{1,0:T(8,128)(2,1)S(1)} %bitcast.28), channel_id=1, source_target_pairs={{0,24},{8,0},{16,8},{24,16},{1,25},{9,1},{17,9},{25,17},{2,26},{10... | collective-permute-start | bytes 1179656 | tf_op jit(solution)/shard_map/ppermute | solution.py:41
  98.1 6.0 %collective-permute-done.19.refs_3_ = bf16[48,1024]{1,0:T(8,128)(2,1)S(1)} collective-permute-done((bf16[48,1024]{1,0:T(8,128)(2,1)S(1)}, bf16[48,1024]{1,0:T(8,128)(2,1)S(1)}, u32[]{:S(2)}, u32[]{:S(2)}) %collective-permute-start.19) | collective-permute-done | bytes 98336 | tf_op jit(solution)/shard_map/ppermute | solution.py:435
  104.1 1.4 %add_landed.1 = bf16[48,4096]{1,0:T(8,128)(2,1)} custom-call(s32[5]{0:T(128)S(1)} %pad_add_fusion.refs_0_.words_ref, bf16[48,4096]{1,0:T(8,128)(2,1)S(1)} %collective-permute-done.residual_ref, bf16[48,1024]{1,0:T(8,128)(2,1)S(1)} %collective-permute-done.14.refs_0_, bf16[48,1024]{1,0:T(8,128)(2,1)S(1)} %collective-permute-done.15.refs_1_, ...), custom_call_target="tpu_custom_call" | custom-call | tf_op jit(solution)/shard_map/add_landed/pallas_call | solution.py:359
  106.4 1.3 %fusion.6 = (f32[48]{0:T(128)S(1)}, f32[48]{0:T(128)S(1)}) fusion(bf16[48,4096]{1,0:T(8,128)(2,1)} %collective-permute-done.21, bf16[48,2048]{1,0:T(8,128)(2,1)S(1)} %collective-permute-done.28, bf16[48,2048]{1,0:T(8,128)(2,1)S(1)} %collective-permute-done.26), kind=kLoop, calls=%fused_computation.13 | loop fusion | flops 1769376 | bytes 786816 | tf_op jit(solution)/shard_map/reduce_sum | solution.py:68
  107.6 7.1 %collective-permute-done.20 = bf16[48,4096]{1,0:T(8,128)(2,1)S(1)} collective-permute-done((bf16[48,4096]{1,0:T(8,128)(2,1)S(1)}, bf16[48,4096]{1,0:T(8,128)(2,1)S(1)}, u32[]{:S(2)}, u32[]{:S(2)}) %collective-permute-start.20) | collective-permute-done | bytes 393248 | tf_op jit(solution)/shard_map/ppermute | solution.py:41
  114.7 2.1 %fusion.11 = bf16[1,1,48,4096]{3,2,1,0:T(8,128)(2,1)} fusion(bf16[48,4096]{1,0:T(8,128)(2,1)} %collective-permute-done.21, bf16[48,4096]{1,0:T(8,128)(2,1)S(1)} %collective-permute-done.20, f32[48]{0:T(128)S(1)} %get-tuple-element.46, f32[48]{0:T(128)S(1)} %get-tuple-element.45, bf16[48,2048]{1,0:T(8,128)(2,1)S(1)} %collective-permute-done.28, ...), kind=kLoop, calls=%fused_computation.19 | loop fusion | flops 2752512 | bytes 1573248 | tf_op jit(solution)/shard_map/broadcast_in_dim | solution.py:441
  (64 shorter events, 6.8 us)
Async XLA Ops:
  1.7 12.0 %collective-permute-start.9 = (bf16[48,1024]{1,0:T(8,128)(2,1)S(1)}, bf16[48,1024]{1,0:T(8,128)(2,1)S(1)}, u32[]{:S(2)}, u32[]{:S(2)}) collective-permute-start(bf16[48,1024]{1,0:T(8,128)(2,1)S(1)} %get-tuple-element.37), channel_id=1, source_target_pairs={{0,2},{1,3},{2,0},{3,1},{4,6},{5,7},{6,4},{7,5},{8,10},{9,11},{10,... | collective-permute-start | bytes 294920 | tf_op jit(solution)/shard_map/ppermute | solution.py:37
  5.9 7.9 %collective-permute-start.11 = (bf16[48,1024]{1,0:T(8,128)(2,1)S(1)}, bf16[48,1024]{1,0:T(8,128)(2,1)S(1)}, u32[]{:S(2)}, u32[]{:S(2)}) collective-permute-start(bf16[48,1024]{1,0:T(8,128)(2,1)S(1)} %get-tuple-element.36), channel_id=1, source_target_pairs={{0,3},{1,2},{2,1},{3,0},{4,7},{5,6},{6,5},{7,4},{8,11},{9,10},{10,... | collective-permute-start | bytes 294920 | tf_op jit(solution)/shard_map/ppermute | solution.py:37
  7.2 7.1 %collective-permute-start.7 = (bf16[48,1024]{1,0:T(8,128)(2,1)S(1)}, bf16[48,1024]{1,0:T(8,128)(2,1)S(1)}, u32[]{:S(2)}, u32[]{:S(2)}) collective-permute-start(bf16[48,1024]{1,0:T(8,128)(2,1)S(1)} %get-tuple-element.38), channel_id=1, source_target_pairs={{0,1},{1,0},{2,3},{3,2},{4,5},{5,4},{6,7},{7,6},{8,9},{9,8},{10,11... | collective-permute-start | bytes 294920 | tf_op jit(solution)/shard_map/ppermute | solution.py:37
  7.4 8.6 %collective-permute-start.6 = (bf16[48,1024]{1,0:T(8,128)(2,1)S(1)}, bf16[48,1024]{1,0:T(8,128)(2,1)S(1)}, u32[]{:S(2)}, u32[]{:S(2)}) collective-permute-start(bf16[48,1024]{1,0:T(8,128)(2,1)S(1)} %get-tuple-element.39.refs_0_), channel_id=1, source_target_pairs={{0,4},{4,0},{1,5},{5,1},{2,6},{6,2},{3,7},{7,3},{8,12},{12,8},{9,1... | collective-permute-start | bytes 294920 | tf_op jit(solution)/shard_map/ppermute | solution.py:47
  13.8 5.7 %collective-permute-start.10 = (bf16[48,1024]{1,0:T(8,128)(2,1)S(1)}, bf16[48,1024]{1,0:T(8,128)(2,1)S(1)}, u32[]{:S(2)}, u32[]{:S(2)}) collective-permute-start(bf16[48,1024]{1,0:T(8,128)(2,1)S(1)} %collective-permute-done.9.refs_4_), channel_id=1, source_target_pairs={{0,4},{4,0},{1,5},{5,1},{2,6},{6,2},{3,7},{7,3},{8,12},{12,8},{9,1... | collective-permute-start | bytes 294920 | tf_op jit(solution)/shard_map/ppermute | solution.py:47
  13.8 6.2 %collective-permute-start.12 = (bf16[48,1024]{1,0:T(8,128)(2,1)S(1)}, bf16[48,1024]{1,0:T(8,128)(2,1)S(1)}, u32[]{:S(2)}, u32[]{:S(2)}) collective-permute-start(bf16[48,1024]{1,0:T(8,128)(2,1)S(1)} %collective-permute-done.11.refs_6_), channel_id=1, source_target_pairs={{0,4},{4,0},{1,5},{5,1},{2,6},{6,2},{3,7},{7,3},{8,12},{12,8},{9,1... | collective-permute-start | bytes 294920 | tf_op jit(solution)/shard_map/ppermute | solution.py:47
  14.3 8.1 %collective-permute-start.8 = (bf16[48,1024]{1,0:T(8,128)(2,1)S(1)}, bf16[48,1024]{1,0:T(8,128)(2,1)S(1)}, u32[]{:S(2)}, u32[]{:S(2)}) collective-permute-start(bf16[48,1024]{1,0:T(8,128)(2,1)S(1)} %collective-permute-done.7.refs_2_), channel_id=1, source_target_pairs={{0,4},{4,0},{1,5},{5,1},{2,6},{6,2},{3,7},{7,3},{8,12},{12,8},{9,1... | collective-permute-start | bytes 294920 | tf_op jit(solution)/shard_map/ppermute | solution.py:47
  15.5 15.0 %collective-permute-start.1 = (bf16[48,4096]{1,0:T(8,128)(2,1)S(1)}, bf16[48,4096]{1,0:T(8,128)(2,1)S(1)}, u32[]{:S(2)}, u32[]{:S(2)}) collective-permute-start(bf16[48,4096]{1,0:T(8,128)(2,1)S(1)} %fusion.2.refs_1_), channel_id=1, source_target_pairs={{0,4},{4,0},{1,5},{5,1},{2,6},{6,2},{3,7},{7,3},{8,12},{12,8},{9,1... | collective-permute-start | bytes 1179656 | tf_op jit(solution)/shard_map/ppermute | solution.py:47
  16.0 24.6 %collective-permute-start.4 = (bf16[48,4096]{1,0:T(8,128)(2,1)S(1)}, bf16[48,4096]{1,0:T(8,128)(2,1)S(1)}, u32[]{:S(2)}, u32[]{:S(2)}) collective-permute-start(bf16[48,4096]{1,0:T(8,128)(2,1)S(1)} %fusion.2.refs_1_), channel_id=1, source_target_pairs={{0,2},{1,3},{2,0},{3,1},{4,6},{5,7},{6,4},{7,5},{8,10},{9,11},{10,... | collective-permute-start | bytes 1179656 | tf_op jit(solution)/shard_map/ppermute | solution.py:37
  19.5 21.7 %collective-permute-start.2 = (bf16[48,4096]{1,0:T(8,128)(2,1)S(1)}, bf16[48,4096]{1,0:T(8,128)(2,1)S(1)}, u32[]{:S(2)}, u32[]{:S(2)}) collective-permute-start(bf16[48,4096]{1,0:T(8,128)(2,1)S(1)} %fusion.2.refs_1_), channel_id=1, source_target_pairs={{0,1},{1,0},{2,3},{3,2},{4,5},{5,4},{6,7},{7,6},{8,9},{9,8},{10,11... | collective-permute-start | bytes 1179656 | tf_op jit(solution)/shard_map/ppermute | solution.py:37
  19.9 85.6 %collective-permute-start.21 = (bf16[48,4096]{1,0:T(8,128)(2,1)}, bf16[48,4096]{1,0:T(8,128)(2,1)}, u32[]{:S(2)}, u32[]{:S(2)}) collective-permute-start(bf16[48,4096]{1,0:T(8,128)(2,1)} %bitcast.34), channel_id=1, source_target_pairs={{0,24},{8,0},{16,8},{24,16},{1,25},{9,1},{17,9},{25,17},{2,26},{10... | collective-permute-start | bytes 1179656 | tf_op jit(solution)/shard_map/ppermute | solution.py:41
  28.8 20.4 %collective-permute-start.23 = (bf16[96,2304]{1,0:T(8,128)(2,1)S(1)}, bf16[96,2304]{1,0:T(8,128)(2,1)}, u32[]{:S(2)}, u32[]{:S(2)}) collective-permute-start(bf16[96,2304]{1,0:T(8,128)(2,1)S(1)} %get-tuple-element.28), channel_id=1, source_target_pairs={{0,1},{1,0},{2,3},{3,2},{4,5},{5,4},{6,7},{7,6},{8,9},{9,8},{10,11... | collective-permute-start | bytes 1327112 | tf_op jit(solution)/shard_map/ppermute | solution.py:37
  30.5 56.9 %collective-permute-start = (bf16[48,4096]{1,0:T(8,128)(2,1)}, bf16[48,4096]{1,0:T(8,128)(2,1)S(1)}, u32[]{:S(2)}, u32[]{:S(2)}) collective-permute-start(bf16[48,4096]{1,0:T(8,128)(2,1)} %bitcast.27), channel_id=1, source_target_pairs={{0,8},{8,16},{16,24},{24,0},{1,9},{9,17},{17,25},{25,1},{2,10},{10... | collective-permute-start | bytes 1179656 | tf_op jit(solution)/shard_map/ppermute | solution.py:41
  40.7 23.9 %collective-permute-start.22 = (bf16[96,2304]{1,0:T(8,128)(2,1)S(1)}, bf16[96,2304]{1,0:T(8,128)(2,1)S(1)}, u32[]{:S(2)}, u32[]{:S(2)}) collective-permute-start(bf16[96,2304]{1,0:T(8,128)(2,1)S(1)} %get-tuple-element.26), channel_id=1, source_target_pairs={{0,1},{1,0},{2,3},{3,2},{4,5},{5,4},{6,7},{7,6},{8,9},{9,8},{10,11... | collective-permute-start | bytes 1327112 | tf_op jit(solution)/shard_map/ppermute | solution.py:37
  41.2 9.2 %collective-permute-start.5 = (bf16[48,4096]{1,0:T(8,128)(2,1)S(1)}, bf16[48,4096]{1,0:T(8,128)(2,1)S(1)}, u32[]{:S(2)}, u32[]{:S(2)}) collective-permute-start(bf16[48,4096]{1,0:T(8,128)(2,1)S(1)} %collective-permute-done.4.refs_1_), channel_id=1, source_target_pairs={{0,4},{4,0},{1,5},{5,1},{2,6},{6,2},{3,7},{7,3},{8,12},{12,8},{9,1... | collective-permute-start | bytes 1179656 | tf_op jit(solution)/shard_map/ppermute | solution.py:47
  49.2 7.1 %collective-permute-start.3 = (bf16[48,4096]{1,0:T(8,128)(2,1)S(1)}, bf16[48,4096]{1,0:T(8,128)(2,1)S(1)}, u32[]{:S(2)}, u32[]{:S(2)}) collective-permute-start(bf16[48,4096]{1,0:T(8,128)(2,1)S(1)} %collective-permute-done.2.refs_1_), channel_id=1, source_target_pairs={{0,4},{4,0},{1,5},{5,1},{2,6},{6,2},{3,7},{7,3},{8,12},{12,8},{9,1... | collective-permute-start | bytes 1179656 | tf_op jit(solution)/shard_map/ppermute | solution.py:47
  50.4 23.2 %collective-permute-start.24 = (bf16[96,2304]{1,0:T(8,128)(2,1)S(1)}, bf16[96,2304]{1,0:T(8,128)(2,1)S(1)}, u32[]{:S(2)}, u32[]{:S(2)}) collective-permute-start(bf16[96,2304]{1,0:T(8,128)(2,1)S(1)} %add_convert_fusion), channel_id=1, source_target_pairs={{0,2},{1,3},{2,0},{3,1},{4,6},{5,7},{6,4},{7,5},{8,10},{9,11},{10,... | collective-permute-start | bytes 1327112 | tf_op jit(solution)/shard_map/ppermute | solution.py:37
  50.5 14.1 %copy-start.3 = (f32[1,4096]{1,0:T(1,128)S(1)}, f32[1,4096]{1,0:T(1,128)}, u32[]{:S(2)}) copy-start(f32[1,4096]{1,0:T(1,128)} %param.11) | copy-start | bytes 49156
  50.5 23.1 %copy-start.1 = (bf16[1,1,96,3072]{3,2,1,0:T(8,128)(2,1)S(1)}, bf16[1,1,96,3072]{3,2,1,0:T(8,128)(2,1)}, u32[]{:S(2)}) copy-start(bf16[1,1,96,3072]{3,2,1,0:T(8,128)(2,1)} %param.10) | copy-start | bytes 1769476
  64.0 20.0 %collective-permute-start.13 = (bf16[144,1024]{1,0:T(8,128)(2,1)S(1)}, bf16[144,1024]{1,0:T(8,128)(2,1)S(1)}, u32[]{:S(2)}, u32[]{:S(2)}) collective-permute-start(bf16[144,1024]{1,0:T(8,128)(2,1)S(1)} %get-tuple-element.22), channel_id=1, source_target_pairs={{0,4},{4,0},{1,5},{5,1},{2,6},{6,2},{3,7},{7,3},{8,12},{12,8},{9,1... | collective-permute-start | bytes 884744 | tf_op jit(solution)/shard_map/ppermute | solution.py:55
  64.6 20.1 %collective-permute-start.17 = (bf16[96,2304]{1,0:T(8,128)(2,1)S(1)}, bf16[96,2304]{1,0:T(8,128)(2,1)S(1)}, u32[]{:S(2)}, u32[]{:S(2)}) collective-permute-start(bf16[96,2304]{1,0:T(8,128)(2,1)S(1)} %shard_map.88.refs_2_), channel_id=1, source_target_pairs={{0,1},{1,0},{2,3},{3,2},{4,5},{5,4},{6,7},{7,6},{8,9},{9,8},{10,11... | collective-permute-start | bytes 1327112 | tf_op jit(solution)/shard_map/ppermute | solution.py:37
  73.5 23.2 %copy-start.2 = (bf16[1,1,48,4096]{3,2,1,0:T(8,128)(2,1)S(1)}, bf16[1,1,48,4096]{3,2,1,0:T(8,128)(2,1)}, u32[]{:S(2)}) copy-start(bf16[1,1,48,4096]{3,2,1,0:T(8,128)(2,1)} %param.9) | copy-start | bytes 1179652
  80.0 7.1 %collective-permute-start.25 = (bf16[48,2048]{1,0:T(8,128)(2,1)S(1)}, bf16[48,2048]{1,0:T(8,128)(2,1)S(1)}, u32[]{:S(2)}, u32[]{:S(2)}) collective-permute-start(bf16[48,2048]{1,0:T(8,128)(2,1)S(1)} %get-tuple-element.30), channel_id=1, source_target_pairs={{0,4},{4,0},{1,5},{5,1},{2,6},{6,2},{3,7},{7,3},{8,12},{12,8},{9,1... | collective-permute-start | bytes 589832 | tf_op jit(solution)/shard_map/ppermute | solution.py:55
  84.0 3.3 %collective-permute-start.27 = (bf16[48,2048]{1,0:T(8,128)(2,1)S(1)}, bf16[48,2048]{1,0:T(8,128)(2,1)S(1)}, u32[]{:S(2)}, u32[]{:S(2)}) collective-permute-start(bf16[48,2048]{1,0:T(8,128)(2,1)S(1)} %get-tuple-element.33), channel_id=1, source_target_pairs={{0,4},{4,0},{1,5},{5,1},{2,6},{6,2},{3,7},{7,3},{8,12},{12,8},{9,1... | collective-permute-start | bytes 589832 | tf_op jit(solution)/shard_map/ppermute | solution.py:55
  84.7 5.7 %collective-permute-start.14 = (bf16[48,1024]{1,0:T(8,128)(2,1)S(1)}, bf16[48,1024]{1,0:T(8,128)(2,1)S(1)}, u32[]{:S(2)}, u32[]{:S(2)}) collective-permute-start(bf16[48,1024]{1,0:T(8,128)(2,1)S(1)} %get-tuple-element.42), channel_id=1, source_target_pairs={{0,8},{1,9},{2,10},{3,11},{8,16},{9,17},{10,18},{11,19},{16,24},{1... | collective-permute-start | bytes 294920 | tf_op jit(solution)/shard_map/ppermute | solution.py:435
  87.1 8.7 %collective-permute-start.15 = (bf16[48,1024]{1,0:T(8,128)(2,1)S(1)}, bf16[48,1024]{1,0:T(8,128)(2,1)S(1)}, u32[]{:S(2)}, u32[]{:S(2)}) collective-permute-start(bf16[48,1024]{1,0:T(8,128)(2,1)S(1)} %get-tuple-element.41), channel_id=1, source_target_pairs={{0,9},{1,8},{2,11},{3,10},{8,17},{9,16},{10,19},{11,18},{16,25},{1... | collective-permute-start | bytes 294920 | tf_op jit(solution)/shard_map/ppermute | solution.py:435
  87.3 4.6 %collective-permute-start.18 = (bf16[48,1024]{1,0:T(8,128)(2,1)S(1)}, bf16[48,1024]{1,0:T(8,128)(2,1)S(1)}, u32[]{:S(2)}, u32[]{:S(2)}) collective-permute-start(bf16[48,1024]{1,0:T(8,128)(2,1)S(1)} %get-tuple-element.24), channel_id=1, source_target_pairs={{0,4},{4,0},{1,5},{5,1},{2,6},{6,2},{3,7},{7,3},{8,12},{12,8},{9,1... | collective-permute-start | bytes 294920 | tf_op jit(solution)/shard_map/ppermute | solution.py:55
  87.4 9.3 %collective-permute-start.16 = (bf16[48,1024]{1,0:T(8,128)(2,1)S(1)}, bf16[48,1024]{1,0:T(8,128)(2,1)S(1)}, u32[]{:S(2)}, u32[]{:S(2)}) collective-permute-start(bf16[48,1024]{1,0:T(8,128)(2,1)S(1)} %get-tuple-element.40), channel_id=1, source_target_pairs={{0,10},{1,11},{2,8},{3,9},{8,18},{9,19},{10,16},{11,17},{16,26},{1... | collective-permute-start | bytes 294920 | tf_op jit(solution)/shard_map/ppermute | solution.py:435
  90.3 15.2 %collective-permute-start.26 = (bf16[48,2048]{1,0:T(8,128)(2,1)S(1)}, bf16[48,2048]{1,0:T(8,128)(2,1)S(1)}, u32[]{:S(2)}, u32[]{:S(2)}) collective-permute-start(bf16[48,2048]{1,0:T(8,128)(2,1)S(1)} %multiply_convert_fusion.1), channel_id=1, source_target_pairs={{0,24},{8,0},{16,8},{24,16},{1,25},{9,1},{17,9},{25,17},{2,26},{10... | collective-permute-start | bytes 589832 | tf_op jit(solution)/shard_map/ppermute | solution.py:41
  91.9 14.5 %collective-permute-start.28 = (bf16[48,2048]{1,0:T(8,128)(2,1)S(1)}, bf16[48,2048]{1,0:T(8,128)(2,1)S(1)}, u32[]{:S(2)}, u32[]{:S(2)}) collective-permute-start(bf16[48,2048]{1,0:T(8,128)(2,1)S(1)} %multiply_convert_fusion), channel_id=1, source_target_pairs={{0,24},{8,0},{16,8},{24,16},{1,25},{9,1},{17,9},{25,17},{2,26},{10... | collective-permute-start | bytes 589832 | tf_op jit(solution)/shard_map/ppermute | solution.py:41
  95.8 8.3 %collective-permute-start.19 = (bf16[48,1024]{1,0:T(8,128)(2,1)S(1)}, bf16[48,1024]{1,0:T(8,128)(2,1)S(1)}, u32[]{:S(2)}, u32[]{:S(2)}) collective-permute-start(bf16[48,1024]{1,0:T(8,128)(2,1)S(1)} %add_convert_fusion.2), channel_id=1, source_target_pairs={{0,11},{1,10},{2,9},{3,8},{8,19},{9,18},{10,17},{11,16},{16,27},{1... | collective-permute-start | bytes 294920 | tf_op jit(solution)/shard_map/ppermute | solution.py:435
  96.7 18.0 %collective-permute-start.20 = (bf16[48,4096]{1,0:T(8,128)(2,1)S(1)}, bf16[48,4096]{1,0:T(8,128)(2,1)S(1)}, u32[]{:S(2)}, u32[]{:S(2)}) collective-permute-start(bf16[48,4096]{1,0:T(8,128)(2,1)S(1)} %bitcast.28), channel_id=1, source_target_pairs={{0,24},{8,0},{16,8},{24,16},{1,25},{9,1},{17,9},{25,17},{2,26},{10... | collective-permute-start | bytes 1179656 | tf_op jit(solution)/shard_map/ppermute | solution.py:41
  (3 other events, 20.3 us)

commit v2 on v1

--- a/solution.py
+++ b/solution.py
@@ -155,30 +155,37 @@
 REMOTE = pl.BlockSpec(memory_space=pltpu.HBM)
 
 
-def call(kernel, args, weight, outs, blocks, keep, flops):
+def call(kernel, args, weight, helds, outs, blocks, keep, flops):
     count = len(args)
-    moved = 0
-    if blocks:
-        shape = (len(blocks), blocks[0][0].size, blocks[0][1].size)
-        moved = 2 * math.prod(shape)
+    extra = 1 if blocks else len(helds)
+    shape = (len(blocks), blocks[0][0].size, blocks[0][1].size) if blocks else ()
+    moved = 2 * math.prod(shape) if blocks else 0
 
     def body(*refs):
-        ins, weight_ref = refs[:count], refs[count]
-        results = refs[count + 1 : count + 1 + len(outs)]
+        ins, weight_refs = refs[:count], refs[count : count + extra]
+        results = refs[count + extra : count + extra + len(outs)]
         if not blocks:
-            kernel(ins, results, weight_ref, lambda index: None)
+            places = [ref.at[index] for ref in weight_refs for index in range(ref.shape[0])]
+            kernel(ins, results, lambda index: places[index][...])
             return
-        held, sems = refs[count + 1 + len(outs) :]
+        held, sems = refs[count + extra + len(outs) :]
         moves = [
-            pltpu.make_async_copy(weight_ref.at[part], held.at[index], sems.at[index])
+            pltpu.make_async_copy(weight_refs[0].at[part], held.at[index], sems.at[index])
             for index, part in enumerate(blocks)
         ]
         for move in moves:
             move.start()
-        kernel(ins, results, held, lambda index: moves[index].wait())
+
+        def loaded(index):
+            moves[index].wait()
+            return held[index]
+
+        kernel(ins, results, loaded)
 
     out_specs = [LOCAL for _ in outs]
-    out_shape = [jax.ShapeDtypeStruct(out, jnp.bfloat16) for out in outs]
+    out_shape = [
+        out if hasattr(out, "dtype") else jax.ShapeDtypeStruct(out, jnp.bfloat16) for out in outs
+    ]
     scratch = []
     if blocks:
         scratch = [pltpu.SemaphoreType.DMA((len(blocks),))]
@@ -187,20 +194,20 @@
             out_shape.append(pltpu.VMEM(shape, jnp.bfloat16))
         else:
             scratch.insert(0, pltpu.VMEM(shape, jnp.bfloat16))
-        weight = pltpu.with_memory_space_constraint(weight, pltpu.HBM)
+        weights = [pltpu.with_memory_space_constraint(weight, pltpu.HBM)]
     else:
-        weight = pltpu.with_memory_space_constraint(weight, pltpu.VMEM)
+        weights = [pltpu.with_memory_space_constraint(held, pltpu.VMEM) for held in helds]
     limit = (0 if keep else moved) + (8 << 20)
     return pl.pallas_call(
         body,
         in_specs=[SCALAR if arg.dtype == jnp.int32 else LOCAL for arg in args]
-        + [REMOTE if blocks else LOCAL],
+        + [REMOTE if blocks else LOCAL for _ in weights],
         out_specs=out_specs,
         out_shape=out_shape,
         scratch_shapes=scratch,
         compiler_params=pltpu.CompilerParams(vmem_limit_bytes=limit),
         cost_estimate=pl.CostEstimate(flops=flops, bytes_accessed=moved, transcendentals=0),
-    )(*args, weight)
+    )(*args, *weights)
 
 
 def row_blocks(size, columns, most):
@@ -208,72 +215,84 @@
     return [(pl.ds(row, block), pl.ds(0, columns)) for row in range(0, size, block)]
 
 
-def forward_heads(parts, weight, held, start):
-    rows, width = parts[0].shape
-    length = rows * len(parts)
-    units = weight.shape[1] // UNIT
+def forward_heads(batches, weight, helds, start):
+    rows, width = batches[0][0].shape
+    length = rows * len(batches[0])
+    flat = [part for parts in batches for part in parts]
     depth = divisor(width, 1024)
     steps = width // depth
-
-    def kernel(ins, outs, blocks, wait):
+    units = sum(held.shape[0] for held in helds) // steps if helds else weight.shape[1] // UNIT
+
+    def kernel(ins, outs, block):
         masked = later_keys(length, ins[0][0])
         for unit in range(units):
             total = None
             for step in range(steps):
                 at = slice(step * depth, (step + 1) * depth)
                 left = jnp.concatenate([ref[:, at] for ref in ins[1:]], axis=0)
-                wait(unit * steps + step)
-                product = mxu(left, blocks[unit * steps + step], 1, 0)
+                product = mxu(left, block(unit * steps + step), 1, 0)
                 total = product if total is None else total + product
-            attend_unit(total.astype(jnp.bfloat16), masked, outs[0], unit * GROUP * HD)
-
-    blocks = [
-        (pl.ds(step * depth, depth), pl.ds(unit * UNIT, UNIT))
-        for unit in range(units)
-        for step in range(steps)
-    ]
-    flops = 2 * length * width * units * UNIT
-    outs = [(length, units * GROUP * HD)]
-    if held is None:
-        return call(kernel, [start] + parts, weight, outs, blocks, True, flops)
-    return call(kernel, [start] + parts, held, outs, [], False, flops)[0]
-
-
-def head_terms(pieces, weight):
+            total = total.astype(jnp.bfloat16)
+            for index, out_ref in enumerate(outs):
+                qkv = total[index * length : (index + 1) * length]
+                attend_unit(qkv, masked, out_ref, unit * GROUP * HD)
+
+    blocks = []
+    if not helds:
+        blocks = [
+            (pl.ds(step * depth, depth), pl.ds(unit * UNIT, UNIT))
+            for unit in range(units)
+            for step in range(steps)
+        ]
+    flops = 2 * length * len(batches) * width * units * UNIT
+    outs = [(length, units * GROUP * HD) for _ in batches]
+    return call(kernel, [start] + flat, weight, helds, outs, blocks, not helds, flops)
+
+
+def column_parts(depth):
+    first = GROUP * HD
+    return [(0, first), (first, depth)] if depth > first else [(0, depth)]
+
+
+def head_terms(pieces, weight, whole):
     rows, columns = pieces[0][0].shape
     length = rows * len(pieces[0])
     depth = weight.shape[0]
     flat = [part for parts in pieces for part in parts]
     blocks = row_blocks(depth, columns, 768)
     block = depth // len(blocks)
-
-    def kernel(ins, outs, held, wait):
+    places = [(k, 0, depth) for k in range(whole)]
+    for first, last in column_parts(depth):
+        places += [(k, first, last) for k in range(whole, len(pieces))]
+
+    def kernel(ins, outs, loaded):
         left = jnp.concatenate([ref[...] for ref in ins], axis=0)
         for step in range(len(blocks)):
-            wait(step)
-            product = mxu(left, held[step], 1, 1).astype(jnp.bfloat16)
-            for index, out_ref in enumerate(outs):
-                out_ref[:, step * block : (step + 1) * block] = product[
-                    index * length : (index + 1) * length
-                ]
-
-    outs = [(length, depth) for _ in pieces]
+            product = mxu(left, loaded(step), 1, 1).astype(jnp.bfloat16)
+            at = step * block
+            for (k, first, last), out_ref in zip(places, outs):
+                if first <= at < last:
+                    out_ref[:, at - first : at - first + block] = product[
+                        k * length : (k + 1) * length
+                    ]
+
+    outs = [(length, last - first) for _, first, last in places]
     flops = 2 * len(pieces) * length * depth * columns
-    *terms, held = call(kernel, flat, weight, outs, blocks, True, flops)
+    *terms, held = call(kernel, flat, weight, [], outs, blocks, True, flops)
     return terms, held
 
 
 def project(heads, held, cores):
-    length, depth = heads[0].shape
+    length = heads[0].shape[0]
     count, (steps, block, columns) = len(heads), held.shape
     rows = length // cores
 
-    def kernel(ins, outs, blocks, wait):
+    def kernel(ins, outs, held_block):
         total = None
         for step in range(steps):
             at = slice(step * block, (step + 1) * block)
             left = jnp.concatenate([ref[:, at] for ref in ins], axis=0)
-            product = mxu(left, blocks[step], 1, 0)
+            product = mxu(left, held_block(step), 1, 0)
             total = product if total is None else total + product
         total = total.astype(jnp.bfloat16)
         for core, out_ref in enumerate(outs):
@@ -282,20 +301,71 @@
                 out_ref[index * rows : (index + 1) * rows] = total[at : at + rows]
 
     outs = [(count * rows, columns) for _ in range(cores)]
-    flops = 2 * count * length * depth * columns
-    return call(kernel, heads, held, outs, [], False, flops)
-
-
-def back_columns(grad_ref, outs, held, picked, steps):
-    depth = held.shape[1]
-    units = held.shape[0] // steps
+    flops = 2 * count * length * steps * block * columns
+    return call(kernel, heads, None, [held], outs, [], False, flops)
+
+
+def rolled_rows(ref, start, cores):
+    length = ref.shape[0]
+    rows = length // cores
+    ranges = []
+    for core in range(cores):
+        at = start + core * rows
+        at = jnp.where(at >= length, at - length, at)
+        ranges.append(pl.ds(pl.multiple_of(at, rows), rows))
+    return lambda columns: jnp.concatenate([ref[part, columns] for part in ranges], axis=0)
+
+
+def back_units(start_ref, qkv_ref, own_ref, landed, grad_ref, units, cores):
+    masked = later_keys(qkv_ref.shape[0], start_ref[0])
+    saved = rolled_rows(qkv_ref, start_ref[0], cores)
+    wide = GROUP * HD
+    for place, unit in enumerate(units):
+        grads = own_ref[:, unit * wide : (unit + 1) * wide].astype(jnp.float32)
+        for ref in landed:
+            grads = grads + ref[:, place * wide : (place + 1) * wide].astype(jnp.float32)
+        attend_back_unit(
+            saved(slice(unit * UNIT, (unit + 1) * UNIT)),
+            grads.astype(jnp.bfloat16),
+            masked,
+            grad_ref,
+            place * UNIT,
+        )
+
+
+def back_product(grad_ref, block, units, step, steps):
+    total = None
+    for place, unit in enumerate(units):
+        grads = grad_ref[:, place * UNIT : (place + 1) * UNIT]
+        product = mxu(grads, block(unit * steps + step), 1, 1)
+        total = product if total is None else total + product
+    return total
+
+
+def back_early(qkv, own, landed, helds, start, cores, units, steps):
+    length = qkv.shape[0]
+    depth = helds[0].shape[1]
+
+    def kernel(ins, outs, block):
+        back_units(ins[0], ins[1], ins[2], ins[3:], outs[0], units, cores)
+        for step in range(steps):
+            outs[1][:, step * depth : (step + 1) * depth] = back_product(
+                outs[0], block, units, step, steps
+            )
+
+    wide = len(units) * UNIT
+    outs = [(length, wide), jax.ShapeDtypeStruct((length, steps * depth), jnp.float32)]
+    flops = 2 * length * wide * steps * depth
+    args = [start, qkv, own] + landed
+    return call(kernel, args, None, helds, outs, [], False, flops)[1]
+
+
+def back_columns(grad_ref, early, outs, block, units, picked, steps, depth):
     rows = grad_ref.shape[0] // len(outs)
     for place, step in enumerate(picked):
-        total = None
-        for unit in range(units):
-            grads = grad_ref[:, unit * UNIT : (unit + 1) * UNIT]
-            product = mxu(grads, held[unit * steps + step], 1, 1)
-            total = product if total is None else total + product
+        total = back_product(grad_ref, block, units, step, steps)
+        for ref in early:
+            total = total + ref[:, step * depth : (step + 1) * depth]
         total = total.astype(jnp.bfloat16)
         for core, out_ref in enumerate(outs):
             out_ref[:, place * depth : (place + 1) * depth] = total[
@@ -303,47 +373,36 @@
             ]
 
 
-def back_first(qkv, terms, held, start, cores, picked, steps):
-    length, merged = qkv.shape
+def back_first(qkv, own, landed, early, helds, start, cores, units, picked, steps):
+    length = qkv.shape[0]
     rows = length // cores
-
-    def kernel(ins, outs, blocks, wait):
-        start = ins[0][0]
-        masked = later_keys(length, start)
-        ranges = []
-        for core in range(cores):
-            at = start + core * rows
-            at = jnp.where(at >= length, at - length, at)
-            ranges.append(pl.ds(pl.multiple_of(at, rows), rows))
-        rolled = jnp.concatenate([ins[1][part] for part in ranges], axis=0)
-        for unit in range(merged // UNIT):
-            at = unit * UNIT
-            part = slice(unit * GROUP * HD, (unit + 1) * GROUP * HD)
-            grads = ins[2][:, part].astype(jnp.float32)
-            for ref in ins[3:]:
-                grads = grads + ref[:, part].astype(jnp.float32)
-            attend_back_unit(
-                rolled[:, at : at + UNIT], grads.astype(jnp.bfloat16), masked, outs[0], at
-            )
-        back_columns(outs[0], outs[1:], blocks, picked, steps)
-
-    columns = len(picked) * held.shape[1]
-    outs = [qkv.shape] + [(rows, columns) for _ in range(cores)]
-    flops = 2 * length * merged * columns
-    results = call(kernel, [start, qkv] + terms, held, outs, [], False, flops)
+    depth = helds[0].shape[1]
+    count = 3 + len(landed)
+
+    def kernel(ins, outs, block):
+        back_units(ins[0], ins[1], ins[2], ins[3:count], outs[0], units, cores)
+        back_columns(outs[0], ins[count:], outs[1:], block, units, picked, steps, depth)
+
+    wide = len(units) * UNIT
+    columns = len(picked) * depth
+    outs = [(length, wide)] + [(rows, columns) for _ in range(cores)]
+    flops = 2 * length * wide * columns
+    args = [start, qkv, own] + landed + early
+    results = call(kernel, args, None, helds, outs, [], False, flops)
     return results[0], results[1:]
 
 
-def back_rest(grad_qkv, held, cores, picked, steps):
-    length, merged = grad_qkv.shape
-
-    def kernel(ins, outs, blocks, wait):
-        back_columns(ins[0], outs, blocks, picked, steps)
-
-    columns = len(picked) * held.shape[1]
+def back_rest(grad_qkv, early, helds, cores, units, picked, steps):
+    length, wide = grad_qkv.shape
+    depth = helds[0].shape[1]
+
+    def kernel(ins, outs, block):
+        back_columns(ins[0], ins[1:], outs, block, units, picked, steps, depth)
+
+    columns = len(picked) * depth
     outs = [(length // cores, columns) for _ in range(cores)]
-    flops = 2 * length * merged * columns
-    return call(kernel, [grad_qkv], held, outs, [], False, flops)
+    flops = 2 * length * wide * columns
+    return call(kernel, [grad_qkv] + early, None, helds, outs, [], False, flops)
 
 
 def add_landed(words, residual, pieces):
@@ -398,46 +457,60 @@
     normed_rows = normalize(fwd_rows, gain_row)
     normed_far = over_dp(normed_rows, 2)
     normed_near = over_dp(normed_rows, 1)
-    own_heads, held = forward_heads(blocks_of_cores(normed_rows), weight_qkv, None, words)
-    far_heads = forward_heads(blocks_of_cores(normed_far), weight_qkv, held, words)
-    near_heads = forward_heads(blocks_of_cores(normed_near), weight_qkv, held, words)
+    own_parts = blocks_of_cores(normed_rows)
+    own_heads, *helds = forward_heads([own_parts], weight_qkv, [], words)
+    near_parts = blocks_of_cores(normed_near)
+    far_parts = blocks_of_cores(normed_far)
+    near_heads, far_heads = forward_heads([near_parts, far_parts], None, helds, words)
     last_heads = over_dp(far_heads, 1)
 
     exchanged = [blocks_of_cores(piece) for piece in pieces]
-    terms, held_out = head_terms(exchanged, weight_out)
-    relay = over_dp(terms[3], 1)
-    near = over_dp(terms[1], 1)
-    joined = (terms[2].astype(jnp.float32) + relay.astype(jnp.float32)).astype(jnp.bfloat16)
-    terms = [terms[0], near, over_dp(joined, 2)]
+    (own, *rest), held_out = head_terms(exchanged, weight_out, 1)
+    landed = []
+    for index in range(len(rest) // 3):
+        near, far, relay = rest[3 * index : 3 * index + 3]
+        near = over_dp(near, 1)
+        relay = over_dp(relay, 1)
+        far = (far.astype(jnp.float32) + relay.astype(jnp.float32)).astype(jnp.bfloat16)
+        landed.append([near, over_dp(far, 2)])
 
     fwd_prev = over_pipe(fwd_rows, 1)
     bwd_next = over_pipe(bwd_rows, -1)
     grad_next = over_pipe(grad_rows, -1)
 
-    steps = width // held.shape[1]
-    first, rest = range(steps // 2), range(steps // 2, steps)
-    half = len(first) * held.shape[1]
-    grad_qkv, (keep, *sends) = back_first(qkv_saved, terms, held, words, cores, first, steps)
+    depth = helds[0].shape[1]
+    steps = width // depth
+    some = steps - max(1, steps // 4)
+    first, rest = range(some), range(some, steps)
+    half = len(first) * depth
+    units = range(qkv_saved.shape[1] // UNIT)
+    early = []
+    if len(landed) > 1:
+        early = [back_early(qkv_saved, own, landed[0], helds, words, cores, units[:1], steps)]
+        units = units[1:]
+    grad_qkv, (keep, *sends) = back_first(
+        qkv_saved, own, landed[-1], early, helds, words, cores, units, first, steps
+    )
     scaled = sum_over_cores(keep, sends) * gain_row[:, :half]
     arrived = [over_pipe(scaled.astype(jnp.bfloat16), -1)]
-    keep, *sends = back_rest(grad_qkv, held, cores, rest, steps)
+    keep, *sends = back_rest(grad_qkv, early, helds, cores, units, rest, steps)
     scaled = sum_over_cores(keep, sends) * gain_row[:, half:]
     arrived.append(over_pipe(scaled.astype(jnp.bfloat16), -1))
     scaled = jnp.concatenate(arrived, axis=1).astype(jnp.float32)
     grad_input = norm_back(bwd_next, grad_next, scaled)
 
-    landed = {}
-    groups = (((0, 1, 2), [own_heads, near_heads, far_heads]), ((3,), [last_heads]))
+    pieces = {}
+    groups = (((0,), [own_heads]), ((1, 2), [near_heads, far_heads]), ((3,), [last_heads]))
     for group, heads in groups:
         keep, *sends = project(heads, held_out, cores)
         summed = sum_over_cores(keep, sends).astype(jnp.bfloat16)
         for index, step in enumerate(group):
-            landed[step] = lax.ppermute(
+            pieces[step] = lax.ppermute(
                 summed[index * rows : (index + 1) * rows],
                 ("pipe", "dp"),
                 cross_pairs(step, 1),
             )
-    output = add_landed(words, fwd_prev, [landed[step] for step in range(replicas)])
+    output = add_landed(words, fwd_prev, [pieces[step] for step in range(replicas)])
     return (output[None, None], grad_input[None, None])
 
 

time: 117 us -> 128 us (1.094)
  starting transfers between devices: 26.9 us -> 36.7 us
  waiting for transfers between devices: 38.2 us -> 44.4 us
  other arithmetic: 7.12 us -> 4.14 us
  Pallas kernels: 40.4 us -> 38.1 us
    ppermute x9 -> x12, waiting for transfers between devices: 21.6 us -> 34.5 us  [over_dp(): return lax.ppermute(value, 'dp', partner_pairs(lax.axis_size('dp'), step))]
    ppermute x5, waiting for transfers between devices: 7.94 us -> 2.74 us  [over_pipe(): lax.ppermute(value, 'pipe', shift_pairs(lax.axis_size('pipe'), steps))]
    ppermute x4, waiting for transfers between devices: 8.64 us -> 4.49 us  [window(): lax.ppermute(summed[index * rows:(index + 1) * rows], ('pipe', 'dp'), cro...]
    ppermute x9 -> x12, starting transfers between devices: 12.3 us -> 16.3 us  [over_dp(): return lax.ppermute(value, 'dp', partner_pairs(lax.axis_size('dp'), step))]
    ppermute x4, starting transfers between devices: 5.18 us -> 8.56 us  [window(): lax.ppermute(summed[index * rows:(index + 1) * rows], ('pipe', 'dp'), cro...]
    ppermute x4 -> x5, waiting for transfers between devices: 0.01 us -> 2.67 us  [sum_over_cores(): block = lax.ppermute(sends[step - 1], 'tensor', shift_pairs(count, step))]
    pallas_call x8 -> x9, Pallas kernels: 39 us -> 36.7 us  [call(): pl.pallas_call(body, in_specs=[SCALAR if arg.dtype == jnp.int32 else LOCA...]
    ppermute x5, starting transfers between devices: 7.04 us -> 9.28 us  [over_pipe(): lax.ppermute(value, 'pipe', shift_pairs(lax.axis_size('pipe'), steps))]
  transfers between devices with their start and end apart: 29 -> 33, of which waited for: 8 -> 10; matrix products, arithmetic and copies ran while one was open for 4% -> 3% of each run, Pallas kernels for 35% -> 29%
where the time goes in v2:
time: 128 us
  waiting for transfers between devices  44.4 us (35%)
  Pallas kernels  38.1 us (30%)
  starting transfers between devices  36.7 us (29%)
  other arithmetic  4.14 us (3%)
  local copies, waits for them, and re-layouts  3.27 us (3%)
    pallas_call x9, Pallas kernels, call(): pl.pallas_call(body, in_specs=[SCALAR if arg.dtype == jnp.int32 else LOCA...  36.7 us
    ppermute x12, waiting for transfers between devices, over_dp(): return lax.ppermute(value, 'dp', partner_pairs(lax.axis_size('dp'), step))  34.5 us
    ppermute x12, starting transfers between devices, over_dp(): return lax.ppermute(value, 'dp', partner_pairs(lax.axis_size('dp'), step))  16.3 us
    ppermute x5, starting transfers between devices, over_pipe(): lax.ppermute(value, 'pipe', shift_pairs(lax.axis_size('pipe'), steps))  9.28 us
    ppermute x4, starting transfers between devices, window(): lax.ppermute(summed[index * rows:(index + 1) * rows], ('pipe', 'dp'), cro...  8.56 us
    ppermute x4, waiting for transfers between devices, window(): lax.ppermute(summed[index * rows:(index + 1) * rows], ('pipe', 'dp'), cro...  4.49 us
    ppermute x5, waiting for transfers between devices, over_pipe(): lax.ppermute(value, 'pipe', shift_pairs(lax.axis_size('pipe'), steps))  2.74 us
    ppermute x5, waiting for transfers between devices, sum_over_cores(): block = lax.ppermute(sends[step - 1], 'tensor', shift_pairs(count, step))  2.67 us
  transfers between devices with their start and end apart: 33, of which 10 were waited for; matrix products, arithmetic and copies ran while one was open for 3% of the time, Pallas kernels for 29%

profile of v2, /device:TPU:0, one launch (start us, length us, event | category | flops | bytes accessed | tf_op | source)
XLA Modules:
  0.0 127.5 jit_solution(14972786746488131877)
XLA Ops:
  1.7 3.1 %collective-permute-start.3 = (bf16[48,1024]{1,0:T(8,128)(2,1)S(1)}, bf16[48,1024]{1,0:T(8,128)(2,1)S(1)}, u32[]{:S(2)}, u32[]{:S(2)}) collective-permute-start(bf16[48,1024]{1,0:T(8,128)(2,1)S(1)} %get-tuple-element.54), channel_id=1, source_target_pairs={{0,1},{1,0},{2,3},{3,2},{4,5},{5,4},{6,7},{7,6},{8,9},{9,8},{10,11... | collective-permute-start | bytes 294920 | tf_op jit(solution)/shard_map/ppermute | solution.py:37
  4.9 2.6 %collective-permute-start.5 = (bf16[48,1024]{1,0:T(8,128)(2,1)S(1)}, bf16[48,1024]{1,0:T(8,128)(2,1)S(1)}, u32[]{:S(2)}, u32[]{:S(2)}) collective-permute-start(bf16[48,1024]{1,0:T(8,128)(2,1)S(1)} %get-tuple-element.53), channel_id=1, source_target_pairs={{0,2},{1,3},{2,0},{3,1},{4,6},{5,7},{6,4},{7,5},{8,10},{9,11},{10,... | collective-permute-start | bytes 294920 | tf_op jit(solution)/shard_map/ppermute | solution.py:37
  9.2 6.1 %collective-permute-done.5.refs_4_ = bf16[48,1024]{1,0:T(8,128)(2,1)S(1)} collective-permute-done((bf16[48,1024]{1,0:T(8,128)(2,1)S(1)}, bf16[48,1024]{1,0:T(8,128)(2,1)S(1)}, u32[]{:S(2)}, u32[]{:S(2)}) %collective-permute-start.5) | collective-permute-done | bytes 98336 | tf_op jit(solution)/shard_map/ppermute | solution.py:37
  17.1 1.6 %collective-permute-start.11 = (bf16[48,4096]{1,0:T(8,128)(2,1)S(1)}, bf16[48,4096]{1,0:T(8,128)(2,1)S(1)}, u32[]{:S(2)}, u32[]{:S(2)}) collective-permute-start(bf16[48,4096]{1,0:T(8,128)(2,1)S(1)} %fusion.2.refs_1_), channel_id=1, source_target_pairs={{0,1},{1,0},{2,3},{3,2},{4,5},{5,4},{6,7},{7,6},{8,9},{9,8},{10,11... | collective-permute-start | bytes 1179656 | tf_op jit(solution)/shard_map/ppermute | solution.py:37
  18.7 1.5 %collective-permute-start.13 = (bf16[48,4096]{1,0:T(8,128)(2,1)S(1)}, bf16[48,4096]{1,0:T(8,128)(2,1)S(1)}, u32[]{:S(2)}, u32[]{:S(2)}) collective-permute-start(bf16[48,4096]{1,0:T(8,128)(2,1)S(1)} %fusion.2.refs_1_), channel_id=1, source_target_pairs={{0,2},{1,3},{2,0},{3,1},{4,6},{5,7},{6,4},{7,5},{8,10},{9,11},{10,... | collective-permute-start | bytes 1179656 | tf_op jit(solution)/shard_map/ppermute | solution.py:37
  20.2 4.3 %shard_map.87 = (bf16[96,2304]{1,0:T(8,128)(2,1)S(1)}, bf16[96,768]{1,0:T(8,128)(2,1)S(1)}, bf16[96,768]{1,0:T(8,128)(2,1)S(1)}, bf16[96,768]{1,0:T(8,128)(2,1)S...) custom-call(bf16[48,1024]{1,0:T(8,128)(2,1)S(1)} %get-tuple-element., ...), custom_call_target="tpu_custom_call" | custom-call | flops 1811939328 | bytes 4718592 | tf_op jit(solution)/shard_map/pallas_call | solution.py:201
  24.5 2.1 %copy-done = bf16[3,768,1024]{2,1,0:T(8,128)(2,1)} copy-done((bf16[3,768,1024]{2,1,0:T(8,128)(2,1)}, bf16[3,768,1024]{2,1,0:T(8,128)(2,1)S(1)}, u32[]{:S(2)}) %copy-start) | copy-done | bytes 4718616
  26.6 1.5 %collective-permute-start.27 = (bf16[96,768]{1,0:T(8,128)(2,1)S(1)}, bf16[96,768]{1,0:T(8,128)(2,1)S(1)}, u32[]{:S(2)}, u32[]{:S(2)}) collective-permute-start(bf16[96,768]{1,0:T(8,128)(2,1)S(1)} %get-tuple-element.43), channel_id=1, source_target_pairs={{0,1},{1,0},{2,3},{3,2},{4,5},{5,4},{6,7},{7,6},{8,9},{9,8},{10,11... | collective-permute-start | bytes 442376 | tf_op jit(solution)/shard_map/ppermute | solution.py:37
  28.7 12.0 %collective-permute-done.27 = bf16[96,768]{1,0:T(8,128)(2,1)S(1)} collective-permute-done((bf16[96,768]{1,0:T(8,128)(2,1)S(1)}, bf16[96,768]{1,0:T(8,128)(2,1)S(1)}, u32[]{:S(2)}, u32[]{:S(2)}) %collective-permute-start.27) | collective-permute-done | bytes 147488 | tf_op jit(solution)/shard_map/ppermute | solution.py:37
  40.7 1.6 %collective-permute-start.24 = (bf16[96,1536]{1,0:T(8,128)(2,1)S(1)}, bf16[96,1536]{1,0:T(8,128)(2,1)S(1)}, u32[]{:S(2)}, u32[]{:S(2)}) collective-permute-start(bf16[96,1536]{1,0:T(8,128)(2,1)S(1)} %get-tuple-element.40), channel_id=1, source_target_pairs={{0,1},{1,0},{2,3},{3,2},{4,5},{5,4},{6,7},{7,6},{8,9},{9,8},{10,11... | collective-permute-start | bytes 884744 | tf_op jit(solution)/shard_map/ppermute | solution.py:37
  42.3 1.5 %collective-permute-start.28 = (bf16[96,768]{1,0:T(8,128)(2,1)S(1)}, bf16[96,768]{1,0:T(8,128)(2,1)S(1)}, u32[]{:S(2)}, u32[]{:S(2)}) collective-permute-start(bf16[96,768]{1,0:T(8,128)(2,1)S(1)} %add_convert_fusion.2), channel_id=1, source_target_pairs={{0,2},{1,3},{2,0},{3,1},{4,6},{5,7},{6,4},{7,5},{8,10},{9,11},{10,... | collective-permute-start | bytes 442376 | tf_op jit(solution)/shard_map/ppermute | solution.py:37
  43.9 10.0 %shard_map.86 = (bf16[96,2304]{1,0:T(8,128)(2,1)S(1)}, bf16[12,1024,1024]{2,1,0:T(8,128)(2,1)S(1)}) custom-call(s32[5]{0:T(128)S(1)} %pad_add_fusion.refs_0_.words_ref, bf16[48,4096]{1,0:T(8,128)(2,1)S(1)} %fusion.2.refs_1_, bf16[48,4096]{1,0:T(8,128)(2,1)S(1)} %collective-permute-done.1.refs_2_, bf16[4096,3072]{1,0:T(8,128)(2,1)} %bitcast.27), custom_call_target="tpu_custom_call" | custom-call | flops 2415919104 | bytes 25165824 | tf_op jit(solution)/shard_map/pallas_call | solution.py:201
  55.0 1.6 %collective-permute-start.23 = (bf16[96,1536]{1,0:T(8,128)(2,1)S(1)}, bf16[96,1536]{1,0:T(8,128)(2,1)S(1)}, u32[]{:S(2)}, u32[]{:S(2)}) collective-permute-start(bf16[96,1536]{1,0:T(8,128)(2,1)S(1)} %get-tuple-element.38), channel_id=1, source_target_pairs={{0,1},{1,0},{2,3},{3,2},{4,5},{5,4},{6,7},{7,6},{8,9},{9,8},{10,11... | collective-permute-start | bytes 884744 | tf_op jit(solution)/shard_map/ppermute | solution.py:37
  57.9 4.6 %shard_map.92 = (bf16[96,1024]{1,0:T(8,128)(2,1)}, f32[96,4096]{1,0:T(8,128)S(1)}) custom-call(s32[5]{0:T(128)S(1)} %pad_add_fusion.refs_0_.words_ref, bf16[96,3072]{1,0:T(8,128)(2,1)S(1)} %bitcast.25, bf16[96,2304]{1,0:T(8,128)(2,1)S(1)} %get-tuple-element.37.refs_2_, bf16[96,768]{1,0:T(8,128)(2,1)S(1)} %collective-permute-done.26.refs_3_, ...), custom_call_target="tpu_custom_call" | custom-call | flops 805306368 | tf_op jit(solution)/shard_map/pallas_call | solution.py:201
  62.6 2.4 %collective-permute-start.22 = (bf16[48,4096]{1,0:T(8,128)(2,1)S(1)}, bf16[48,4096]{1,0:T(8,128)(2,1)S(1)}, u32[]{:S(2)}, u32[]{:S(2)}) collective-permute-start(bf16[48,4096]{1,0:T(8,128)(2,1)S(1)} %bitcast.35), channel_id=1, source_target_pairs={{0,24},{8,0},{16,8},{24,16},{1,25},{9,1},{17,9},{25,17},{2,26},{10... | collective-permute-start | bytes 1179656 | tf_op jit(solution)/shard_map/ppermute | solution.py:41
  65.0 4.0 %collective-permute-done.23.refs_3_ = bf16[96,1536]{1,0:T(8,128)(2,1)S(1)} collective-permute-done((bf16[96,1536]{1,0:T(8,128)(2,1)S(1)}, bf16[96,1536]{1,0:T(8,128)(2,1)S(1)}, u32[]{:S(2)}, u32[]{:S(2)}) %collective-permute-start.23) | collective-permute-done | bytes 294944 | tf_op jit(solution)/shard_map/ppermute | solution.py:37
  69.0 2.4 %collective-permute-start.21 = (bf16[48,4096]{1,0:T(8,128)(2,1)S(1)}, bf16[48,4096]{1,0:T(8,128)(2,1)S(1)}, u32[]{:S(2)}, u32[]{:S(2)}) collective-permute-start(bf16[48,4096]{1,0:T(8,128)(2,1)S(1)} %bitcast.29), channel_id=1, source_target_pairs={{0,24},{8,0},{16,8},{24,16},{1,25},{9,1},{17,9},{25,17},{2,26},{10... | collective-permute-start | bytes 1179656 | tf_op jit(solution)/shard_map/ppermute | solution.py:41
  71.5 2.1 %collective-permute-done.25.refs_4_ = bf16[96,1536]{1,0:T(8,128)(2,1)S(1)} collective-permute-done((bf16[96,1536]{1,0:T(8,128)(2,1)S(1)}, bf16[96,1536]{1,0:T(8,128)(2,1)S(1)}, u32[]{:S(2)}, u32[]{:S(2)}) %collective-permute-start.25) | collective-permute-done | bytes 294944 | tf_op jit(solution)/shard_map/ppermute | solution.py:37
  73.5 1.5 %collective-permute-start = (bf16[48,4096]{1,0:T(8,128)(2,1)S(1)}, bf16[48,4096]{1,0:T(8,128)(2,1)S(1)}, u32[]{:S(2)}, u32[]{:S(2)}) collective-permute-start(bf16[48,4096]{1,0:T(8,128)(2,1)S(1)} %bitcast.28), channel_id=1, source_target_pairs={{0,8},{8,16},{16,24},{24,0},{1,9},{9,17},{17,25},{25,1},{2,10},{10... | collective-permute-start | bytes 1179656 | tf_op jit(solution)/shard_map/ppermute | solution.py:41
  75.0 5.8 %shard_map.93 = (bf16[96,2048]{1,0:T(8,128)(2,1)S(1)}, bf16[48,3072]{1,0:T(8,128)(2,1)S(1)}, bf16[48,3072]{1,0:T(8,128)(2,1)S(1)}) custom-call(s32[5]{0:T(128)S(1)} %pad_add_fusion.refs_0_.words_ref, bf16[96,3072]{1,0:T(8,128)(2,1)S(1)} %bitcast.26, bf16[96,2304]{1,0:T(8,128)(2,1)S(1)} %get-tuple-element.37.refs_2_, ...), custom_call_target="tpu_custom_call" | custom-call | flops 1207959552 | tf_op jit(solution)/shard_map/pallas_call | solution.py:201
  80.9 1.4 %shard_map.94 = (bf16[48,1024]{1,0:T(8,128)(2,1)S(1)}, bf16[48,1024]{1,0:T(8,128)(2,1)S(1)}) custom-call(bf16[96,2048]{1,0:T(8,128)(2,1)S(1)} %get-tuple-element.47.refs_0_, f32[96,4096]{1,0:T(8,128)S(1)} %get-tuple-element.44.refs_5_.refs_1_, bf16[12,1024,1024]{2,1,0:T(8,128)(2,1)S(1)} %get-tuple-element.30.refs_5_.refs_6_.refs_2_), custom_call_target="tpu_custom_call" | custom-call | flops 402653184 | tf_op jit(solution)/shard_map/pallas_call | solution.py:201
  82.4 7.7 %shard_map.89 = (bf16[96,2304]{1,0:T(8,128)(2,1)S(1)}, bf16[96,2304]{1,0:T(8,128)(2,1)S(1)}) custom-call(s32[5]{0:T(128)S(1)} %pad_add_fusion.refs_0_.words_ref, bf16[48,4096]{1,0:T(8,128)(2,1)S(1)} %collective-permute-done.11.refs_1_, bf16[48,4096]{1,0:T(8,128)(2,1)S(1)} %collective-permute-done.12.refs_2_, ...), custom_call_target="tpu_custom_call" | custom-call | flops 4831838208 | tf_op jit(solution)/shard_map/pallas_call | solution.py:201
  93.4 1.5 %collective-permute-start.30 = (bf16[48,3072]{1,0:T(8,128)(2,1)S(1)}, bf16[48,3072]{1,0:T(8,128)(2,1)S(1)}, u32[]{:S(2)}, u32[]{:S(2)}) collective-permute-start(bf16[48,3072]{1,0:T(8,128)(2,1)S(1)} %multiply_convert_fusion), channel_id=1, source_target_pairs={{0,24},{8,0},{16,8},{24,16},{1,25},{9,1},{17,9},{25,17},{2,26},{10... | collective-permute-start | bytes 884744 | tf_op jit(solution)/shard_map/ppermute | solution.py:41
  94.9 10.4 %collective-permute-done.18.refs_0_ = bf16[96,2304]{1,0:T(8,128)(2,1)S(1)} collective-permute-done((bf16[96,2304]{1,0:T(8,128)(2,1)S(1)}, bf16[96,2304]{1,0:T(8,128)(2,1)S(1)}, u32[]{:S(2)}, u32[]{:S(2)}) %collective-permute-start.18) | collective-permute-done | bytes 442400 | tf_op jit(solution)/shard_map/ppermute | solution.py:37
  106.2 1.3 collective-permute-done.19
  107.5 1.4 %collective-permute-start.32 = (bf16[48,1024]{1,0:T(8,128)(2,1)S(1)}, bf16[48,1024]{1,0:T(8,128)(2,1)S(1)}, u32[]{:S(2)}, u32[]{:S(2)}) collective-permute-start(bf16[48,1024]{1,0:T(8,128)(2,1)S(1)} %multiply_convert_fusion.1), channel_id=1, source_target_pairs={{0,24},{8,0},{16,8},{24,16},{1,25},{9,1},{17,9},{25,17},{2,26},{10... | collective-permute-start | bytes 294920 | tf_op jit(solution)/shard_map/ppermute | solution.py:41
  109.6 2.7 %collective-permute-done.32 = bf16[48,1024]{1,0:T(8,128)(2,1)S(1)} collective-permute-done((bf16[48,1024]{1,0:T(8,128)(2,1)S(1)}, bf16[48,1024]{1,0:T(8,128)(2,1)S(1)}, u32[]{:S(2)}, u32[]{:S(2)}) %collective-permute-start.32) | collective-permute-done | bytes 98336 | tf_op jit(solution)/shard_map/ppermute | solution.py:41
  112.4 2.9 %collective-permute-start.16 = (bf16[48,1024]{1,0:T(8,128)(2,1)S(1)}, bf16[48,1024]{1,0:T(8,128)(2,1)S(1)}, u32[]{:S(2)}, u32[]{:S(2)}) collective-permute-start(bf16[48,1024]{1,0:T(8,128)(2,1)S(1)} %get-tuple-element.57), channel_id=1, source_target_pairs={{0,9},{1,8},{2,11},{3,10},{8,17},{9,16},{10,19},{11,18},{16,25},{1... | collective-permute-start | bytes 294920 | tf_op jit(solution)/shard_map/ppermute | solution.py:508
  115.3 1.7 %collective-permute-start.17 = (bf16[48,1024]{1,0:T(8,128)(2,1)S(1)}, bf16[48,1024]{1,0:T(8,128)(2,1)S(1)}, u32[]{:S(2)}, u32[]{:S(2)}) collective-permute-start(bf16[48,1024]{1,0:T(8,128)(2,1)S(1)} %get-tuple-element.56), channel_id=1, source_target_pairs={{0,10},{1,11},{2,8},{3,9},{8,18},{9,19},{10,16},{11,17},{16,26},{1... | collective-permute-start | bytes 294920 | tf_op jit(solution)/shard_map/ppermute | solution.py:508
  117.2 3.3 %collective-permute-start.20 = (bf16[48,1024]{1,0:T(8,128)(2,1)S(1)}, bf16[48,1024]{1,0:T(8,128)(2,1)S(1)}, u32[]{:S(2)}, u32[]{:S(2)}) collective-permute-start(bf16[48,1024]{1,0:T(8,128)(2,1)S(1)} %add_convert_fusion.3), channel_id=1, source_target_pairs={{0,11},{1,10},{2,9},{3,8},{8,19},{9,18},{10,17},{11,16},{16,27},{1... | collective-permute-start | bytes 294920 | tf_op jit(solution)/shard_map/ppermute | solution.py:508
  121.7 4.5 %collective-permute-done.17.refs_2_ = bf16[48,1024]{1,0:T(8,128)(2,1)S(1)} collective-permute-done((bf16[48,1024]{1,0:T(8,128)(2,1)S(1)}, bf16[48,1024]{1,0:T(8,128)(2,1)S(1)}, u32[]{:S(2)}, u32[]{:S(2)}) %collective-permute-start.17) | collective-permute-done | bytes 98336 | tf_op jit(solution)/shard_map/ppermute | solution.py:508
  126.1 1.4 %add_landed.1 = bf16[48,4096]{1,0:T(8,128)(2,1)} custom-call(s32[5]{0:T(128)S(1)} %pad_add_fusion.refs_0_.words_ref, bf16[48,4096]{1,0:T(8,128)(2,1)S(1)} %collective-permute-done.residual_ref, bf16[48,1024]{1,0:T(8,128)(2,1)S(1)} %collective-permute-done.10.refs_0_, bf16[48,1024]{1,0:T(8,128)(2,1)S(1)} %collective-permute-done.16.refs_1_, ...), custom_call_target="tpu_custom_call" | custom-call | tf_op jit(solution)/shard_map/add_landed/pallas_call | solution.py:418
  (80 shorter events, 14.1 us)
Async XLA Ops:
  1.7 6.9 %collective-permute-start.3 = (bf16[48,1024]{1,0:T(8,128)(2,1)S(1)}, bf16[48,1024]{1,0:T(8,128)(2,1)S(1)}, u32[]{:S(2)}, u32[]{:S(2)}) collective-permute-start(bf16[48,1024]{1,0:T(8,128)(2,1)S(1)} %get-tuple-element.54), channel_id=1, source_target_pairs={{0,1},{1,0},{2,3},{3,2},{4,5},{5,4},{6,7},{7,6},{8,9},{9,8},{10,11... | collective-permute-start | bytes 294920 | tf_op jit(solution)/shard_map/ppermute | solution.py:37
  4.9 10.4 %collective-permute-start.5 = (bf16[48,1024]{1,0:T(8,128)(2,1)S(1)}, bf16[48,1024]{1,0:T(8,128)(2,1)S(1)}, u32[]{:S(2)}, u32[]{:S(2)}) collective-permute-start(bf16[48,1024]{1,0:T(8,128)(2,1)S(1)} %get-tuple-element.53), channel_id=1, source_target_pairs={{0,2},{1,3},{2,0},{3,1},{4,6},{5,7},{6,4},{7,5},{8,10},{9,11},{10,... | collective-permute-start | bytes 294920 | tf_op jit(solution)/shard_map/ppermute | solution.py:37
  7.4 7.8 %collective-permute-start.7 = (bf16[48,1024]{1,0:T(8,128)(2,1)S(1)}, bf16[48,1024]{1,0:T(8,128)(2,1)S(1)}, u32[]{:S(2)}, u32[]{:S(2)}) collective-permute-start(bf16[48,1024]{1,0:T(8,128)(2,1)S(1)} %get-tuple-element.52), channel_id=1, source_target_pairs={{0,3},{1,2},{2,1},{3,0},{4,7},{5,6},{6,5},{7,4},{8,11},{9,10},{10,... | collective-permute-start | bytes 294920 | tf_op jit(solution)/shard_map/ppermute | solution.py:37
  7.5 9.6 %collective-permute-start.2 = (bf16[48,1024]{1,0:T(8,128)(2,1)S(1)}, bf16[48,1024]{1,0:T(8,128)(2,1)S(1)}, u32[]{:S(2)}, u32[]{:S(2)}) collective-permute-start(bf16[48,1024]{1,0:T(8,128)(2,1)S(1)} %get-tuple-element.55.refs_0_), channel_id=1, source_target_pairs={{0,4},{4,0},{1,5},{5,1},{2,6},{6,2},{3,7},{7,3},{8,12},{12,8},{9,1... | collective-permute-start | bytes 294920 | tf_op jit(solution)/shard_map/ppermute | solution.py:47
  8.7 10.0 %collective-permute-start.4 = (bf16[48,1024]{1,0:T(8,128)(2,1)S(1)}, bf16[48,1024]{1,0:T(8,128)(2,1)S(1)}, u32[]{:S(2)}, u32[]{:S(2)}) collective-permute-start(bf16[48,1024]{1,0:T(8,128)(2,1)S(1)} %collective-permute-done.3.refs_2_), channel_id=1, source_target_pairs={{0,4},{4,0},{1,5},{5,1},{2,6},{6,2},{3,7},{7,3},{8,12},{12,8},{9,1... | collective-permute-start | bytes 294920 | tf_op jit(solution)/shard_map/ppermute | solution.py:47
  15.3 4.9 %collective-permute-start.6 = (bf16[48,1024]{1,0:T(8,128)(2,1)S(1)}, bf16[48,1024]{1,0:T(8,128)(2,1)S(1)}, u32[]{:S(2)}, u32[]{:S(2)}) collective-permute-start(bf16[48,1024]{1,0:T(8,128)(2,1)S(1)} %collective-permute-done.5.refs_4_), channel_id=1, source_target_pairs={{0,4},{4,0},{1,5},{5,1},{2,6},{6,2},{3,7},{7,3},{8,12},{12,8},{9,1... | collective-permute-start | bytes 294920 | tf_op jit(solution)/shard_map/ppermute | solution.py:47
  15.3 4.9 %collective-permute-start.8 = (bf16[48,1024]{1,0:T(8,128)(2,1)S(1)}, bf16[48,1024]{1,0:T(8,128)(2,1)S(1)}, u32[]{:S(2)}, u32[]{:S(2)}) collective-permute-start(bf16[48,1024]{1,0:T(8,128)(2,1)S(1)} %collective-permute-done.7.refs_6_), channel_id=1, source_target_pairs={{0,4},{4,0},{1,5},{5,1},{2,6},{6,2},{3,7},{7,3},{8,12},{12,8},{9,1... | collective-permute-start | bytes 294920 | tf_op jit(solution)/shard_map/ppermute | solution.py:47
  17.0 25.3 %collective-permute-start.1 = (bf16[48,4096]{1,0:T(8,128)(2,1)S(1)}, bf16[48,4096]{1,0:T(8,128)(2,1)S(1)}, u32[]{:S(2)}, u32[]{:S(2)}) collective-permute-start(bf16[48,4096]{1,0:T(8,128)(2,1)S(1)} %fusion.2.refs_1_), channel_id=1, source_target_pairs={{0,4},{4,0},{1,5},{5,1},{2,6},{6,2},{3,7},{7,3},{8,12},{12,8},{9,1... | collective-permute-start | bytes 1179656 | tf_op jit(solution)/shard_map/ppermute | solution.py:47
  17.1 39.6 %collective-permute-start.11 = (bf16[48,4096]{1,0:T(8,128)(2,1)S(1)}, bf16[48,4096]{1,0:T(8,128)(2,1)S(1)}, u32[]{:S(2)}, u32[]{:S(2)}) collective-permute-start(bf16[48,4096]{1,0:T(8,128)(2,1)S(1)} %fusion.2.refs_1_), channel_id=1, source_target_pairs={{0,1},{1,0},{2,3},{3,2},{4,5},{5,4},{6,7},{7,6},{8,9},{9,8},{10,11... | collective-permute-start | bytes 1179656 | tf_op jit(solution)/shard_map/ppermute | solution.py:37
  18.7 38.2 %collective-permute-start.13 = (bf16[48,4096]{1,0:T(8,128)(2,1)S(1)}, bf16[48,4096]{1,0:T(8,128)(2,1)S(1)}, u32[]{:S(2)}, u32[]{:S(2)}) collective-permute-start(bf16[48,4096]{1,0:T(8,128)(2,1)S(1)} %fusion.2.refs_1_), channel_id=1, source_target_pairs={{0,2},{1,3},{2,0},{3,1},{4,6},{5,7},{6,4},{7,5},{8,10},{9,11},{10,... | collective-permute-start | bytes 1179656 | tf_op jit(solution)/shard_map/ppermute | solution.py:37
  26.6 14.1 %collective-permute-start.27 = (bf16[96,768]{1,0:T(8,128)(2,1)S(1)}, bf16[96,768]{1,0:T(8,128)(2,1)S(1)}, u32[]{:S(2)}, u32[]{:S(2)}) collective-permute-start(bf16[96,768]{1,0:T(8,128)(2,1)S(1)} %get-tuple-element.43), channel_id=1, source_target_pairs={{0,1},{1,0},{2,3},{3,2},{4,5},{5,4},{6,7},{7,6},{8,9},{9,8},{10,11... | collective-permute-start | bytes 442376 | tf_op jit(solution)/shard_map/ppermute | solution.py:37
  28.2 26.8 %collective-permute-start.26 = (bf16[96,768]{1,0:T(8,128)(2,1)S(1)}, bf16[96,768]{1,0:T(8,128)(2,1)S(1)}, u32[]{:S(2)}, u32[]{:S(2)}) collective-permute-start(bf16[96,768]{1,0:T(8,128)(2,1)S(1)} %get-tuple-element.41), channel_id=1, source_target_pairs={{0,1},{1,0},{2,3},{3,2},{4,5},{5,4},{6,7},{7,6},{8,9},{9,8},{10,11... | collective-permute-start | bytes 442376 | tf_op jit(solution)/shard_map/ppermute | solution.py:37
  40.7 14.1 %collective-permute-start.24 = (bf16[96,1536]{1,0:T(8,128)(2,1)S(1)}, bf16[96,1536]{1,0:T(8,128)(2,1)S(1)}, u32[]{:S(2)}, u32[]{:S(2)}) collective-permute-start(bf16[96,1536]{1,0:T(8,128)(2,1)S(1)} %get-tuple-element.40), channel_id=1, source_target_pairs={{0,1},{1,0},{2,3},{3,2},{4,5},{5,4},{6,7},{7,6},{8,9},{9,8},{10,11... | collective-permute-start | bytes 884744 | tf_op jit(solution)/shard_map/ppermute | solution.py:37
  42.3 14.8 %collective-permute-start.28 = (bf16[96,768]{1,0:T(8,128)(2,1)S(1)}, bf16[96,768]{1,0:T(8,128)(2,1)S(1)}, u32[]{:S(2)}, u32[]{:S(2)}) collective-permute-start(bf16[96,768]{1,0:T(8,128)(2,1)S(1)} %add_convert_fusion.2), channel_id=1, source_target_pairs={{0,2},{1,3},{2,0},{3,1},{4,6},{5,7},{6,4},{7,5},{8,10},{9,11},{10,... | collective-permute-start | bytes 442376 | tf_op jit(solution)/shard_map/ppermute | solution.py:37
  54.8 7.7 %collective-permute-start.9 = (bf16[48,1024]{1,0:T(8,128)(2,1)S(1)}, bf16[48,1024]{1,0:T(8,128)(2,1)S(1)}, u32[]{:S(2)}, u32[]{:S(2)}) collective-permute-start(bf16[48,1024]{1,0:T(8,128)(2,1)S(1)} %get-tuple-element.29), channel_id=1, source_target_pairs={{0,4},{4,0},{1,5},{5,1},{2,6},{6,2},{3,7},{7,3},{8,12},{12,8},{9,1... | collective-permute-start | bytes 294920 | tf_op jit(solution)/shard_map/ppermute | solution.py:55
  55.0 14.0 %collective-permute-start.23 = (bf16[96,1536]{1,0:T(8,128)(2,1)S(1)}, bf16[96,1536]{1,0:T(8,128)(2,1)S(1)}, u32[]{:S(2)}, u32[]{:S(2)}) collective-permute-start(bf16[96,1536]{1,0:T(8,128)(2,1)S(1)} %get-tuple-element.38), channel_id=1, source_target_pairs={{0,1},{1,0},{2,3},{3,2},{4,5},{5,4},{6,7},{7,6},{8,9},{9,8},{10,11... | collective-permute-start | bytes 884744 | tf_op jit(solution)/shard_map/ppermute | solution.py:37
  56.6 25.7 %collective-permute-start.12 = (bf16[48,4096]{1,0:T(8,128)(2,1)S(1)}, bf16[48,4096]{1,0:T(8,128)(2,1)S(1)}, u32[]{:S(2)}, u32[]{:S(2)}) collective-permute-start(bf16[48,4096]{1,0:T(8,128)(2,1)S(1)} %collective-permute-done.11.refs_1_), channel_id=1, source_target_pairs={{0,4},{4,0},{1,5},{5,1},{2,6},{6,2},{3,7},{7,3},{8,12},{12,8},{9,1... | collective-permute-start | bytes 1179656 | tf_op jit(solution)/shard_map/ppermute | solution.py:47
  56.8 25.5 %collective-permute-start.14 = (bf16[48,4096]{1,0:T(8,128)(2,1)S(1)}, bf16[48,4096]{1,0:T(8,128)(2,1)S(1)}, u32[]{:S(2)}, u32[]{:S(2)}) collective-permute-start(bf16[48,4096]{1,0:T(8,128)(2,1)S(1)} %collective-permute-done.13.refs_3_), channel_id=1, source_target_pairs={{0,4},{4,0},{1,5},{5,1},{2,6},{6,2},{3,7},{7,3},{8,12},{12,8},{9,1... | collective-permute-start | bytes 1179656 | tf_op jit(solution)/shard_map/ppermute | solution.py:47
  57.2 16.4 %collective-permute-start.25 = (bf16[96,1536]{1,0:T(8,128)(2,1)S(1)}, bf16[96,1536]{1,0:T(8,128)(2,1)S(1)}, u32[]{:S(2)}, u32[]{:S(2)}) collective-permute-start(bf16[96,1536]{1,0:T(8,128)(2,1)S(1)} %add_convert_fusion), channel_id=1, source_target_pairs={{0,2},{1,3},{2,0},{3,1},{4,6},{5,7},{6,4},{7,5},{8,10},{9,11},{10,... | collective-permute-start | bytes 884744 | tf_op jit(solution)/shard_map/ppermute | solution.py:37
  62.6 46.4 %collective-permute-start.22 = (bf16[48,4096]{1,0:T(8,128)(2,1)S(1)}, bf16[48,4096]{1,0:T(8,128)(2,1)S(1)}, u32[]{:S(2)}, u32[]{:S(2)}) collective-permute-start(bf16[48,4096]{1,0:T(8,128)(2,1)S(1)} %bitcast.35), channel_id=1, source_target_pairs={{0,24},{8,0},{16,8},{24,16},{1,25},{9,1},{17,9},{25,17},{2,26},{10... | collective-permute-start | bytes 1179656 | tf_op jit(solution)/shard_map/ppermute | solution.py:41
  69.0 48.2 %collective-permute-start.21 = (bf16[48,4096]{1,0:T(8,128)(2,1)S(1)}, bf16[48,4096]{1,0:T(8,128)(2,1)S(1)}, u32[]{:S(2)}, u32[]{:S(2)}) collective-permute-start(bf16[48,4096]{1,0:T(8,128)(2,1)S(1)} %bitcast.29), channel_id=1, source_target_pairs={{0,24},{8,0},{16,8},{24,16},{1,25},{9,1},{17,9},{25,17},{2,26},{10... | collective-permute-start | bytes 1179656 | tf_op jit(solution)/shard_map/ppermute | solution.py:41
  73.5 48.1 %collective-permute-start = (bf16[48,4096]{1,0:T(8,128)(2,1)S(1)}, bf16[48,4096]{1,0:T(8,128)(2,1)S(1)}, u32[]{:S(2)}, u32[]{:S(2)}) collective-permute-start(bf16[48,4096]{1,0:T(8,128)(2,1)S(1)} %bitcast.28), channel_id=1, source_target_pairs={{0,8},{8,16},{16,24},{24,0},{1,9},{9,17},{17,25},{25,1},{2,10},{10... | collective-permute-start | bytes 1179656 | tf_op jit(solution)/shard_map/ppermute | solution.py:41
  82.3 9.4 %collective-permute-start.31 = (bf16[48,1024]{1,0:T(8,128)(2,1)S(1)}, bf16[48,1024]{1,0:T(8,128)(2,1)S(1)}, u32[]{:S(2)}, u32[]{:S(2)}) collective-permute-start(bf16[48,1024]{1,0:T(8,128)(2,1)S(1)} %get-tuple-element.49), channel_id=1, source_target_pairs={{0,4},{4,0},{1,5},{5,1},{2,6},{6,2},{3,7},{7,3},{8,12},{12,8},{9,1... | collective-permute-start | bytes 294920 | tf_op jit(solution)/shard_map/ppermute | solution.py:55
  91.2 1.6 %collective-permute-start.15 = (bf16[96,1024]{1,0:T(8,128)(2,1)S(1)}, bf16[96,1024]{1,0:T(8,128)(2,1)S(1)}, u32[]{:S(2)}, u32[]{:S(2)}) collective-permute-start(bf16[96,1024]{1,0:T(8,128)(2,1)S(1)} %get-tuple-element.34), channel_id=1, source_target_pairs={{0,4},{4,0},{1,5},{5,1},{2,6},{6,2},{3,7},{7,3},{8,12},{12,8},{9,1... | collective-permute-start | bytes 589832 | tf_op jit(solution)/shard_map/ppermute | solution.py:55
  91.7 1.6 %collective-permute-start.29 = (bf16[48,3072]{1,0:T(8,128)(2,1)S(1)}, bf16[48,3072]{1,0:T(8,128)(2,1)S(1)}, u32[]{:S(2)}, u32[]{:S(2)}) collective-permute-start(bf16[48,3072]{1,0:T(8,128)(2,1)S(1)} %get-tuple-element.46), channel_id=1, source_target_pairs={{0,4},{4,0},{1,5},{5,1},{2,6},{6,2},{3,7},{7,3},{8,12},{12,8},{9,1... | collective-permute-start | bytes 884744 | tf_op jit(solution)/shard_map/ppermute | solution.py:55
  92.8 12.4 %collective-permute-start.18 = (bf16[96,2304]{1,0:T(8,128)(2,1)S(1)}, bf16[96,2304]{1,0:T(8,128)(2,1)S(1)}, u32[]{:S(2)}, u32[]{:S(2)}) collective-permute-start(bf16[96,2304]{1,0:T(8,128)(2,1)S(1)} %get-tuple-element.32.refs_1_), channel_id=1, source_target_pairs={{0,1},{1,0},{2,3},{3,2},{4,5},{5,4},{6,7},{7,6},{8,9},{9,8},{10,11... | collective-permute-start | bytes 1327112 | tf_op jit(solution)/shard_map/ppermute | solution.py:37
  93.4 21.9 %collective-permute-start.30 = (bf16[48,3072]{1,0:T(8,128)(2,1)S(1)}, bf16[48,3072]{1,0:T(8,128)(2,1)S(1)}, u32[]{:S(2)}, u32[]{:S(2)}) collective-permute-start(bf16[48,3072]{1,0:T(8,128)(2,1)S(1)} %multiply_convert_fusion), channel_id=1, source_target_pairs={{0,24},{8,0},{16,8},{24,16},{1,25},{9,1},{17,9},{25,17},{2,26},{10... | collective-permute-start | bytes 884744 | tf_op jit(solution)/shard_map/ppermute | solution.py:41
  107.5 4.9 %collective-permute-start.32 = (bf16[48,1024]{1,0:T(8,128)(2,1)S(1)}, bf16[48,1024]{1,0:T(8,128)(2,1)S(1)}, u32[]{:S(2)}, u32[]{:S(2)}) collective-permute-start(bf16[48,1024]{1,0:T(8,128)(2,1)S(1)} %multiply_convert_fusion.1), channel_id=1, source_target_pairs={{0,24},{8,0},{16,8},{24,16},{1,25},{9,1},{17,9},{25,17},{2,26},{10... | collective-permute-start | bytes 294920 | tf_op jit(solution)/shard_map/ppermute | solution.py:41
  109.0 12.7 %collective-permute-start.10 = (bf16[48,1024]{1,0:T(8,128)(2,1)S(1)}, bf16[48,1024]{1,0:T(8,128)(2,1)S(1)}, u32[]{:S(2)}, u32[]{:S(2)}) collective-permute-start(bf16[48,1024]{1,0:T(8,128)(2,1)S(1)} %add_convert_fusion.4), channel_id=1, source_target_pairs={{0,8},{1,9},{2,10},{3,11},{8,16},{9,17},{10,18},{11,19},{16,24},{1... | collective-permute-start | bytes 294920 | tf_op jit(solution)/shard_map/ppermute | solution.py:508
  112.4 9.3 %collective-permute-start.16 = (bf16[48,1024]{1,0:T(8,128)(2,1)S(1)}, bf16[48,1024]{1,0:T(8,128)(2,1)S(1)}, u32[]{:S(2)}, u32[]{:S(2)}) collective-permute-start(bf16[48,1024]{1,0:T(8,128)(2,1)S(1)} %get-tuple-element.57), channel_id=1, source_target_pairs={{0,9},{1,8},{2,11},{3,10},{8,17},{9,16},{10,19},{11,18},{16,25},{1... | collective-permute-start | bytes 294920 | tf_op jit(solution)/shard_map/ppermute | solution.py:508
  115.3 10.9 %collective-permute-start.17 = (bf16[48,1024]{1,0:T(8,128)(2,1)S(1)}, bf16[48,1024]{1,0:T(8,128)(2,1)S(1)}, u32[]{:S(2)}, u32[]{:S(2)}) collective-permute-start(bf16[48,1024]{1,0:T(8,128)(2,1)S(1)} %get-tuple-element.56), channel_id=1, source_target_pairs={{0,10},{1,11},{2,8},{3,9},{8,18},{9,19},{10,16},{11,17},{16,26},{1... | collective-permute-start | bytes 294920 | tf_op jit(solution)/shard_map/ppermute | solution.py:508
  117.2 8.9 %collective-permute-start.20 = (bf16[48,1024]{1,0:T(8,128)(2,1)S(1)}, bf16[48,1024]{1,0:T(8,128)(2,1)S(1)}, u32[]{:S(2)}, u32[]{:S(2)}) collective-permute-start(bf16[48,1024]{1,0:T(8,128)(2,1)S(1)} %add_convert_fusion.3), channel_id=1, source_target_pairs={{0,11},{1,10},{2,9},{3,8},{8,19},{9,18},{10,17},{11,16},{16,27},{1... | collective-permute-start | bytes 294920 | tf_op jit(solution)/shard_map/ppermute | solution.py:508
  (9 other events, 88.1 us)

commit v3 on v2

--- a/solution.py
+++ b/solution.py
@@ -55,24 +55,6 @@
         block = lax.ppermute(sends[step - 1], "tensor", shift_pairs(count, step))
         total = total + block.astype(jnp.float32)
     return total
-
-
-def normalize(inputs, gain_row):
-    widened = inputs.astype(jnp.float32)
-    inverse = lax.rsqrt(jnp.mean(widened * widened, axis=-1, keepdims=True) + 1e-05)
-    return (widened * inverse * gain_row).astype(jnp.bfloat16)
-
-
-def norm_back(inputs, grad_rows, scaled):
-    widened = inputs.astype(jnp.float32)
-    inverse = lax.rsqrt(jnp.mean(widened * widened, axis=-1, keepdims=True) + 1e-05)
-    middle = jnp.mean(widened * scaled, axis=-1, keepdims=True)
-    result = (
-        grad_rows.astype(jnp.float32)
-        + inverse * scaled
-        - widened * inverse * inverse * inverse * middle
-    )
-    return result.astype(jnp.bfloat16)
 
 
 def mxu(left, right, left_dim, right_dim):
@@ -155,18 +137,32 @@
 REMOTE = pl.BlockSpec(memory_space=pltpu.HBM)
 
 
-def call(kernel, args, weight, helds, outs, blocks, keep, flops):
+def call(kernel, args, weight, helds, outs, blocks, keep, flops, temps=(), fetch=()):
     count = len(args)
     extra = 1 if blocks else len(helds)
     shape = (len(blocks), blocks[0][0].size, blocks[0][1].size) if blocks else ()
     moved = 2 * math.prod(shape) if blocks else 0
 
     def body(*refs):
-        ins, weight_refs = refs[:count], refs[count : count + extra]
+        split = len(refs) - len(temps)
+        refs, rest = refs[:split], refs[split:]
+        ins, weight_refs = list(refs[:count]), refs[count : count + extra]
+        if fetch:
+            *landing, fetch_sems = refs[len(refs) - len(fetch) - 1 :]
+            refs = refs[: len(refs) - len(fetch) - 1]
+            fetches = [
+                pltpu.make_async_copy(ins[index], ref, fetch_sems.at[place])
+                for place, (index, ref) in enumerate(zip(fetch, landing))
+            ]
+            for move in fetches:
+                move.start()
+            for move, index, ref in zip(fetches, fetch, landing):
+                move.wait()
+                ins[index] = ref
         results = refs[count + extra : count + extra + len(outs)]
         if not blocks:
             places = [ref.at[index] for ref in weight_refs for index in range(ref.shape[0])]
-            kernel(ins, results, lambda index: places[index][...])
+            kernel(ins, results, lambda index: places[index][...], *rest)
             return
         held, sems = refs[count + extra + len(outs) :]
         moves = [
@@ -180,7 +176,7 @@
             moves[index].wait()
             return held[index]
 
-        kernel(ins, results, loaded)
+        kernel(ins, results, loaded, *rest)
 
     out_specs = [LOCAL for _ in outs]
     out_shape = [
@@ -197,14 +193,23 @@
         weights = [pltpu.with_memory_space_constraint(weight, pltpu.HBM)]
     else:
         weights = [pltpu.with_memory_space_constraint(held, pltpu.VMEM) for held in helds]
+    if fetch:
+        scratch += [pltpu.VMEM(args[index].shape, args[index].dtype) for index in fetch]
+        scratch.append(pltpu.SemaphoreType.DMA((len(fetch),)))
+        args = [
+            pltpu.with_memory_space_constraint(arg, pltpu.HBM) if index in fetch else arg
+            for index, arg in enumerate(args)
+        ]
+    specs = [SCALAR if arg.dtype == jnp.int32 else LOCAL for arg in args]
+    for index in fetch:
+        specs[index] = REMOTE
     limit = (0 if keep else moved) + (8 << 20)
     return pl.pallas_call(
         body,
-        in_specs=[SCALAR if arg.dtype == jnp.int32 else LOCAL for arg in args]
-        + [REMOTE if blocks else LOCAL for _ in weights],
+        in_specs=specs + [REMOTE if blocks else LOCAL for _ in weights],
         out_specs=out_specs,
         out_shape=out_shape,
-        scratch_shapes=scratch,
+        scratch_shapes=scratch + list(temps),
         compiler_params=pltpu.CompilerParams(vmem_limit_bytes=limit),
         cost_estimate=pl.CostEstimate(flops=flops, bytes_accessed=moved, transcendentals=0),
     )(*args, *weights)
@@ -215,7 +220,16 @@
     return [(pl.ds(row, block), pl.ds(0, columns)) for row in range(0, size, block)]
 
 
-def forward_heads(batches, weight, helds, start):
+def normalize_rows(ref, gain_ref, out_ref, first):
+    step = 16 if ref.shape[0] % 16 == 0 else ref.shape[0]
+    for at in range(0, ref.shape[0], step):
+        wide = ref[at : at + step].astype(jnp.float32)
+        inverse = lax.rsqrt(jnp.mean(wide * wide, axis=-1, keepdims=True) + 1e-05)
+        normed = (wide * inverse * gain_ref[...]).astype(jnp.bfloat16)
+        out_ref[first + at : first + at + step] = normed
+
+
+def forward_heads(batches, weight, helds, start, gain, fetch):
     rows, width = batches[0][0].shape
     length = rows * len(batches[0])
     flat = [part for parts in batches for part in parts]
@@ -223,13 +237,14 @@
     steps = width // depth
     units = sum(held.shape[0] for held in helds) // steps if helds else weight.shape[1] // UNIT
 
-    def kernel(ins, outs, block):
+    def kernel(ins, outs, block, normed_ref):
+        for index, ref in enumerate(ins[2:]):
+            normalize_rows(ref, ins[1], normed_ref, index * rows)
         masked = later_keys(length, ins[0][0])
         for unit in range(units):
             total = None
             for step in range(steps):
-                at = slice(step * depth, (step + 1) * depth)
-                left = jnp.concatenate([ref[:, at] for ref in ins[1:]], axis=0)
+                left = normed_ref[:, step * depth : (step + 1) * depth]
                 product = mxu(left, block(unit * steps + step), 1, 0)
                 total = product if total is None else total + product
             total = total.astype(jnp.bfloat16)
@@ -246,7 +261,10 @@
         ]
     flops = 2 * length * len(batches) * width * units * UNIT
     outs = [(length, units * GROUP * HD) for _ in batches]
-    return call(kernel, [start] + flat, weight, helds, outs, blocks, not helds, flops)
+    temps = [pltpu.VMEM((length * len(batches), width), jnp.bfloat16)]
+    args = [start, gain] + flat
+    keep = not helds
+    return call(kernel, args, weight, helds, outs, blocks, keep, flops, temps, fetch)
 
 
 def column_parts(depth):
@@ -405,24 +423,33 @@
     return call(kernel, [grad_qkv] + early, None, helds, outs, [], False, flops)
 
 
-def add_landed(words, residual, pieces):
-    columns = pieces[0].shape[1]
-
-    def kernel(words_ref, residual_ref, *refs):
-        out_ref = refs[-1]
-        for step, piece_ref in enumerate(refs[:-1]):
-            at = pl.ds(pl.multiple_of(words_ref[1 + step], columns), columns)
-            total = residual_ref[:, at].astype(jnp.float32) + piece_ref[...].astype(jnp.float32)
-            out_ref[:, at] = total.astype(jnp.bfloat16)
+def norm_back(inputs, grad_rows, parts):
+    rows, _ = inputs.shape
+    step = 16 if rows % 16 == 0 else rows
+
+    def kernel(inputs_ref, grad_ref, *refs):
+        *part_refs, out_ref = refs
+        for at in range(0, rows, step):
+            wide = inputs_ref[at : at + step].astype(jnp.float32)
+            scaled = [ref[at : at + step].astype(jnp.float32) for ref in part_refs]
+            scaled = jnp.concatenate(scaled, axis=1)
+            inverse = lax.rsqrt(jnp.mean(wide * wide, axis=-1, keepdims=True) + 1e-05)
+            middle = jnp.mean(wide * scaled, axis=-1, keepdims=True)
+            result = (
+                grad_ref[at : at + step].astype(jnp.float32)
+                + inverse * scaled
+                - wide * (inverse * inverse * inverse * middle)
+            )
+            out_ref[at : at + step] = result.astype(jnp.bfloat16)
 
     return pl.pallas_call(
         kernel,
-        in_specs=[SCALAR] + [LOCAL for _ in range(1 + len(pieces))],
+        in_specs=[LOCAL for _ in range(2 + len(parts))],
         out_specs=LOCAL,
-        out_shape=jax.ShapeDtypeStruct(residual.shape, jnp.bfloat16),
+        out_shape=jax.ShapeDtypeStruct(inputs.shape, jnp.bfloat16),
         compiler_params=pltpu.CompilerParams(vmem_limit_bytes=8 << 20),
-        name="add_landed",
-    )(words, residual, *pieces)
+        name="norm_back",
+    )(inputs, grad_rows, *parts)
 
 
 def per_device(x_fwd, x_bwd, grad_out, saved_qkv, norm_gain, w_qkv, w_out):
@@ -442,29 +469,30 @@
     cores = lax.axis_size("tensor")
     replicas = lax.axis_size("dp")
     columns = weight_out.shape[1]
-    places = jnp.bitwise_xor(lax.axis_index("dp"), jnp.arange(replicas, dtype=jnp.int32)) * columns
-    words = jnp.concatenate([jnp.full((1,), lax.axis_index("tensor") * rows), places])
+    words = jnp.full((1,), lax.axis_index("tensor") * rows, jnp.int32)
+
+    def columns_of(step):
+        return jnp.bitwise_xor(lax.axis_index("dp"), step) * columns
+
     if replicas != 4:
         raise ValueError("dp size")
 
     def grad_piece(step):
-        at = jnp.bitwise_xor(lax.axis_index("dp"), step) * columns
-        return lax.dynamic_slice_in_dim(grad_rows, at, columns, axis=1)
-
-    pieces = [grad_piece(0)]
-    pieces += [over_dp(grad_piece(step), step) for step in range(1, replicas)]
-
-    normed_rows = normalize(fwd_rows, gain_row)
-    normed_far = over_dp(normed_rows, 2)
-    normed_near = over_dp(normed_rows, 1)
-    own_parts = blocks_of_cores(normed_rows)
-    own_heads, *helds = forward_heads([own_parts], weight_qkv, [], words)
-    near_parts = blocks_of_cores(normed_near)
-    far_parts = blocks_of_cores(normed_far)
-    near_heads, far_heads = forward_heads([near_parts, far_parts], None, helds, words)
+        return lax.dynamic_slice_in_dim(grad_rows, columns_of(step), columns, axis=1)
+
+    moved = [grad_piece(0)]
+    moved += [over_dp(grad_piece(step), step) for step in range(1, replicas)]
+
+    far_rows = over_dp(fwd_rows, 3)
+    near_rows = over_dp(fwd_rows, 1)
+    own_parts = blocks_of_cores(fwd_rows)
+    own_heads, *helds = forward_heads([own_parts], weight_qkv, [], words, gain_row, (1, 2))
+    near_parts = blocks_of_cores(near_rows)
+    far_parts = blocks_of_cores(far_rows)
+    near_heads, far_heads = forward_heads([near_parts, far_parts], None, helds, words, gain_row, ())
     last_heads = over_dp(far_heads, 1)
 
-    exchanged = [blocks_of_cores(piece) for piece in pieces]
+    exchanged = [blocks_of_cores(piece) for piece in moved]
     (own, *rest), held_out = head_terms(exchanged, weight_out, 1)
     landed = []
     for index in range(len(rest) // 3):
@@ -481,6 +509,7 @@
     depth = helds[0].shape[1]
     steps = width // depth
     some = steps - max(1, steps // 4)
+    some = steps - max(1, steps // 2)
     first, rest = range(some), range(some, steps)
     half = len(first) * depth
     units = range(qkv_saved.shape[1] // UNIT)
@@ -496,21 +525,26 @@
     keep, *sends = back_rest(grad_qkv, early, helds, cores, units, rest, steps)
     scaled = sum_over_cores(keep, sends) * gain_row[:, half:]
     arrived.append(over_pipe(scaled.astype(jnp.bfloat16), -1))
-    scaled = jnp.concatenate(arrived, axis=1).astype(jnp.float32)
-    grad_input = norm_back(bwd_next, grad_next, scaled)
-
-    pieces = {}
-    groups = (((0,), [own_heads]), ((1, 2), [near_heads, far_heads]), ((3,), [last_heads]))
+    grad_input = norm_back(bwd_next, grad_next, arrived)
+
+    pieces = []
+    groups = (((0,), [own_heads]), ((1, 3), [near_heads, far_heads]), ((2,), [last_heads]))
     for group, heads in groups:
         keep, *sends = project(heads, held_out, cores)
         summed = sum_over_cores(keep, sends).astype(jnp.bfloat16)
         for index, step in enumerate(group):
-            pieces[step] = lax.ppermute(
+            piece = lax.ppermute(
                 summed[index * rows : (index + 1) * rows],
                 ("pipe", "dp"),
                 cross_pairs(step, 1),
             )
-    output = add_landed(words, fwd_prev, [pieces[step] for step in range(replicas)])
+            pieces.append((step, piece))
+    output = fwd_prev
+    for step, piece in reversed(pieces):
+        at = columns_of(step)
+        part = lax.dynamic_slice_in_dim(fwd_prev, at, columns, axis=1).astype(jnp.float32)
+        part = (part + piece.astype(jnp.float32)).astype(jnp.bfloat16)
+        output = lax.dynamic_update_slice_in_dim(output, part, at, axis=1)
     return (output[None, None], grad_input[None, None])
 
 

time: 128 us -> 120 us (0.938)
  other arithmetic: 4.14 us -> 0.45 us
  starting transfers between devices: 36.7 us -> 33.5 us
  waiting for transfers between devices: 44.4 us -> 42.6 us
    ppermute x5, waiting for transfers between devices: 2.74 us -> 0.01 us  [over_pipe(): lax.ppermute(value, 'pipe', shift_pairs(lax.axis_size('pipe'), steps))]
    ppermute x4, starting transfers between devices: 8.56 us -> 6.86 us  [window(): lax.ppermute(summed[index * rows:(index + 1) * rows], ('pipe', 'dp'), cro...]
    reduce_sum x2 -> x0, other arithmetic: 1.45 us -> none  [the longest x1 1.18 us: normalize(): jnp.mean(widened * widened, axis=-1, keepdims=True) + 1e-05]
    unnamed x16 -> x19, local copies, waits for them, and re-layouts: 2.17 us -> 2.96 us
  transfers between devices with their start and end apart: 33 -> 33, of which waited for: 10 -> 10; matrix products, arithmetic and copies ran while one was open for 3% -> 0% of each run, Pallas kernels for 29% -> 32%
where the time goes in v3:
time: 120 us; the launch traced here: 119 us
  waiting for transfers between devices  42.6 us (36%)
  Pallas kernels  37.9 us (32%)
  starting transfers between devices  33.5 us (28%)
  local copies, waits for them, and re-layouts  4.05 us (3%)
    pallas_call x9, Pallas kernels, call(): pl.pallas_call(body, in_specs=specs + [REMOTE if blocks else LOCAL for _...  36.7 us
    ppermute x12, waiting for transfers between devices, over_dp(): return lax.ppermute(value, 'dp', partner_pairs(lax.axis_size('dp'), step))  34.4 us
    ppermute x12, starting transfers between devices, over_dp(): return lax.ppermute(value, 'dp', partner_pairs(lax.axis_size('dp'), step))  15.3 us
    ppermute x5, starting transfers between devices, over_pipe(): lax.ppermute(value, 'pipe', shift_pairs(lax.axis_size('pipe'), steps))  9.05 us
    ppermute x4, starting transfers between devices, window(): lax.ppermute(summed[index * rows:(index + 1) * rows], ('pipe', 'dp'), cro...  6.86 us
    ppermute x4, waiting for transfers between devices, window(): lax.ppermute(summed[index * rows:(index + 1) * rows], ('pipe', 'dp'), cro...  5.59 us
    unnamed x19, local copies, waits for them, and re-layouts  2.96 us
    ppermute x5, waiting for transfers between devices, sum_over_cores(): block = lax.ppermute(sends[step - 1], 'tensor', shift_pairs(count, step))  2.5 us
  transfers between devices with their start and end apart: 33, of which 10 were waited for; matrix products, arithmetic and copies ran while one was open for 0% of the time, Pallas kernels for 32%

profile of v3, /device:TPU:0, one launch (start us, length us, event | category | flops | bytes accessed | tf_op | source)
XLA Modules:
  0.0 119.4 jit_solution(8629831101580430612)
XLA Ops:
  1.7 4.1 %collective-permute-start.10 = (bf16[48,1024]{1,0:T(8,128)(2,1)S(1)}, bf16[48,1024]{1,0:T(8,128)(2,1)S(1)}, u32[]{:S(2)}, u32[]{:S(2)}) collective-permute-start(bf16[48,1024]{1,0:T(8,128)(2,1)S(1)} %get-tuple-element.51), channel_id=1, source_target_pairs={{0,2},{1,3},{2,0},{3,1},{4,6},{5,7},{6,4},{7,5},{8,10},{9,11},{10,... | collective-permute-start | bytes 294920 | tf_op jit(solution)/shard_map/ppermute | solution.py:37
  5.9 1.3 %collective-permute-start.12 = (bf16[48,1024]{1,0:T(8,128)(2,1)S(1)}, bf16[48,1024]{1,0:T(8,128)(2,1)S(1)}, u32[]{:S(2)}, u32[]{:S(2)}) collective-permute-start(bf16[48,1024]{1,0:T(8,128)(2,1)S(1)} %get-tuple-element.50), channel_id=1, source_target_pairs={{0,3},{1,2},{2,1},{3,0},{4,7},{5,6},{6,5},{7,4},{8,11},{9,10},{10,... | collective-permute-start | bytes 294920 | tf_op jit(solution)/shard_map/ppermute | solution.py:37
  7.5 6.3 %collective-permute-done.10.refs_4_ = bf16[48,1024]{1,0:T(8,128)(2,1)S(1)} collective-permute-done((bf16[48,1024]{1,0:T(8,128)(2,1)S(1)}, bf16[48,1024]{1,0:T(8,128)(2,1)S(1)}, u32[]{:S(2)}, u32[]{:S(2)}) %collective-permute-start.10) | collective-permute-done | bytes 98336 | tf_op jit(solution)/shard_map/ppermute | solution.py:37
  14.8 1.5 %collective-permute-start.1 = (bf16[48,4096]{1,0:T(8,128)(2,1)}, bf16[48,4096]{1,0:T(8,128)(2,1)S(1)}, u32[]{:S(2)}, u32[]{:S(2)}) collective-permute-start(bf16[48,4096]{1,0:T(8,128)(2,1)} %bitcast.44), channel_id=1, source_target_pairs={{0,1},{1,0},{2,3},{3,2},{4,5},{5,4},{6,7},{7,6},{8,9},{9,8},{10,11... | collective-permute-start | bytes 1179656 | tf_op jit(solution)/shard_map/ppermute | solution.py:37
  16.3 3.4 %collective-permute-start.3 = (bf16[48,4096]{1,0:T(8,128)(2,1)}, bf16[48,4096]{1,0:T(8,128)(2,1)S(1)}, u32[]{:S(2)}, u32[]{:S(2)}) collective-permute-start(bf16[48,4096]{1,0:T(8,128)(2,1)} %bitcast.45), channel_id=1, source_target_pairs={{0,3},{1,2},{2,1},{3,0},{4,7},{5,6},{6,5},{7,4},{8,11},{9,10},{10,... | collective-permute-start | bytes 1179656 | tf_op jit(solution)/shard_map/ppermute | solution.py:37
  19.7 1.5 %collective-permute-start = (bf16[48,4096]{1,0:T(8,128)(2,1)}, bf16[48,4096]{1,0:T(8,128)(2,1)S(1)}, u32[]{:S(2)}, u32[]{:S(2)}) collective-permute-start(bf16[48,4096]{1,0:T(8,128)(2,1)} %bitcast.46), channel_id=1, source_target_pairs={{0,8},{8,16},{16,24},{24,0},{1,9},{9,17},{17,25},{25,1},{2,10},{10... | collective-permute-start | bytes 1179656 | tf_op jit(solution)/shard_map/ppermute | solution.py:41
  21.2 4.3 %shard_map.88 = (bf16[96,2304]{1,0:T(8,128)(2,1)S(1)}, bf16[96,768]{1,0:T(8,128)(2,1)S(1)}, bf16[96,768]{1,0:T(8,128)(2,1)S(1)}, bf16[96,768]{1,0:T(8,128)(2,1)S...) custom-call(bf16[48,1024]{1,0:T(8,128)(2,1)S(1)} %get-tuple-element., ...), custom_call_target="tpu_custom_call" | custom-call | flops 1811939328 | bytes 4718592 | tf_op jit(solution)/shard_map/pallas_call | solution.py:207
  25.4 2.2 %copy-done = bf16[3,768,1024]{2,1,0:T(8,128)(2,1)} copy-done((bf16[3,768,1024]{2,1,0:T(8,128)(2,1)}, bf16[3,768,1024]{2,1,0:T(8,128)(2,1)S(1)}, u32[]{:S(2)}) %copy-start) | copy-done | bytes 4718616
  27.6 13.3 %collective-permute-done.27 = bf16[96,768]{1,0:T(8,128)(2,1)S(1)} collective-permute-done((bf16[96,768]{1,0:T(8,128)(2,1)S(1)}, bf16[96,768]{1,0:T(8,128)(2,1)S(1)}, u32[]{:S(2)}, u32[]{:S(2)}) %collective-permute-start.27) | collective-permute-done | bytes 147488 | tf_op jit(solution)/shard_map/ppermute | solution.py:37
  41.0 2.1 %collective-permute-start.26 = (bf16[96,768]{1,0:T(8,128)(2,1)S(1)}, bf16[96,768]{1,0:T(8,128)(2,1)S(1)}, u32[]{:S(2)}, u32[]{:S(2)}) collective-permute-start(bf16[96,768]{1,0:T(8,128)(2,1)S(1)} %get-tuple-element.41), channel_id=1, source_target_pairs={{0,1},{1,0},{2,3},{3,2},{4,5},{5,4},{6,7},{7,6},{8,9},{9,8},{10,11... | collective-permute-start | bytes 442376 | tf_op jit(solution)/shard_map/ppermute | solution.py:37
  43.8 10.8 %shard_map.86 = (bf16[96,2304]{1,0:T(8,128)(2,1)S(1)}, bf16[12,1024,1024]{2,1,0:T(8,128)(2,1)S(1)}) custom-call(s32[1]{0:T(128)} %bitcast.2.refs_0_, f32[1,4096]{1,0:T(1,128)} %refs_1_.3, bf16[48,4096]{1,0:T(8,128)(2,1)} %bitcast.47, bf16[48,4096]{1,0:T(8,128)(2,1)S(1)} %collective-permute-done.5.refs_3_, bf16[4096,3072]{1,0:T(8,128)(2,1)} %bitcast.39), custom_call_target="tpu_custom_call" | custom-call | flops 2415919104 | bytes 25165824 | tf_op jit(solution)/shard_map/pallas_call | solution.py:207
  56.7 1.9 %collective-permute-start.25 = (bf16[96,1536]{1,0:T(8,128)(2,1)S(1)}, bf16[96,1536]{1,0:T(8,128)(2,1)S(1)}, u32[]{:S(2)}, u32[]{:S(2)}) collective-permute-start(bf16[96,1536]{1,0:T(8,128)(2,1)S(1)} %add_convert_fusion), channel_id=1, source_target_pairs={{0,2},{1,3},{2,0},{3,1},{4,6},{5,7},{6,4},{7,5},{8,10},{9,11},{10,... | collective-permute-start | bytes 884744 | tf_op jit(solution)/shard_map/ppermute | solution.py:37
  58.6 3.9 %shard_map.92 = (bf16[96,1024]{1,0:T(8,128)(2,1)}, f32[96,4096]{1,0:T(8,128)S(1)}) custom-call(s32[1]{0:T(128)} %bitcast.2.refs_0_, bf16[96,3072]{1,0:T(8,128)(2,1)S(1)} %bitcast.37, bf16[96,2304]{1,0:T(8,128)(2,1)S(1)} %get-tuple-element.37.refs_2_, bf16[96,768]{1,0:T(8,128)(2,1)S(1)} %collective-permute-done.26.refs_3_, ...), custom_call_target="tpu_custom_call" | custom-call | flops 805306368 | tf_op jit(solution)/shard_map/pallas_call | solution.py:207
  62.5 1.9 %collective-permute-start.21 = (bf16[48,4096]{1,0:T(8,128)(2,1)S(1)}, bf16[48,4096]{1,0:T(8,128)(2,1)S(1)}, u32[]{:S(2)}, u32[]{:S(2)}) collective-permute-start(bf16[48,4096]{1,0:T(8,128)(2,1)S(1)} %bitcast.51), channel_id=1, source_target_pairs={{0,24},{8,0},{16,8},{24,16},{1,25},{9,1},{17,9},{25,17},{2,26},{10... | collective-permute-start | bytes 1179656 | tf_op jit(solution)/shard_map/ppermute | solution.py:41
  64.5 7.1 %collective-permute-done.23.refs_3_ = bf16[96,1536]{1,0:T(8,128)(2,1)S(1)} collective-permute-done((bf16[96,1536]{1,0:T(8,128)(2,1)S(1)}, bf16[96,1536]{1,0:T(8,128)(2,1)S(1)}, u32[]{:S(2)}, u32[]{:S(2)}) %collective-permute-start.23) | collective-permute-done | bytes 294944 | tf_op jit(solution)/shard_map/ppermute | solution.py:37
  71.5 2.0 %collective-permute-start.22 = (bf16[48,4096]{1,0:T(8,128)(2,1)S(1)}, bf16[48,4096]{1,0:T(8,128)(2,1)S(1)}, u32[]{:S(2)}, u32[]{:S(2)}) collective-permute-start(bf16[48,4096]{1,0:T(8,128)(2,1)S(1)} %bitcast.41), channel_id=1, source_target_pairs={{0,24},{8,0},{16,8},{24,16},{1,25},{9,1},{17,9},{25,17},{2,26},{10... | collective-permute-start | bytes 1179656 | tf_op jit(solution)/shard_map/ppermute | solution.py:41
  73.6 4.1 %shard_map.93 = (bf16[96,2048]{1,0:T(8,128)(2,1)S(1)}, bf16[48,2048]{1,0:T(8,128)(2,1)S(1)}, bf16[48,2048]{1,0:T(8,128)(2,1)S(1)}) custom-call(s32[1]{0:T(128)} %bitcast.2.refs_0_, bf16[96,3072]{1,0:T(8,128)(2,1)S(1)} %bitcast.38, bf16[96,2304]{1,0:T(8,128)(2,1)S(1)} %get-tuple-element.37.refs_2_, bf16[96,1536]{1,0:T(8,128)(2,1)S(1)} %collective-permute-done.23.refs_3_, ...), custom_call_target="tpu_custom_call" | custom-call | flops 805306368 | tf_op jit(solution)/shard_map/pallas_call | solution.py:207
  77.6 2.7 %shard_map.94 = (bf16[48,2048]{1,0:T(8,128)(2,1)S(1)}, bf16[48,2048]{1,0:T(8,128)(2,1)S(1)}) custom-call(bf16[96,2048]{1,0:T(8,128)(2,1)S(1)} %get-tuple-element.47.refs_0_, f32[96,4096]{1,0:T(8,128)S(1)} %get-tuple-element.44.refs_5_.refs_1_, bf16[12,1024,1024]{2,1,0:T(8,128)(2,1)S(1)} %get-tuple-element.26.refs_6_.refs_5_.refs_2_), custom_call_target="tpu_custom_call" | custom-call | flops 805306368 | tf_op jit(solution)/shard_map/pallas_call | solution.py:207
  80.4 7.8 %shard_map.87 = (bf16[96,2304]{1,0:T(8,128)(2,1)S(1)}, bf16[96,2304]{1,0:T(8,128)(2,1)S(1)}) custom-call(s32[1]{0:T(128)} %bitcast.2.refs_0_, f32[1,4096]{1,0:T(1,128)S(1)} %copy-done.3, bf16[48,4096]{1,0:T(8,128)(2,1)S(1)} %collective-permute-done.1.refs_2_, bf16[48,4096]{1,0:T(8,128)(2,1)S(1)} %collective-permute-done.2.refs_3_, ...), custom_call_target="tpu_custom_call" | custom-call | flops 4831838208 | tf_op jit(solution)/shard_map/pallas_call | solution.py:207
  88.4 1.3 %shard_map.90 = (bf16[96,1024]{1,0:T(8,128)(2,1)S(1)}, bf16[96,1024]{1,0:T(8,128)(2,1)S(1)}) custom-call(bf16[96,2304]{1,0:T(8,128)(2,1)S(1)} %get-tuple-element.31.refs_0_, bf16[96,2304]{1,0:T(8,128)(2,1)S(1)} %get-tuple-element.27.refs_1_, bf16[3,768,1024]{2,1,0:T(8,128)(2,1)S(1)} %bitcast.36), custom_call_target="tpu_custom_call" | custom-call | flops 905969664 | tf_op jit(solution)/shard_map/pallas_call | solution.py:207
  90.4 1.3 %collective-permute-done.29 = bf16[48,2048]{1,0:T(8,128)(2,1)S(1)} collective-permute-done((bf16[48,2048]{1,0:T(8,128)(2,1)S(1)}, bf16[48,2048]{1,0:T(8,128)(2,1)S(1)}, u32[]{:S(2)}, u32[]{:S(2)}) %collective-permute-start.29) | collective-permute-done | bytes 196640 | tf_op jit(solution)/shard_map/ppermute | solution.py:55
  91.6 1.9 %collective-permute-start.32 = (bf16[48,2048]{1,0:T(8,128)(2,1)S(1)}, bf16[48,2048]{1,0:T(8,128)(2,1)S(1)}, u32[]{:S(2)}, u32[]{:S(2)}) collective-permute-start(bf16[48,2048]{1,0:T(8,128)(2,1)S(1)} %multiply_convert_fusion), channel_id=1, source_target_pairs={{0,24},{8,0},{16,8},{24,16},{1,25},{9,1},{17,9},{25,17},{2,26},{10... | collective-permute-start | bytes 589832 | tf_op jit(solution)/shard_map/ppermute | solution.py:41
  93.6 7.2 %collective-permute-done.6.refs_0_ = bf16[96,2304]{1,0:T(8,128)(2,1)S(1)} collective-permute-done((bf16[96,2304]{1,0:T(8,128)(2,1)S(1)}, bf16[96,2304]{1,0:T(8,128)(2,1)S(1)}, u32[]{:S(2)}, u32[]{:S(2)}) %collective-permute-start.6) | collective-permute-done | bytes 442400 | tf_op jit(solution)/shard_map/ppermute | solution.py:37
  100.8 1.7 %collective-permute-start.30 = (bf16[48,2048]{1,0:T(8,128)(2,1)S(1)}, bf16[48,2048]{1,0:T(8,128)(2,1)S(1)}, u32[]{:S(2)}, u32[]{:S(2)}) collective-permute-start(bf16[48,2048]{1,0:T(8,128)(2,1)S(1)} %multiply_convert_fusion.1), channel_id=1, source_target_pairs={{0,24},{8,0},{16,8},{24,16},{1,25},{9,1},{17,9},{25,17},{2,26},{10... | collective-permute-start | bytes 589832 | tf_op jit(solution)/shard_map/ppermute | solution.py:41
  103.6 1.2 %collective-permute-done.14 = bf16[48,1024]{1,0:T(8,128)(2,1)S(1)} collective-permute-done((bf16[48,1024]{1,0:T(8,128)(2,1)S(1)}, bf16[48,1024]{1,0:T(8,128)(2,1)S(1)}, u32[]{:S(2)}, u32[]{:S(2)}) %collective-permute-start.14) | collective-permute-done | bytes 98336 | tf_op jit(solution)/shard_map/ppermute | solution.py:55
  104.8 1.3 %collective-permute-start.15 = (bf16[48,1024]{1,0:T(8,128)(2,1)S(1)}, bf16[48,1024]{1,0:T(8,128)(2,1)S(1)}, u32[]{:S(2)}, u32[]{:S(2)}) collective-permute-start(bf16[48,1024]{1,0:T(8,128)(2,1)S(1)} %add_convert_fusion.8), channel_id=1, source_target_pairs={{0,10},{1,11},{2,8},{3,9},{8,18},{9,19},{10,16},{11,17},{16,26},{1... | collective-permute-start | bytes 294920 | tf_op jit(solution)/shard_map/ppermute | solution.py:536
  106.2 2.4 %collective-permute-start.20 = (bf16[48,1024]{1,0:T(8,128)(2,1)S(1)}, bf16[48,1024]{1,0:T(8,128)(2,1)S(1)}, u32[]{:S(2)}, u32[]{:S(2)}) collective-permute-start(bf16[48,1024]{1,0:T(8,128)(2,1)S(1)} %add_convert_fusion.4), channel_id=1, source_target_pairs={{0,8},{1,9},{2,10},{3,11},{8,16},{9,17},{10,18},{11,19},{16,24},{1... | collective-permute-start | bytes 294920 | tf_op jit(solution)/shard_map/ppermute | solution.py:536
  108.6 1.2 %collective-permute-start.17 = (bf16[48,1024]{1,0:T(8,128)(2,1)S(1)}, bf16[48,1024]{1,0:T(8,128)(2,1)S(1)}, u32[]{:S(2)}, u32[]{:S(2)}) collective-permute-start(bf16[48,1024]{1,0:T(8,128)(2,1)S(1)} %get-tuple-element.55), channel_id=1, source_target_pairs={{0,11},{1,10},{2,9},{3,8},{8,19},{9,18},{10,17},{11,16},{16,27},{1... | collective-permute-start | bytes 294920 | tf_op jit(solution)/shard_map/ppermute | solution.py:536
  109.8 1.9 %collective-permute-start.18 = (bf16[48,1024]{1,0:T(8,128)(2,1)S(1)}, bf16[48,1024]{1,0:T(8,128)(2,1)S(1)}, u32[]{:S(2)}, u32[]{:S(2)}) collective-permute-start(bf16[48,1024]{1,0:T(8,128)(2,1)S(1)} %get-tuple-element.54), channel_id=1, source_target_pairs={{0,9},{1,8},{2,11},{3,10},{8,17},{9,16},{10,19},{11,18},{16,25},{1... | collective-permute-start | bytes 294920 | tf_op jit(solution)/shard_map/ppermute | solution.py:536
  111.7 1.2 norm_back.1
  112.9 1.5 %collective-permute-done.15 = bf16[48,1024]{1,0:T(8,128)(2,1)S(1)} collective-permute-done((bf16[48,1024]{1,0:T(8,128)(2,1)S(1)}, bf16[48,1024]{1,0:T(8,128)(2,1)S(1)}, u32[]{:S(2)}, u32[]{:S(2)}) %collective-permute-start.15) | collective-permute-done | bytes 98336 | tf_op jit(solution)/shard_map/ppermute | solution.py:536
  114.5 3.2 %collective-permute-done.17 = bf16[48,1024]{1,0:T(8,128)(2,1)S(1)} collective-permute-done((bf16[48,1024]{1,0:T(8,128)(2,1)S(1)}, bf16[48,1024]{1,0:T(8,128)(2,1)S(1)}, u32[]{:S(2)}, u32[]{:S(2)}) %collective-permute-start.17) | collective-permute-done | bytes 98336 | tf_op jit(solution)/shard_map/ppermute | solution.py:536
  (78 shorter events, 8.9 us)
Async XLA Ops:
  1.7 12.0 %collective-permute-start.10 = (bf16[48,1024]{1,0:T(8,128)(2,1)S(1)}, bf16[48,1024]{1,0:T(8,128)(2,1)S(1)}, u32[]{:S(2)}, u32[]{:S(2)}) collective-permute-start(bf16[48,1024]{1,0:T(8,128)(2,1)S(1)} %get-tuple-element.51), channel_id=1, source_target_pairs={{0,2},{1,3},{2,0},{3,1},{4,6},{5,7},{6,4},{7,5},{8,10},{9,11},{10,... | collective-permute-start | bytes 294920 | tf_op jit(solution)/shard_map/ppermute | solution.py:37
  5.9 7.9 %collective-permute-start.12 = (bf16[48,1024]{1,0:T(8,128)(2,1)S(1)}, bf16[48,1024]{1,0:T(8,128)(2,1)S(1)}, u32[]{:S(2)}, u32[]{:S(2)}) collective-permute-start(bf16[48,1024]{1,0:T(8,128)(2,1)S(1)} %get-tuple-element.50), channel_id=1, source_target_pairs={{0,3},{1,2},{2,1},{3,0},{4,7},{5,6},{6,5},{7,4},{8,11},{9,10},{10,... | collective-permute-start | bytes 294920 | tf_op jit(solution)/shard_map/ppermute | solution.py:37
  7.2 7.1 %collective-permute-start.8 = (bf16[48,1024]{1,0:T(8,128)(2,1)S(1)}, bf16[48,1024]{1,0:T(8,128)(2,1)S(1)}, u32[]{:S(2)}, u32[]{:S(2)}) collective-permute-start(bf16[48,1024]{1,0:T(8,128)(2,1)S(1)} %get-tuple-element.52), channel_id=1, source_target_pairs={{0,1},{1,0},{2,3},{3,2},{4,5},{5,4},{6,7},{7,6},{8,9},{9,8},{10,11... | collective-permute-start | bytes 294920 | tf_op jit(solution)/shard_map/ppermute | solution.py:37
  7.5 7.4 %collective-permute-start.7 = (bf16[48,1024]{1,0:T(8,128)(2,1)S(1)}, bf16[48,1024]{1,0:T(8,128)(2,1)S(1)}, u32[]{:S(2)}, u32[]{:S(2)}) collective-permute-start(bf16[48,1024]{1,0:T(8,128)(2,1)S(1)} %get-tuple-element.53.refs_0_), channel_id=1, source_target_pairs={{0,4},{4,0},{1,5},{5,1},{2,6},{6,2},{3,7},{7,3},{8,12},{12,8},{9,1... | collective-permute-start | bytes 294920 | tf_op jit(solution)/shard_map/ppermute | solution.py:47
  13.8 2.5 %collective-permute-start.11 = (bf16[48,1024]{1,0:T(8,128)(2,1)S(1)}, bf16[48,1024]{1,0:T(8,128)(2,1)S(1)}, u32[]{:S(2)}, u32[]{:S(2)}) collective-permute-start(bf16[48,1024]{1,0:T(8,128)(2,1)S(1)} %collective-permute-done.10.refs_4_), channel_id=1, source_target_pairs={{0,4},{4,0},{1,5},{5,1},{2,6},{6,2},{3,7},{7,3},{8,12},{12,8},{9,1... | collective-permute-start | bytes 294920 | tf_op jit(solution)/shard_map/ppermute | solution.py:47
  13.8 5.9 %collective-permute-start.13 = (bf16[48,1024]{1,0:T(8,128)(2,1)S(1)}, bf16[48,1024]{1,0:T(8,128)(2,1)S(1)}, u32[]{:S(2)}, u32[]{:S(2)}) collective-permute-start(bf16[48,1024]{1,0:T(8,128)(2,1)S(1)} %collective-permute-done.12.refs_6_), channel_id=1, source_target_pairs={{0,4},{4,0},{1,5},{5,1},{2,6},{6,2},{3,7},{7,3},{8,12},{12,8},{9,1... | collective-permute-start | bytes 294920 | tf_op jit(solution)/shard_map/ppermute | solution.py:47
  14.3 6.9 %collective-permute-start.9 = (bf16[48,1024]{1,0:T(8,128)(2,1)S(1)}, bf16[48,1024]{1,0:T(8,128)(2,1)S(1)}, u32[]{:S(2)}, u32[]{:S(2)}) collective-permute-start(bf16[48,1024]{1,0:T(8,128)(2,1)S(1)} %collective-permute-done.8.refs_2_), channel_id=1, source_target_pairs={{0,4},{4,0},{1,5},{5,1},{2,6},{6,2},{3,7},{7,3},{8,12},{12,8},{9,1... | collective-permute-start | bytes 294920 | tf_op jit(solution)/shard_map/ppermute | solution.py:47
  14.4 28.8 %collective-permute-start.5 = (bf16[48,4096]{1,0:T(8,128)(2,1)}, bf16[48,4096]{1,0:T(8,128)(2,1)S(1)}, u32[]{:S(2)}, u32[]{:S(2)}) collective-permute-start(bf16[48,4096]{1,0:T(8,128)(2,1)} %bitcast.43), channel_id=1, source_target_pairs={{0,4},{4,0},{1,5},{5,1},{2,6},{6,2},{3,7},{7,3},{8,12},{12,8},{9,1... | collective-permute-start | bytes 1179656 | tf_op jit(solution)/shard_map/ppermute | solution.py:47
  14.8 41.4 %collective-permute-start.1 = (bf16[48,4096]{1,0:T(8,128)(2,1)}, bf16[48,4096]{1,0:T(8,128)(2,1)S(1)}, u32[]{:S(2)}, u32[]{:S(2)}) collective-permute-start(bf16[48,4096]{1,0:T(8,128)(2,1)} %bitcast.44), channel_id=1, source_target_pairs={{0,1},{1,0},{2,3},{3,2},{4,5},{5,4},{6,7},{7,6},{8,9},{9,8},{10,11... | collective-permute-start | bytes 1179656 | tf_op jit(solution)/shard_map/ppermute | solution.py:37
  16.3 40.1 %collective-permute-start.3 = (bf16[48,4096]{1,0:T(8,128)(2,1)}, bf16[48,4096]{1,0:T(8,128)(2,1)S(1)}, u32[]{:S(2)}, u32[]{:S(2)}) collective-permute-start(bf16[48,4096]{1,0:T(8,128)(2,1)} %bitcast.45), channel_id=1, source_target_pairs={{0,3},{1,2},{2,1},{3,0},{4,7},{5,6},{6,5},{7,4},{8,11},{9,10},{10,... | collective-permute-start | bytes 1179656 | tf_op jit(solution)/shard_map/ppermute | solution.py:37
  19.7 21.3 %collective-permute-start = (bf16[48,4096]{1,0:T(8,128)(2,1)}, bf16[48,4096]{1,0:T(8,128)(2,1)S(1)}, u32[]{:S(2)}, u32[]{:S(2)}) collective-permute-start(bf16[48,4096]{1,0:T(8,128)(2,1)} %bitcast.46), channel_id=1, source_target_pairs={{0,8},{8,16},{16,24},{24,0},{1,9},{9,17},{17,25},{25,1},{2,10},{10... | collective-permute-start | bytes 1179656 | tf_op jit(solution)/shard_map/ppermute | solution.py:41
  27.6 13.4 %collective-permute-start.27 = (bf16[96,768]{1,0:T(8,128)(2,1)S(1)}, bf16[96,768]{1,0:T(8,128)(2,1)S(1)}, u32[]{:S(2)}, u32[]{:S(2)}) collective-permute-start(bf16[96,768]{1,0:T(8,128)(2,1)S(1)} %get-tuple-element.43), channel_id=1, source_target_pairs={{0,1},{1,0},{2,3},{3,2},{4,5},{5,4},{6,7},{7,6},{8,9},{9,8},{10,11... | collective-permute-start | bytes 442376 | tf_op jit(solution)/shard_map/ppermute | solution.py:37
  41.0 14.6 %collective-permute-start.24 = (bf16[96,1536]{1,0:T(8,128)(2,1)S(1)}, bf16[96,1536]{1,0:T(8,128)(2,1)S(1)}, u32[]{:S(2)}, u32[]{:S(2)}) collective-permute-start(bf16[96,1536]{1,0:T(8,128)(2,1)S(1)} %get-tuple-element.40), channel_id=1, source_target_pairs={{0,1},{1,0},{2,3},{3,2},{4,5},{5,4},{6,7},{7,6},{8,9},{9,8},{10,11... | collective-permute-start | bytes 884744 | tf_op jit(solution)/shard_map/ppermute | solution.py:37
  41.0 15.2 %collective-permute-start.26 = (bf16[96,768]{1,0:T(8,128)(2,1)S(1)}, bf16[96,768]{1,0:T(8,128)(2,1)S(1)}, u32[]{:S(2)}, u32[]{:S(2)}) collective-permute-start(bf16[96,768]{1,0:T(8,128)(2,1)S(1)} %get-tuple-element.41), channel_id=1, source_target_pairs={{0,1},{1,0},{2,3},{3,2},{4,5},{5,4},{6,7},{7,6},{8,9},{9,8},{10,11... | collective-permute-start | bytes 442376 | tf_op jit(solution)/shard_map/ppermute | solution.py:37
  43.1 13.6 %collective-permute-start.28 = (bf16[96,768]{1,0:T(8,128)(2,1)S(1)}, bf16[96,768]{1,0:T(8,128)(2,1)S(1)}, u32[]{:S(2)}, u32[]{:S(2)}) collective-permute-start(bf16[96,768]{1,0:T(8,128)(2,1)S(1)} %add_convert_fusion.2), channel_id=1, source_target_pairs={{0,2},{1,3},{2,0},{3,1},{4,6},{5,7},{6,4},{7,5},{8,10},{9,11},{10,... | collective-permute-start | bytes 442376 | tf_op jit(solution)/shard_map/ppermute | solution.py:37
  55.6 6.9 %collective-permute-start.19 = (bf16[48,1024]{1,0:T(8,128)(2,1)S(1)}, bf16[48,1024]{1,0:T(8,128)(2,1)S(1)}, u32[]{:S(2)}, u32[]{:S(2)}) collective-permute-start(bf16[48,1024]{1,0:T(8,128)(2,1)S(1)} %get-tuple-element.36), channel_id=1, source_target_pairs={{0,4},{4,0},{1,5},{5,1},{2,6},{6,2},{3,7},{7,3},{8,12},{12,8},{9,1... | collective-permute-start | bytes 294920 | tf_op jit(solution)/shard_map/ppermute | solution.py:55
  56.2 15.3 %collective-permute-start.23 = (bf16[96,1536]{1,0:T(8,128)(2,1)S(1)}, bf16[96,1536]{1,0:T(8,128)(2,1)S(1)}, u32[]{:S(2)}, u32[]{:S(2)}) collective-permute-start(bf16[96,1536]{1,0:T(8,128)(2,1)S(1)} %get-tuple-element.38), channel_id=1, source_target_pairs={{0,1},{1,0},{2,3},{3,2},{4,5},{5,4},{6,7},{7,6},{8,9},{9,8},{10,11... | collective-permute-start | bytes 884744 | tf_op jit(solution)/shard_map/ppermute | solution.py:37
  56.2 24.2 %collective-permute-start.2 = (bf16[48,4096]{1,0:T(8,128)(2,1)S(1)}, bf16[48,4096]{1,0:T(8,128)(2,1)S(1)}, u32[]{:S(2)}, u32[]{:S(2)}) collective-permute-start(bf16[48,4096]{1,0:T(8,128)(2,1)S(1)} %collective-permute-done.1.refs_2_), channel_id=1, source_target_pairs={{0,4},{4,0},{1,5},{5,1},{2,6},{6,2},{3,7},{7,3},{8,12},{12,8},{9,1... | collective-permute-start | bytes 1179656 | tf_op jit(solution)/shard_map/ppermute | solution.py:47
  56.4 24.0 %collective-permute-start.4 = (bf16[48,4096]{1,0:T(8,128)(2,1)S(1)}, bf16[48,4096]{1,0:T(8,128)(2,1)S(1)}, u32[]{:S(2)}, u32[]{:S(2)}) collective-permute-start(bf16[48,4096]{1,0:T(8,128)(2,1)S(1)} %collective-permute-done.3.refs_4_), channel_id=1, source_target_pairs={{0,4},{4,0},{1,5},{5,1},{2,6},{6,2},{3,7},{7,3},{8,12},{12,8},{9,1... | collective-permute-start | bytes 1179656 | tf_op jit(solution)/shard_map/ppermute | solution.py:47
  56.7 16.8 %collective-permute-start.25 = (bf16[96,1536]{1,0:T(8,128)(2,1)S(1)}, bf16[96,1536]{1,0:T(8,128)(2,1)S(1)}, u32[]{:S(2)}, u32[]{:S(2)}) collective-permute-start(bf16[96,1536]{1,0:T(8,128)(2,1)S(1)} %add_convert_fusion), channel_id=1, source_target_pairs={{0,2},{1,3},{2,0},{3,1},{4,6},{5,7},{6,4},{7,5},{8,10},{9,11},{10,... | collective-permute-start | bytes 884744 | tf_op jit(solution)/shard_map/ppermute | solution.py:37
  62.5 43.7 %collective-permute-start.21 = (bf16[48,4096]{1,0:T(8,128)(2,1)S(1)}, bf16[48,4096]{1,0:T(8,128)(2,1)S(1)}, u32[]{:S(2)}, u32[]{:S(2)}) collective-permute-start(bf16[48,4096]{1,0:T(8,128)(2,1)S(1)} %bitcast.51), channel_id=1, source_target_pairs={{0,24},{8,0},{16,8},{24,16},{1,25},{9,1},{17,9},{25,17},{2,26},{10... | collective-permute-start | bytes 1179656 | tf_op jit(solution)/shard_map/ppermute | solution.py:41
  71.5 37.1 %collective-permute-start.22 = (bf16[48,4096]{1,0:T(8,128)(2,1)S(1)}, bf16[48,4096]{1,0:T(8,128)(2,1)S(1)}, u32[]{:S(2)}, u32[]{:S(2)}) collective-permute-start(bf16[48,4096]{1,0:T(8,128)(2,1)S(1)} %bitcast.41), channel_id=1, source_target_pairs={{0,24},{8,0},{16,8},{24,16},{1,25},{9,1},{17,9},{25,17},{2,26},{10... | collective-permute-start | bytes 1179656 | tf_op jit(solution)/shard_map/ppermute | solution.py:41
  80.3 9.9 %collective-permute-start.31 = (bf16[48,2048]{1,0:T(8,128)(2,1)S(1)}, bf16[48,2048]{1,0:T(8,128)(2,1)S(1)}, u32[]{:S(2)}, u32[]{:S(2)}) collective-permute-start(bf16[48,2048]{1,0:T(8,128)(2,1)S(1)} %get-tuple-element.49), channel_id=1, source_target_pairs={{0,4},{4,0},{1,5},{5,1},{2,6},{6,2},{3,7},{7,3},{8,12},{12,8},{9,1... | collective-permute-start | bytes 589832 | tf_op jit(solution)/shard_map/ppermute | solution.py:55
  88.2 12.6 %collective-permute-start.6 = (bf16[96,2304]{1,0:T(8,128)(2,1)S(1)}, bf16[96,2304]{1,0:T(8,128)(2,1)S(1)}, u32[]{:S(2)}, u32[]{:S(2)}) collective-permute-start(bf16[96,2304]{1,0:T(8,128)(2,1)S(1)} %get-tuple-element.27.refs_1_), channel_id=1, source_target_pairs={{0,1},{1,0},{2,3},{3,2},{4,5},{5,4},{6,7},{7,6},{8,9},{9,8},{10,11... | collective-permute-start | bytes 1327112 | tf_op jit(solution)/shard_map/ppermute | solution.py:37
  89.7 13.7 %collective-permute-start.16 = (bf16[96,1024]{1,0:T(8,128)(2,1)S(1)}, bf16[96,1024]{1,0:T(8,128)(2,1)S(1)}, u32[]{:S(2)}, u32[]{:S(2)}) collective-permute-start(bf16[96,1024]{1,0:T(8,128)(2,1)S(1)} %get-tuple-element.33), channel_id=1, source_target_pairs={{0,4},{4,0},{1,5},{5,1},{2,6},{6,2},{3,7},{7,3},{8,12},{12,8},{9,1... | collective-permute-start | bytes 589832 | tf_op jit(solution)/shard_map/ppermute | solution.py:55
  90.2 1.4 %collective-permute-start.29 = (bf16[48,2048]{1,0:T(8,128)(2,1)S(1)}, bf16[48,2048]{1,0:T(8,128)(2,1)S(1)}, u32[]{:S(2)}, u32[]{:S(2)}) collective-permute-start(bf16[48,2048]{1,0:T(8,128)(2,1)S(1)} %get-tuple-element.46), channel_id=1, source_target_pairs={{0,4},{4,0},{1,5},{5,1},{2,6},{6,2},{3,7},{7,3},{8,12},{12,8},{9,1... | collective-permute-start | bytes 589832 | tf_op jit(solution)/shard_map/ppermute | solution.py:55
  91.6 18.2 %collective-permute-start.32 = (bf16[48,2048]{1,0:T(8,128)(2,1)S(1)}, bf16[48,2048]{1,0:T(8,128)(2,1)S(1)}, u32[]{:S(2)}, u32[]{:S(2)}) collective-permute-start(bf16[48,2048]{1,0:T(8,128)(2,1)S(1)} %multiply_convert_fusion), channel_id=1, source_target_pairs={{0,24},{8,0},{16,8},{24,16},{1,25},{9,1},{17,9},{25,17},{2,26},{10... | collective-permute-start | bytes 589832 | tf_op jit(solution)/shard_map/ppermute | solution.py:41
  100.8 10.9 %collective-permute-start.30 = (bf16[48,2048]{1,0:T(8,128)(2,1)S(1)}, bf16[48,2048]{1,0:T(8,128)(2,1)S(1)}, u32[]{:S(2)}, u32[]{:S(2)}) collective-permute-start(bf16[48,2048]{1,0:T(8,128)(2,1)S(1)} %multiply_convert_fusion.1), channel_id=1, source_target_pairs={{0,24},{8,0},{16,8},{24,16},{1,25},{9,1},{17,9},{25,17},{2,26},{10... | collective-permute-start | bytes 589832 | tf_op jit(solution)/shard_map/ppermute | solution.py:41
  104.8 9.6 %collective-permute-start.15 = (bf16[48,1024]{1,0:T(8,128)(2,1)S(1)}, bf16[48,1024]{1,0:T(8,128)(2,1)S(1)}, u32[]{:S(2)}, u32[]{:S(2)}) collective-permute-start(bf16[48,1024]{1,0:T(8,128)(2,1)S(1)} %add_convert_fusion.8), channel_id=1, source_target_pairs={{0,10},{1,11},{2,8},{3,9},{8,18},{9,19},{10,16},{11,17},{16,26},{1... | collective-permute-start | bytes 294920 | tf_op jit(solution)/shard_map/ppermute | solution.py:536
  106.2 12.4 %collective-permute-start.20 = (bf16[48,1024]{1,0:T(8,128)(2,1)S(1)}, bf16[48,1024]{1,0:T(8,128)(2,1)S(1)}, u32[]{:S(2)}, u32[]{:S(2)}) collective-permute-start(bf16[48,1024]{1,0:T(8,128)(2,1)S(1)} %add_convert_fusion.4), channel_id=1, source_target_pairs={{0,8},{1,9},{2,10},{3,11},{8,16},{9,17},{10,18},{11,19},{16,24},{1... | collective-permute-start | bytes 294920 | tf_op jit(solution)/shard_map/ppermute | solution.py:536
  108.6 9.0 %collective-permute-start.17 = (bf16[48,1024]{1,0:T(8,128)(2,1)S(1)}, bf16[48,1024]{1,0:T(8,128)(2,1)S(1)}, u32[]{:S(2)}, u32[]{:S(2)}) collective-permute-start(bf16[48,1024]{1,0:T(8,128)(2,1)S(1)} %get-tuple-element.55), channel_id=1, source_target_pairs={{0,11},{1,10},{2,9},{3,8},{8,19},{9,18},{10,17},{11,16},{16,27},{1... | collective-permute-start | bytes 294920 | tf_op jit(solution)/shard_map/ppermute | solution.py:536
  109.8 8.7 %collective-permute-start.18 = (bf16[48,1024]{1,0:T(8,128)(2,1)S(1)}, bf16[48,1024]{1,0:T(8,128)(2,1)S(1)}, u32[]{:S(2)}, u32[]{:S(2)}) collective-permute-start(bf16[48,1024]{1,0:T(8,128)(2,1)S(1)} %get-tuple-element.54), channel_id=1, source_target_pairs={{0,9},{1,8},{2,11},{3,10},{8,17},{9,16},{10,19},{11,18},{16,25},{1... | collective-permute-start | bytes 294920 | tf_op jit(solution)/shard_map/ppermute | solution.py:536
  (10 other events, 77.3 us)

commit v4 on v3

--- a/solution.py
+++ b/solution.py
@@ -84,12 +84,12 @@
 
 def probabilities(queries, keys, masked):
     length = keys.shape[0]
-    scores = mxu(queries, keys, 1, 1) * (1.0 / math.sqrt(HD))
+    scores = mxu(queries, keys, 1, 1) * (math.log2(math.e) / math.sqrt(HD))
     rows = []
     for g in range(GROUP):
         part = jnp.where(masked, -1e30, scores[g * length : (g + 1) * length])
-        part = jnp.exp(part - jnp.max(part, axis=-1, keepdims=True))
-        rows.append(part / jnp.sum(part, axis=-1, keepdims=True))
+        part = jnp.exp2(part - jnp.max(part, axis=-1, keepdims=True))
+        rows.append(part * (1.0 / jnp.sum(part, axis=-1, keepdims=True)))
     return jnp.concatenate(rows, axis=0)
 
 
@@ -102,13 +102,12 @@
         out_ref[:, at + g * HD : at + (g + 1) * HD] = heads[g * length : (g + 1) * length]
 
 
-def attend_back_unit(qkv, grads, masked, out_ref, at):
+def attend_back_unit(qkv, grads, probs, out_ref, at):
     length = qkv.shape[0]
     factor = 1.0 / math.sqrt(HD)
     keys, values = head_columns(qkv, GROUP), head_columns(qkv, GROUP + 1)
     queries = stacked_heads(qkv)
     grads = stacked_heads(grads)
-    probs = probabilities(queries, keys, masked)
     grad_values = mxu(probs.astype(jnp.bfloat16), grads, 0, 0)
     grad_probs = mxu(grads, values, 1, 1)
     grad_scores = probs * (grad_probs - jnp.sum(probs * grad_probs, axis=-1, keepdims=True))
@@ -190,7 +189,7 @@
             out_shape.append(pltpu.VMEM(shape, jnp.bfloat16))
         else:
             scratch.insert(0, pltpu.VMEM(shape, jnp.bfloat16))
-        weights = [pltpu.with_memory_space_constraint(weight, pltpu.HBM)]
+        weights = [pltpu.with_memory_space_constraint(weight, pltpu.HBM) if fetch else weight]
     else:
         weights = [pltpu.with_memory_space_constraint(held, pltpu.VMEM) for held in helds]
     if fetch:
@@ -229,18 +228,27 @@
         out_ref[first + at : first + at + step] = normed
 
 
-def forward_heads(batches, weight, helds, start, gain, fetch):
+def forward_heads(batches, weight, helds, start, gain, saved):
     rows, width = batches[0][0].shape
-    length = rows * len(batches[0])
+    cores = len(batches[0])
+    length = rows * cores
+    wide = GROUP * length
     flat = [part for parts in batches for part in parts]
     depth = divisor(width, 1024)
     steps = width // depth
     units = sum(held.shape[0] for held in helds) // steps if helds else weight.shape[1] // UNIT
 
     def kernel(ins, outs, block, normed_ref):
-        for index, ref in enumerate(ins[2:]):
+        for index, ref in enumerate(ins[2 : 2 + len(flat)]):
             normalize_rows(ref, ins[1], normed_ref, index * rows)
         masked = later_keys(length, ins[0][0])
+        if saved is not None:
+            rolled = rolled_rows(ins[-1], ins[0][0], cores)
+            for unit in range(units):
+                qkv = rolled(slice(unit * UNIT, (unit + 1) * UNIT))
+                outs[-1][unit * wide : (unit + 1) * wide] = probabilities(
+                    stacked_heads(qkv), head_columns(qkv, GROUP), masked
+                )
         for unit in range(units):
             total = None
             for step in range(steps):
@@ -248,9 +256,9 @@
                 product = mxu(left, block(unit * steps + step), 1, 0)
                 total = product if total is None else total + product
             total = total.astype(jnp.bfloat16)
-            for index, out_ref in enumerate(outs):
+            for index in range(len(batches)):
                 qkv = total[index * length : (index + 1) * length]
-                attend_unit(qkv, masked, out_ref, unit * GROUP * HD)
+                attend_unit(qkv, masked, outs[index], unit * GROUP * HD)
 
     blocks = []
     if not helds:
@@ -263,6 +271,11 @@
     outs = [(length, units * GROUP * HD) for _ in batches]
     temps = [pltpu.VMEM((length * len(batches), width), jnp.bfloat16)]
     args = [start, gain] + flat
+    fetch = ()
+    if saved is not None:
+        args.append(saved)
+        fetch = (1, 2, len(args) - 1)
+        outs.append(jax.ShapeDtypeStruct((units * wide, length), jnp.float32))
     keep = not helds
     return call(kernel, args, weight, helds, outs, blocks, keep, flops, temps, fetch)
 
@@ -334,8 +347,8 @@
     return lambda columns: jnp.concatenate([ref[part, columns] for part in ranges], axis=0)
 
 
-def back_units(start_ref, qkv_ref, own_ref, landed, grad_ref, units, cores):
-    masked = later_keys(qkv_ref.shape[0], start_ref[0])
+def back_units(start_ref, qkv_ref, probs_ref, own_ref, landed, grad_ref, units, cores):
+    high = GROUP * qkv_ref.shape[0]
     saved = rolled_rows(qkv_ref, start_ref[0], cores)
     wide = GROUP * HD
     for place, unit in enumerate(units):
@@ -345,7 +358,7 @@
         attend_back_unit(
             saved(slice(unit * UNIT, (unit + 1) * UNIT)),
             grads.astype(jnp.bfloat16),
-            masked,
+            probs_ref[unit * high : (unit + 1) * high],
             grad_ref,
             place * UNIT,
         )
@@ -360,12 +373,12 @@
     return total
 
 
-def back_early(qkv, own, landed, helds, start, cores, units, steps):
+def back_early(qkv, probs, own, landed, helds, start, cores, units, steps):
     length = qkv.shape[0]
     depth = helds[0].shape[1]
 
     def kernel(ins, outs, block):
-        back_units(ins[0], ins[1], ins[2], ins[3:], outs[0], units, cores)
+        back_units(*ins[:4], ins[4:], outs[0], units, cores)
         for step in range(steps):
             outs[1][:, step * depth : (step + 1) * depth] = back_product(
                 outs[0], block, units, step, steps
@@ -374,7 +387,7 @@
     wide = len(units) * UNIT
     outs = [(length, wide), jax.ShapeDtypeStruct((length, steps * depth), jnp.float32)]
     flops = 2 * length * wide * steps * depth
-    args = [start, qkv, own] + landed
+    args = [start, qkv, probs, own] + landed
     return call(kernel, args, None, helds, outs, [], False, flops)[1]
 
 
@@ -391,21 +404,21 @@
             ]
 
 
-def back_first(qkv, own, landed, early, helds, start, cores, units, picked, steps):
+def back_first(qkv, probs, own, landed, early, helds, start, cores, units, picked, steps):
     length = qkv.shape[0]
     rows = length // cores
     depth = helds[0].shape[1]
-    count = 3 + len(landed)
+    count = 4 + len(landed)
 
     def kernel(ins, outs, block):
-        back_units(ins[0], ins[1], ins[2], ins[3:count], outs[0], units, cores)
+        back_units(*ins[:4], ins[4:count], outs[0], units, cores)
         back_columns(outs[0], ins[count:], outs[1:], block, units, picked, steps, depth)
 
     wide = len(units) * UNIT
     columns = len(picked) * depth
     outs = [(length, wide)] + [(rows, columns) for _ in range(cores)]
     flops = 2 * length * wide * columns
-    args = [start, qkv, own] + landed + early
+    args = [start, qkv, probs, own] + landed + early
     results = call(kernel, args, None, helds, outs, [], False, flops)
     return results[0], results[1:]
 
@@ -486,10 +499,14 @@
     far_rows = over_dp(fwd_rows, 3)
     near_rows = over_dp(fwd_rows, 1)
     own_parts = blocks_of_cores(fwd_rows)
-    own_heads, *helds = forward_heads([own_parts], weight_qkv, [], words, gain_row, (1, 2))
+    own_heads, probs, *helds = forward_heads(
+        [own_parts], weight_qkv, [], words, gain_row, qkv_saved
+    )
     near_parts = blocks_of_cores(near_rows)
     far_parts = blocks_of_cores(far_rows)
-    near_heads, far_heads = forward_heads([near_parts, far_parts], None, helds, words, gain_row, ())
+    near_heads, far_heads = forward_heads(
+        [near_parts, far_parts], None, helds, words, gain_row, None
+    )
     last_heads = over_dp(far_heads, 1)
 
     exchanged = [blocks_of_cores(piece) for piece in moved]
@@ -510,16 +527,17 @@
     steps = width // depth
     some = steps - max(1, steps // 4)
     some = steps - max(1, steps // 2)
+    some = steps - max(1, steps // 2)
     first, rest = range(some), range(some, steps)
     half = len(first) * depth
     units = range(qkv_saved.shape[1] // UNIT)
     early = []
     if len(landed) > 1:
-        early = [back_early(qkv_saved, own, landed[0], helds, words, cores, units[:1], steps)]
+        shares = (qkv_saved, probs, own, landed[0], helds, words, cores, units[:1], steps)
+        early = [back_early(*shares)]
         units = units[1:]
-    grad_qkv, (keep, *sends) = back_first(
-        qkv_saved, own, landed[-1], early, helds, words, cores, units, first, steps
-    )
+    shares = (qkv_saved, probs, own, landed[-1], early, helds, words, cores, units, first, steps)
+    grad_qkv, (keep, *sends) = back_first(*shares)
     scaled = sum_over_cores(keep, sends) * gain_row[:, :half]
     arrived = [over_pipe(scaled.astype(jnp.bfloat16), -1)]
     keep, *sends = back_rest(grad_qkv, early, helds, cores, units, rest, steps)

time: 120 us -> 120 us (level)
  local copies, waits for them, and re-layouts: 4.05 us -> 6.42 us
  Pallas kernels: 37.9 us -> 36.1 us
  waiting for transfers between devices: 42.6 us -> 41.2 us
    unnamed x19 -> x21, local copies, waits for them, and re-layouts: 2.96 us -> 5.33 us
    pallas_call x9, Pallas kernels: 36.7 us -> 34.9 us  [call(): pl.pallas_call(body, in_specs=specs + [REMOTE if blocks else LOCAL for _...]
    ppermute x12, waiting for transfers between devices: 34.4 us -> 32.8 us  [over_dp(): return lax.ppermute(value, 'dp', partner_pairs(lax.axis_size('dp'), step))]
  transfers between devices with their start and end apart: 33 -> 33, of which waited for: 10 -> 9; matrix products, arithmetic and copies ran while one was open for 0% -> 1% of each run, Pallas kernels for 32% -> 30%
where the time goes in v4:
time: 120 us
  waiting for transfers between devices  41.2 us (34%)
  Pallas kernels  36.1 us (30%)
  starting transfers between devices  33.7 us (28%)
  local copies, waits for them, and re-layouts  6.42 us (5%)
  other arithmetic  1.37 us (1%)
    pallas_call x9, Pallas kernels, call(): pl.pallas_call(body, in_specs=specs + [REMOTE if blocks else LOCAL for _...  34.9 us
    ppermute x12, waiting for transfers between devices, over_dp(): return lax.ppermute(value, 'dp', partner_pairs(lax.axis_size('dp'), step))  32.8 us
    ppermute x12, starting transfers between devices, over_dp(): return lax.ppermute(value, 'dp', partner_pairs(lax.axis_size('dp'), step))  15.6 us
    ppermute x5, starting transfers between devices, over_pipe(): lax.ppermute(value, 'pipe', shift_pairs(lax.axis_size('pipe'), steps))  8.82 us
    ppermute x4, starting transfers between devices, window(): lax.ppermute(summed[index * rows:(index + 1) * rows], ('pipe', 'dp'), cro...  6.86 us
    ppermute x4, waiting for transfers between devices, window(): lax.ppermute(summed[index * rows:(index + 1) * rows], ('pipe', 'dp'), cro...  5.83 us
    unnamed x21, local copies, waits for them, and re-layouts  5.33 us
    ppermute x5, waiting for transfers between devices, sum_over_cores(): block = lax.ppermute(sends[step - 1], 'tensor', shift_pairs(count, step))  2.53 us
  transfers between devices with their start and end apart: 33, of which 9 were waited for; matrix products, arithmetic and copies ran while one was open for 1% of the time, Pallas kernels for 30%

profile of v4, /device:TPU:0, one launch (start us, length us, event | category | flops | bytes accessed | tf_op | source)
XLA Modules:
  0.0 119.8 jit_solution(4068364164039992228)
XLA Ops:
  1.7 4.1 %collective-permute-start.10 = (bf16[48,1024]{1,0:T(8,128)(2,1)S(1)}, bf16[48,1024]{1,0:T(8,128)(2,1)S(1)}, u32[]{:S(2)}, u32[]{:S(2)}) collective-permute-start(bf16[48,1024]{1,0:T(8,128)(2,1)S(1)} %get-tuple-element.53), channel_id=1, source_target_pairs={{0,2},{1,3},{2,0},{3,1},{4,6},{5,7},{6,4},{7,5},{8,10},{9,11},{10,... | collective-permute-start | bytes 294920 | tf_op jit(solution)/shard_map/ppermute | solution.py:37
  5.9 1.3 %collective-permute-start.12 = (bf16[48,1024]{1,0:T(8,128)(2,1)S(1)}, bf16[48,1024]{1,0:T(8,128)(2,1)S(1)}, u32[]{:S(2)}, u32[]{:S(2)}) collective-permute-start(bf16[48,1024]{1,0:T(8,128)(2,1)S(1)} %get-tuple-element.52), channel_id=1, source_target_pairs={{0,3},{1,2},{2,1},{3,0},{4,7},{5,6},{6,5},{7,4},{8,11},{9,10},{10,... | collective-permute-start | bytes 294920 | tf_op jit(solution)/shard_map/ppermute | solution.py:37
  7.5 6.3 %collective-permute-done.10.refs_4_ = bf16[48,1024]{1,0:T(8,128)(2,1)S(1)} collective-permute-done((bf16[48,1024]{1,0:T(8,128)(2,1)S(1)}, bf16[48,1024]{1,0:T(8,128)(2,1)S(1)}, u32[]{:S(2)}, u32[]{:S(2)}) %collective-permute-start.10) | collective-permute-done | bytes 98336 | tf_op jit(solution)/shard_map/ppermute | solution.py:37
  14.8 1.5 %collective-permute-start.1 = (bf16[48,4096]{1,0:T(8,128)(2,1)}, bf16[48,4096]{1,0:T(8,128)(2,1)S(1)}, u32[]{:S(2)}, u32[]{:S(2)}) collective-permute-start(bf16[48,4096]{1,0:T(8,128)(2,1)} %bitcast.46), channel_id=1, source_target_pairs={{0,1},{1,0},{2,3},{3,2},{4,5},{5,4},{6,7},{7,6},{8,9},{9,8},{10,11... | collective-permute-start | bytes 1179656 | tf_op jit(solution)/shard_map/ppermute | solution.py:37
  16.3 3.4 %collective-permute-start.3 = (bf16[48,4096]{1,0:T(8,128)(2,1)}, bf16[48,4096]{1,0:T(8,128)(2,1)S(1)}, u32[]{:S(2)}, u32[]{:S(2)}) collective-permute-start(bf16[48,4096]{1,0:T(8,128)(2,1)} %bitcast.47), channel_id=1, source_target_pairs={{0,3},{1,2},{2,1},{3,0},{4,7},{5,6},{6,5},{7,4},{8,11},{9,10},{10,... | collective-permute-start | bytes 1179656 | tf_op jit(solution)/shard_map/ppermute | solution.py:37
  19.7 1.5 %collective-permute-start = (bf16[48,4096]{1,0:T(8,128)(2,1)}, bf16[48,4096]{1,0:T(8,128)(2,1)S(1)}, u32[]{:S(2)}, u32[]{:S(2)}) collective-permute-start(bf16[48,4096]{1,0:T(8,128)(2,1)} %bitcast.48), channel_id=1, source_target_pairs={{0,8},{8,16},{16,24},{24,0},{1,9},{9,17},{17,25},{25,1},{2,10},{10... | collective-permute-start | bytes 1179656 | tf_op jit(solution)/shard_map/ppermute | solution.py:41
  21.2 2.3 %copy-done.4 = bf16[1,2304,1024]{2,1,0:T(8,128)(2,1)S(1)} copy-done((bf16[1,2304,1024]{2,1,0:T(8,128)(2,1)S(1)}, bf16[1,2304,1024]{2,1,0:T(8,128)(2,1)}, u32[]{:S(2)}) %copy-start.4) | copy-done | bytes 4718616
  23.5 3.2 %shard_map.88 = (bf16[96,2304]{1,0:T(8,128)(2,1)S(1)}, bf16[96,768]{1,0:T(8,128)(2,1)S(1)}, bf16[96,768]{1,0:T(8,128)(2,1)S(1)}, bf16[96,768]{1,0:T(8,128)(2,1)S...) custom-call(bf16[48,1024]{1,0:T(8,128)(2,1)S(1)} %get-tuple-element., ...), custom_call_target="tpu_custom_call" | custom-call | flops 1811939328 | bytes 4718592 | tf_op jit(solution)/shard_map/pallas_call | solution.py:206
  26.7 2.2 %copy-done = bf16[3,768,1024]{2,1,0:T(8,128)(2,1)} copy-done((bf16[3,768,1024]{2,1,0:T(8,128)(2,1)}, bf16[3,768,1024]{2,1,0:T(8,128)(2,1)S(1)}, u32[]{:S(2)}) %copy-start) | copy-done | bytes 4718616
  28.9 12.1 %collective-permute-done.27 = bf16[96,768]{1,0:T(8,128)(2,1)} collective-permute-done((bf16[96,768]{1,0:T(8,128)(2,1)S(1)}, bf16[96,768]{1,0:T(8,128)(2,1)}, u32[]{:S(2)}, u32[]{:S(2)}) %collective-permute-start.27) | collective-permute-done | bytes 147488 | tf_op jit(solution)/shard_map/ppermute | solution.py:37
  42.0 2.1 %collective-permute-start.26 = (bf16[96,768]{1,0:T(8,128)(2,1)S(1)}, bf16[96,768]{1,0:T(8,128)(2,1)S(1)}, u32[]{:S(2)}, u32[]{:S(2)}) collective-permute-start(bf16[96,768]{1,0:T(8,128)(2,1)S(1)} %get-tuple-element.43), channel_id=1, source_target_pairs={{0,1},{1,0},{2,3},{3,2},{4,5},{5,4},{6,7},{7,6},{8,9},{9,8},{10,11... | collective-permute-start | bytes 442376 | tf_op jit(solution)/shard_map/ppermute | solution.py:37
  44.8 11.3 %shard_map.86 = (bf16[96,2304]{1,0:T(8,128)(2,1)S(1)}, f32[1728,96]{1,0:T(8,128)S(1)}, bf16[12,1024,1024]{2,1,0:T(8,128)(2,1)S(1)}) custom-call(s32[1]{0:T(128)} %bitcast.2.refs_0_, f32[1,4096]{1,0:T(1,128)} %refs_1_.3, bf16[48,4096]{1,0:T(8,128)(2,1)} %bitcast.49, bf16[48,4096]{1,0:T(8,128)(2,1)S(1)} %collective-permute-done.5.refs_3_, ...), custom_call_target="tpu_custom_call" | custom-call | flops 2415919104 | bytes 25165824 | tf_op jit(solution)/shard_map/pallas_call | solution.py:206
  58.1 2.0 %collective-permute-start.25 = (bf16[96,1536]{1,0:T(8,128)(2,1)S(1)}, bf16[96,1536]{1,0:T(8,128)(2,1)S(1)}, u32[]{:S(2)}, u32[]{:S(2)}) collective-permute-start(bf16[96,1536]{1,0:T(8,128)(2,1)S(1)} %add_convert_fusion), channel_id=1, source_target_pairs={{0,2},{1,3},{2,0},{3,1},{4,6},{5,7},{6,4},{7,5},{8,10},{9,11},{10,... | collective-permute-start | bytes 884744 | tf_op jit(solution)/shard_map/ppermute | solution.py:37
  60.1 3.5 %shard_map.92 = (bf16[96,1024]{1,0:T(8,128)(2,1)}, f32[96,4096]{1,0:T(8,128)S(1)}) custom-call(s32[1]{0:T(128)} %bitcast.2.refs_0_, bf16[96,3072]{1,0:T(8,128)(2,1)S(1)} %bitcast.38, f32[1728,96]{1,0:T(8,128)S(1)} %get-tuple-element.38.refs_2_, bf16[96,2304]{1,0:T(8,128)(2,1)S(1)} %get-tuple-element.39.refs_3_, ...), custom_call_target="tpu_custom_call" | custom-call | flops 805306368 | tf_op jit(solution)/shard_map/pallas_call | solution.py:206
  63.6 2.4 %collective-permute-start.21 = (bf16[48,4096]{1,0:T(8,128)(2,1)S(1)}, bf16[48,4096]{1,0:T(8,128)(2,1)S(1)}, u32[]{:S(2)}, u32[]{:S(2)}) collective-permute-start(bf16[48,4096]{1,0:T(8,128)(2,1)S(1)} %bitcast.52), channel_id=1, source_target_pairs={{0,24},{8,0},{16,8},{24,16},{1,25},{9,1},{17,9},{25,17},{2,26},{10... | collective-permute-start | bytes 1179656 | tf_op jit(solution)/shard_map/ppermute | solution.py:41
  66.1 6.9 %collective-permute-done.23.refs_4_ = bf16[96,1536]{1,0:T(8,128)(2,1)S(1)} collective-permute-done((bf16[96,1536]{1,0:T(8,128)(2,1)S(1)}, bf16[96,1536]{1,0:T(8,128)(2,1)S(1)}, u32[]{:S(2)}, u32[]{:S(2)}) %collective-permute-start.23) | collective-permute-done | bytes 294944 | tf_op jit(solution)/shard_map/ppermute | solution.py:37
  73.0 2.4 %collective-permute-start.22 = (bf16[48,4096]{1,0:T(8,128)(2,1)S(1)}, bf16[48,4096]{1,0:T(8,128)(2,1)S(1)}, u32[]{:S(2)}, u32[]{:S(2)}) collective-permute-start(bf16[48,4096]{1,0:T(8,128)(2,1)S(1)} %bitcast.43), channel_id=1, source_target_pairs={{0,24},{8,0},{16,8},{24,16},{1,25},{9,1},{17,9},{25,17},{2,26},{10... | collective-permute-start | bytes 1179656 | tf_op jit(solution)/shard_map/ppermute | solution.py:41
  75.5 3.4 %shard_map.93 = (bf16[96,2048]{1,0:T(8,128)(2,1)S(1)}, bf16[48,2048]{1,0:T(8,128)(2,1)S(1)}, bf16[48,2048]{1,0:T(8,128)(2,1)S(1)}) custom-call(s32[1]{0:T(128)} %bitcast.2.refs_0_, bf16[96,3072]{1,0:T(8,128)(2,1)S(1)} %bitcast.39, f32[1728,96]{1,0:T(8,128)S(1)} %get-tuple-element.38.refs_2_, bf16[96,2304]{1,0:T(8,128)(2,1)S(1)} %get-tuple-element.39.refs_3_, ...), custom_call_target="tpu_custom_call" | custom-call | flops 805306368 | tf_op jit(solution)/shard_map/pallas_call | solution.py:206
  78.9 2.7 %shard_map.94 = (bf16[48,2048]{1,0:T(8,128)(2,1)S(1)}, bf16[48,2048]{1,0:T(8,128)(2,1)S(1)}) custom-call(bf16[96,2048]{1,0:T(8,128)(2,1)S(1)} %get-tuple-element.49.refs_0_, f32[96,4096]{1,0:T(8,128)S(1)} %get-tuple-element.46.refs_6_.refs_1_, bf16[12,1024,1024]{2,1,0:T(8,128)(2,1)S(1)} %get-tuple-element.27.refs_6_.refs_7_.refs_2_), custom_call_target="tpu_custom_call" | custom-call | flops 805306368 | tf_op jit(solution)/shard_map/pallas_call | solution.py:206
  81.7 7.8 %shard_map.87 = (bf16[96,2304]{1,0:T(8,128)(2,1)S(1)}, bf16[96,2304]{1,0:T(8,128)(2,1)S(1)}) custom-call(s32[1]{0:T(128)} %bitcast.2.refs_0_, f32[1,4096]{1,0:T(1,128)S(1)} %copy-done.3, bf16[48,4096]{1,0:T(8,128)(2,1)S(1)} %collective-permute-done.1.refs_2_, bf16[48,4096]{1,0:T(8,128)(2,1)S(1)} %collective-permute-done.2.refs_3_, ...), custom_call_target="tpu_custom_call" | custom-call | flops 4831838208 | tf_op jit(solution)/shard_map/pallas_call | solution.py:206
  89.6 1.1 shard_map.90
  91.4 1.3 %collective-permute-done.29 = bf16[48,2048]{1,0:T(8,128)(2,1)S(1)} collective-permute-done((bf16[48,2048]{1,0:T(8,128)(2,1)S(1)}, bf16[48,2048]{1,0:T(8,128)(2,1)S(1)}, u32[]{:S(2)}, u32[]{:S(2)}) %collective-permute-start.29) | collective-permute-done | bytes 196640 | tf_op jit(solution)/shard_map/ppermute | solution.py:55
  92.7 1.9 %collective-permute-start.32 = (bf16[48,2048]{1,0:T(8,128)(2,1)S(1)}, bf16[48,2048]{1,0:T(8,128)(2,1)S(1)}, u32[]{:S(2)}, u32[]{:S(2)}) collective-permute-start(bf16[48,2048]{1,0:T(8,128)(2,1)S(1)} %multiply_convert_fusion), channel_id=1, source_target_pairs={{0,24},{8,0},{16,8},{24,16},{1,25},{9,1},{17,9},{25,17},{2,26},{10... | collective-permute-start | bytes 589832 | tf_op jit(solution)/shard_map/ppermute | solution.py:41
  94.7 7.5 %collective-permute-done.6.refs_0_ = bf16[96,2304]{1,0:T(8,128)(2,1)S(1)} collective-permute-done((bf16[96,2304]{1,0:T(8,128)(2,1)S(1)}, bf16[96,2304]{1,0:T(8,128)(2,1)S(1)}, u32[]{:S(2)}, u32[]{:S(2)}) %collective-permute-start.6) | collective-permute-done | bytes 442400 | tf_op jit(solution)/shard_map/ppermute | solution.py:37
  103.7 1.2 %collective-permute-done.14 = bf16[48,1024]{1,0:T(8,128)(2,1)S(1)} collective-permute-done((bf16[48,1024]{1,0:T(8,128)(2,1)S(1)}, bf16[48,1024]{1,0:T(8,128)(2,1)S(1)}, u32[]{:S(2)}, u32[]{:S(2)}) %collective-permute-start.14) | collective-permute-done | bytes 98336 | tf_op jit(solution)/shard_map/ppermute | solution.py:55
  105.0 2.1 %collective-permute-start.15 = (bf16[48,1024]{1,0:T(8,128)(2,1)S(1)}, bf16[48,1024]{1,0:T(8,128)(2,1)S(1)}, u32[]{:S(2)}, u32[]{:S(2)}) collective-permute-start(bf16[48,1024]{1,0:T(8,128)(2,1)S(1)} %add_convert_fusion.8), channel_id=1, source_target_pairs={{0,10},{1,11},{2,8},{3,9},{8,18},{9,19},{10,16},{11,17},{16,26},{1... | collective-permute-start | bytes 294920 | tf_op jit(solution)/shard_map/ppermute | solution.py:554
  107.1 2.4 %collective-permute-start.20 = (bf16[48,1024]{1,0:T(8,128)(2,1)S(1)}, bf16[48,1024]{1,0:T(8,128)(2,1)S(1)}, u32[]{:S(2)}, u32[]{:S(2)}) collective-permute-start(bf16[48,1024]{1,0:T(8,128)(2,1)S(1)} %add_convert_fusion.4), channel_id=1, source_target_pairs={{0,8},{1,9},{2,10},{3,11},{8,16},{9,17},{10,18},{11,19},{16,24},{1... | collective-permute-start | bytes 294920 | tf_op jit(solution)/shard_map/ppermute | solution.py:554
  109.5 1.2 %collective-permute-start.17 = (bf16[48,1024]{1,0:T(8,128)(2,1)S(1)}, bf16[48,1024]{1,0:T(8,128)(2,1)S(1)}, u32[]{:S(2)}, u32[]{:S(2)}) collective-permute-start(bf16[48,1024]{1,0:T(8,128)(2,1)S(1)} %get-tuple-element.57), channel_id=1, source_target_pairs={{0,11},{1,10},{2,9},{3,8},{8,19},{9,18},{10,17},{11,16},{16,27},{1... | collective-permute-start | bytes 294920 | tf_op jit(solution)/shard_map/ppermute | solution.py:554
  110.7 1.1 collective-permute-start.18
  111.9 1.2 norm_back.1
  113.1 1.6 %collective-permute-done.15 = bf16[48,1024]{1,0:T(8,128)(2,1)S(1)} collective-permute-done((bf16[48,1024]{1,0:T(8,128)(2,1)S(1)}, bf16[48,1024]{1,0:T(8,128)(2,1)S(1)}, u32[]{:S(2)}, u32[]{:S(2)}) %collective-permute-start.15) | collective-permute-done | bytes 98336 | tf_op jit(solution)/shard_map/ppermute | solution.py:554
  114.7 3.8 %collective-permute-done.17 = bf16[48,1024]{1,0:T(8,128)(2,1)S(1)} collective-permute-done((bf16[48,1024]{1,0:T(8,128)(2,1)S(1)}, bf16[48,1024]{1,0:T(8,128)(2,1)S(1)}, u32[]{:S(2)}, u32[]{:S(2)}) %collective-permute-start.17) | collective-permute-done | bytes 98336 | tf_op jit(solution)/shard_map/ppermute | solution.py:554
  (80 shorter events, 9.7 us)
Async XLA Ops:
  1.7 12.0 %collective-permute-start.10 = (bf16[48,1024]{1,0:T(8,128)(2,1)S(1)}, bf16[48,1024]{1,0:T(8,128)(2,1)S(1)}, u32[]{:S(2)}, u32[]{:S(2)}) collective-permute-start(bf16[48,1024]{1,0:T(8,128)(2,1)S(1)} %get-tuple-element.53), channel_id=1, source_target_pairs={{0,2},{1,3},{2,0},{3,1},{4,6},{5,7},{6,4},{7,5},{8,10},{9,11},{10,... | collective-permute-start | bytes 294920 | tf_op jit(solution)/shard_map/ppermute | solution.py:37
  5.9 7.9 %collective-permute-start.12 = (bf16[48,1024]{1,0:T(8,128)(2,1)S(1)}, bf16[48,1024]{1,0:T(8,128)(2,1)S(1)}, u32[]{:S(2)}, u32[]{:S(2)}) collective-permute-start(bf16[48,1024]{1,0:T(8,128)(2,1)S(1)} %get-tuple-element.52), channel_id=1, source_target_pairs={{0,3},{1,2},{2,1},{3,0},{4,7},{5,6},{6,5},{7,4},{8,11},{9,10},{10,... | collective-permute-start | bytes 294920 | tf_op jit(solution)/shard_map/ppermute | solution.py:37
  7.2 7.1 %collective-permute-start.8 = (bf16[48,1024]{1,0:T(8,128)(2,1)S(1)}, bf16[48,1024]{1,0:T(8,128)(2,1)S(1)}, u32[]{:S(2)}, u32[]{:S(2)}) collective-permute-start(bf16[48,1024]{1,0:T(8,128)(2,1)S(1)} %get-tuple-element.54), channel_id=1, source_target_pairs={{0,1},{1,0},{2,3},{3,2},{4,5},{5,4},{6,7},{7,6},{8,9},{9,8},{10,11... | collective-permute-start | bytes 294920 | tf_op jit(solution)/shard_map/ppermute | solution.py:37
  7.5 7.4 %collective-permute-start.7 = (bf16[48,1024]{1,0:T(8,128)(2,1)S(1)}, bf16[48,1024]{1,0:T(8,128)(2,1)S(1)}, u32[]{:S(2)}, u32[]{:S(2)}) collective-permute-start(bf16[48,1024]{1,0:T(8,128)(2,1)S(1)} %get-tuple-element.55.refs_0_), channel_id=1, source_target_pairs={{0,4},{4,0},{1,5},{5,1},{2,6},{6,2},{3,7},{7,3},{8,12},{12,8},{9,1... | collective-permute-start | bytes 294920 | tf_op jit(solution)/shard_map/ppermute | solution.py:47
  13.8 2.5 %collective-permute-start.11 = (bf16[48,1024]{1,0:T(8,128)(2,1)S(1)}, bf16[48,1024]{1,0:T(8,128)(2,1)S(1)}, u32[]{:S(2)}, u32[]{:S(2)}) collective-permute-start(bf16[48,1024]{1,0:T(8,128)(2,1)S(1)} %collective-permute-done.10.refs_4_), channel_id=1, source_target_pairs={{0,4},{4,0},{1,5},{5,1},{2,6},{6,2},{3,7},{7,3},{8,12},{12,8},{9,1... | collective-permute-start | bytes 294920 | tf_op jit(solution)/shard_map/ppermute | solution.py:47
  13.8 5.9 %collective-permute-start.13 = (bf16[48,1024]{1,0:T(8,128)(2,1)S(1)}, bf16[48,1024]{1,0:T(8,128)(2,1)S(1)}, u32[]{:S(2)}, u32[]{:S(2)}) collective-permute-start(bf16[48,1024]{1,0:T(8,128)(2,1)S(1)} %collective-permute-done.12.refs_6_), channel_id=1, source_target_pairs={{0,4},{4,0},{1,5},{5,1},{2,6},{6,2},{3,7},{7,3},{8,12},{12,8},{9,1... | collective-permute-start | bytes 294920 | tf_op jit(solution)/shard_map/ppermute | solution.py:47
  14.3 6.9 %collective-permute-start.9 = (bf16[48,1024]{1,0:T(8,128)(2,1)S(1)}, bf16[48,1024]{1,0:T(8,128)(2,1)S(1)}, u32[]{:S(2)}, u32[]{:S(2)}) collective-permute-start(bf16[48,1024]{1,0:T(8,128)(2,1)S(1)} %collective-permute-done.8.refs_2_), channel_id=1, source_target_pairs={{0,4},{4,0},{1,5},{5,1},{2,6},{6,2},{3,7},{7,3},{8,12},{12,8},{9,1... | collective-permute-start | bytes 294920 | tf_op jit(solution)/shard_map/ppermute | solution.py:47
  14.4 29.8 %collective-permute-start.5 = (bf16[48,4096]{1,0:T(8,128)(2,1)}, bf16[48,4096]{1,0:T(8,128)(2,1)S(1)}, u32[]{:S(2)}, u32[]{:S(2)}) collective-permute-start(bf16[48,4096]{1,0:T(8,128)(2,1)} %bitcast.45), channel_id=1, source_target_pairs={{0,4},{4,0},{1,5},{5,1},{2,6},{6,2},{3,7},{7,3},{8,12},{12,8},{9,1... | collective-permute-start | bytes 1179656 | tf_op jit(solution)/shard_map/ppermute | solution.py:47
  14.8 42.8 %collective-permute-start.1 = (bf16[48,4096]{1,0:T(8,128)(2,1)}, bf16[48,4096]{1,0:T(8,128)(2,1)S(1)}, u32[]{:S(2)}, u32[]{:S(2)}) collective-permute-start(bf16[48,4096]{1,0:T(8,128)(2,1)} %bitcast.46), channel_id=1, source_target_pairs={{0,1},{1,0},{2,3},{3,2},{4,5},{5,4},{6,7},{7,6},{8,9},{9,8},{10,11... | collective-permute-start | bytes 1179656 | tf_op jit(solution)/shard_map/ppermute | solution.py:37
  16.3 41.6 %collective-permute-start.3 = (bf16[48,4096]{1,0:T(8,128)(2,1)}, bf16[48,4096]{1,0:T(8,128)(2,1)S(1)}, u32[]{:S(2)}, u32[]{:S(2)}) collective-permute-start(bf16[48,4096]{1,0:T(8,128)(2,1)} %bitcast.47), channel_id=1, source_target_pairs={{0,3},{1,2},{2,1},{3,0},{4,7},{5,6},{6,5},{7,4},{8,11},{9,10},{10,... | collective-permute-start | bytes 1179656 | tf_op jit(solution)/shard_map/ppermute | solution.py:37
  19.7 22.3 %collective-permute-start = (bf16[48,4096]{1,0:T(8,128)(2,1)}, bf16[48,4096]{1,0:T(8,128)(2,1)S(1)}, u32[]{:S(2)}, u32[]{:S(2)}) collective-permute-start(bf16[48,4096]{1,0:T(8,128)(2,1)} %bitcast.48), channel_id=1, source_target_pairs={{0,8},{8,16},{16,24},{24,0},{1,9},{9,17},{17,25},{25,1},{2,10},{10... | collective-permute-start | bytes 1179656 | tf_op jit(solution)/shard_map/ppermute | solution.py:41
  28.9 12.1 %collective-permute-start.27 = (bf16[96,768]{1,0:T(8,128)(2,1)S(1)}, bf16[96,768]{1,0:T(8,128)(2,1)}, u32[]{:S(2)}, u32[]{:S(2)}) collective-permute-start(bf16[96,768]{1,0:T(8,128)(2,1)S(1)} %get-tuple-element.45), channel_id=1, source_target_pairs={{0,1},{1,0},{2,3},{3,2},{4,5},{5,4},{6,7},{7,6},{8,9},{9,8},{10,11... | collective-permute-start | bytes 442376 | tf_op jit(solution)/shard_map/ppermute | solution.py:37
  41.1 16.0 %collective-permute-start.24 = (bf16[96,1536]{1,0:T(8,128)(2,1)S(1)}, bf16[96,1536]{1,0:T(8,128)(2,1)S(1)}, u32[]{:S(2)}, u32[]{:S(2)}) collective-permute-start(bf16[96,1536]{1,0:T(8,128)(2,1)S(1)} %get-tuple-element.42), channel_id=1, source_target_pairs={{0,1},{1,0},{2,3},{3,2},{4,5},{5,4},{6,7},{7,6},{8,9},{9,8},{10,11... | collective-permute-start | bytes 884744 | tf_op jit(solution)/shard_map/ppermute | solution.py:37
  42.0 15.2 %collective-permute-start.26 = (bf16[96,768]{1,0:T(8,128)(2,1)S(1)}, bf16[96,768]{1,0:T(8,128)(2,1)S(1)}, u32[]{:S(2)}, u32[]{:S(2)}) collective-permute-start(bf16[96,768]{1,0:T(8,128)(2,1)S(1)} %get-tuple-element.43), channel_id=1, source_target_pairs={{0,1},{1,0},{2,3},{3,2},{4,5},{5,4},{6,7},{7,6},{8,9},{9,8},{10,11... | collective-permute-start | bytes 442376 | tf_op jit(solution)/shard_map/ppermute | solution.py:37
  44.2 14.0 %collective-permute-start.28 = (bf16[96,768]{1,0:T(8,128)(2,1)S(1)}, bf16[96,768]{1,0:T(8,128)(2,1)S(1)}, u32[]{:S(2)}, u32[]{:S(2)}) collective-permute-start(bf16[96,768]{1,0:T(8,128)(2,1)S(1)} %add_convert_fusion.2), channel_id=1, source_target_pairs={{0,2},{1,3},{2,0},{3,1},{4,6},{5,7},{6,4},{7,5},{8,10},{9,11},{10,... | collective-permute-start | bytes 442376 | tf_op jit(solution)/shard_map/ppermute | solution.py:37
  57.1 6.6 %collective-permute-start.19 = (bf16[48,1024]{1,0:T(8,128)(2,1)S(1)}, bf16[48,1024]{1,0:T(8,128)(2,1)S(1)}, u32[]{:S(2)}, u32[]{:S(2)}) collective-permute-start(bf16[48,1024]{1,0:T(8,128)(2,1)S(1)} %get-tuple-element.37), channel_id=1, source_target_pairs={{0,4},{4,0},{1,5},{5,1},{2,6},{6,2},{3,7},{7,3},{8,12},{12,8},{9,1... | collective-permute-start | bytes 294920 | tf_op jit(solution)/shard_map/ppermute | solution.py:55
  57.2 15.8 %collective-permute-start.23 = (bf16[96,1536]{1,0:T(8,128)(2,1)S(1)}, bf16[96,1536]{1,0:T(8,128)(2,1)S(1)}, u32[]{:S(2)}, u32[]{:S(2)}) collective-permute-start(bf16[96,1536]{1,0:T(8,128)(2,1)S(1)} %get-tuple-element.40), channel_id=1, source_target_pairs={{0,1},{1,0},{2,3},{3,2},{4,5},{5,4},{6,7},{7,6},{8,9},{9,8},{10,11... | collective-permute-start | bytes 884744 | tf_op jit(solution)/shard_map/ppermute | solution.py:37
  57.6 24.1 %collective-permute-start.2 = (bf16[48,4096]{1,0:T(8,128)(2,1)S(1)}, bf16[48,4096]{1,0:T(8,128)(2,1)S(1)}, u32[]{:S(2)}, u32[]{:S(2)}) collective-permute-start(bf16[48,4096]{1,0:T(8,128)(2,1)S(1)} %collective-permute-done.1.refs_2_), channel_id=1, source_target_pairs={{0,4},{4,0},{1,5},{5,1},{2,6},{6,2},{3,7},{7,3},{8,12},{12,8},{9,1... | collective-permute-start | bytes 1179656 | tf_op jit(solution)/shard_map/ppermute | solution.py:47
  57.9 23.8 %collective-permute-start.4 = (bf16[48,4096]{1,0:T(8,128)(2,1)S(1)}, bf16[48,4096]{1,0:T(8,128)(2,1)S(1)}, u32[]{:S(2)}, u32[]{:S(2)}) collective-permute-start(bf16[48,4096]{1,0:T(8,128)(2,1)S(1)} %collective-permute-done.3.refs_4_), channel_id=1, source_target_pairs={{0,4},{4,0},{1,5},{5,1},{2,6},{6,2},{3,7},{7,3},{8,12},{12,8},{9,1... | collective-permute-start | bytes 1179656 | tf_op jit(solution)/shard_map/ppermute | solution.py:47
  58.1 17.4 %collective-permute-start.25 = (bf16[96,1536]{1,0:T(8,128)(2,1)S(1)}, bf16[96,1536]{1,0:T(8,128)(2,1)S(1)}, u32[]{:S(2)}, u32[]{:S(2)}) collective-permute-start(bf16[96,1536]{1,0:T(8,128)(2,1)S(1)} %add_convert_fusion), channel_id=1, source_target_pairs={{0,2},{1,3},{2,0},{3,1},{4,6},{5,7},{6,4},{7,5},{8,10},{9,11},{10,... | collective-permute-start | bytes 884744 | tf_op jit(solution)/shard_map/ppermute | solution.py:37
  63.6 43.5 %collective-permute-start.21 = (bf16[48,4096]{1,0:T(8,128)(2,1)S(1)}, bf16[48,4096]{1,0:T(8,128)(2,1)S(1)}, u32[]{:S(2)}, u32[]{:S(2)}) collective-permute-start(bf16[48,4096]{1,0:T(8,128)(2,1)S(1)} %bitcast.52), channel_id=1, source_target_pairs={{0,24},{8,0},{16,8},{24,16},{1,25},{9,1},{17,9},{25,17},{2,26},{10... | collective-permute-start | bytes 1179656 | tf_op jit(solution)/shard_map/ppermute | solution.py:41
  73.0 36.5 %collective-permute-start.22 = (bf16[48,4096]{1,0:T(8,128)(2,1)S(1)}, bf16[48,4096]{1,0:T(8,128)(2,1)S(1)}, u32[]{:S(2)}, u32[]{:S(2)}) collective-permute-start(bf16[48,4096]{1,0:T(8,128)(2,1)S(1)} %bitcast.43), channel_id=1, source_target_pairs={{0,24},{8,0},{16,8},{24,16},{1,25},{9,1},{17,9},{25,17},{2,26},{10... | collective-permute-start | bytes 1179656 | tf_op jit(solution)/shard_map/ppermute | solution.py:41
  81.6 9.7 %collective-permute-start.31 = (bf16[48,2048]{1,0:T(8,128)(2,1)S(1)}, bf16[48,2048]{1,0:T(8,128)(2,1)S(1)}, u32[]{:S(2)}, u32[]{:S(2)}) collective-permute-start(bf16[48,2048]{1,0:T(8,128)(2,1)S(1)} %get-tuple-element.51), channel_id=1, source_target_pairs={{0,4},{4,0},{1,5},{5,1},{2,6},{6,2},{3,7},{7,3},{8,12},{12,8},{9,1... | collective-permute-start | bytes 589832 | tf_op jit(solution)/shard_map/ppermute | solution.py:55
  89.6 12.6 %collective-permute-start.6 = (bf16[96,2304]{1,0:T(8,128)(2,1)S(1)}, bf16[96,2304]{1,0:T(8,128)(2,1)S(1)}, u32[]{:S(2)}, u32[]{:S(2)}) collective-permute-start(bf16[96,2304]{1,0:T(8,128)(2,1)S(1)} %get-tuple-element.28.refs_1_), channel_id=1, source_target_pairs={{0,1},{1,0},{2,3},{3,2},{4,5},{5,4},{6,7},{7,6},{8,9},{9,8},{10,11... | collective-permute-start | bytes 1327112 | tf_op jit(solution)/shard_map/ppermute | solution.py:37
  90.7 12.8 %collective-permute-start.16 = (bf16[96,1024]{1,0:T(8,128)(2,1)S(1)}, bf16[96,1024]{1,0:T(8,128)(2,1)S(1)}, u32[]{:S(2)}, u32[]{:S(2)}) collective-permute-start(bf16[96,1024]{1,0:T(8,128)(2,1)S(1)} %get-tuple-element.34), channel_id=1, source_target_pairs={{0,4},{4,0},{1,5},{5,1},{2,6},{6,2},{3,7},{7,3},{8,12},{12,8},{9,1... | collective-permute-start | bytes 589832 | tf_op jit(solution)/shard_map/ppermute | solution.py:55
  91.3 1.4 %collective-permute-start.29 = (bf16[48,2048]{1,0:T(8,128)(2,1)S(1)}, bf16[48,2048]{1,0:T(8,128)(2,1)S(1)}, u32[]{:S(2)}, u32[]{:S(2)}) collective-permute-start(bf16[48,2048]{1,0:T(8,128)(2,1)S(1)} %get-tuple-element.48), channel_id=1, source_target_pairs={{0,4},{4,0},{1,5},{5,1},{2,6},{6,2},{3,7},{7,3},{8,12},{12,8},{9,1... | collective-permute-start | bytes 589832 | tf_op jit(solution)/shard_map/ppermute | solution.py:55
  92.7 18.0 %collective-permute-start.32 = (bf16[48,2048]{1,0:T(8,128)(2,1)S(1)}, bf16[48,2048]{1,0:T(8,128)(2,1)S(1)}, u32[]{:S(2)}, u32[]{:S(2)}) collective-permute-start(bf16[48,2048]{1,0:T(8,128)(2,1)S(1)} %multiply_convert_fusion), channel_id=1, source_target_pairs={{0,24},{8,0},{16,8},{24,16},{1,25},{9,1},{17,9},{25,17},{2,26},{10... | collective-permute-start | bytes 589832 | tf_op jit(solution)/shard_map/ppermute | solution.py:41
  102.1 9.7 %collective-permute-start.30 = (bf16[48,2048]{1,0:T(8,128)(2,1)S(1)}, bf16[48,2048]{1,0:T(8,128)(2,1)S(1)}, u32[]{:S(2)}, u32[]{:S(2)}) collective-permute-start(bf16[48,2048]{1,0:T(8,128)(2,1)S(1)} %multiply_convert_fusion.1), channel_id=1, source_target_pairs={{0,24},{8,0},{16,8},{24,16},{1,25},{9,1},{17,9},{25,17},{2,26},{10... | collective-permute-start | bytes 589832 | tf_op jit(solution)/shard_map/ppermute | solution.py:41
  105.0 9.7 %collective-permute-start.15 = (bf16[48,1024]{1,0:T(8,128)(2,1)S(1)}, bf16[48,1024]{1,0:T(8,128)(2,1)S(1)}, u32[]{:S(2)}, u32[]{:S(2)}) collective-permute-start(bf16[48,1024]{1,0:T(8,128)(2,1)S(1)} %add_convert_fusion.8), channel_id=1, source_target_pairs={{0,10},{1,11},{2,8},{3,9},{8,18},{9,19},{10,16},{11,17},{16,26},{1... | collective-permute-start | bytes 294920 | tf_op jit(solution)/shard_map/ppermute | solution.py:554
  107.1 11.9 %collective-permute-start.20 = (bf16[48,1024]{1,0:T(8,128)(2,1)S(1)}, bf16[48,1024]{1,0:T(8,128)(2,1)S(1)}, u32[]{:S(2)}, u32[]{:S(2)}) collective-permute-start(bf16[48,1024]{1,0:T(8,128)(2,1)S(1)} %add_convert_fusion.4), channel_id=1, source_target_pairs={{0,8},{1,9},{2,10},{3,11},{8,16},{9,17},{10,18},{11,19},{16,24},{1... | collective-permute-start | bytes 294920 | tf_op jit(solution)/shard_map/ppermute | solution.py:554
  109.5 9.0 %collective-permute-start.17 = (bf16[48,1024]{1,0:T(8,128)(2,1)S(1)}, bf16[48,1024]{1,0:T(8,128)(2,1)S(1)}, u32[]{:S(2)}, u32[]{:S(2)}) collective-permute-start(bf16[48,1024]{1,0:T(8,128)(2,1)S(1)} %get-tuple-element.57), channel_id=1, source_target_pairs={{0,11},{1,10},{2,9},{3,8},{8,19},{9,18},{10,17},{11,16},{16,27},{1... | collective-permute-start | bytes 294920 | tf_op jit(solution)/shard_map/ppermute | solution.py:554
  110.7 8.2 %collective-permute-start.18 = (bf16[48,1024]{1,0:T(8,128)(2,1)S(1)}, bf16[48,1024]{1,0:T(8,128)(2,1)S(1)}, u32[]{:S(2)}, u32[]{:S(2)}) collective-permute-start(bf16[48,1024]{1,0:T(8,128)(2,1)S(1)} %get-tuple-element.56), channel_id=1, source_target_pairs={{0,9},{1,8},{2,11},{3,10},{8,17},{9,16},{10,19},{11,18},{16,25},{1... | collective-permute-start | bytes 294920 | tf_op jit(solution)/shard_map/ppermute | solution.py:554
  (11 other events, 81.6 us)
